TPU v7x, 32 devices: a whole 2x2x4 slice. The times are simulated.
32 devices in a mesh: ty: 4 (over y, x), tx: 4 (over z), corner: 2 (over core).
Axes of the slice: x: 2, y: 2, z: 4, core: 2. Of those that a mesh axis runs over, the one named last changes fastest.
Arguments:
- level_init: int32 [1024, 1024], P('ty', 'tx'), may hold values from -64 to 64
- target: int32 [1024, 1024], P('ty', 'tx'), may hold values 0 or 1
- kernels: float32 [2, 5, 2, 128, 128], P('corner'), may hold values from -12 to 12
- corner_doses: float32 [2], P('corner'), may hold values from 0.7 to 1.4
Outputs:
- resist: float32 [2, 1024, 1024], P('corner', 'ty', 'tx')
- level_set: float32 [1024, 1024], P('ty', 'tx')
All inputs are finite; a program needn't handle non-finite values. No bound on the sum of `target` on one device may be relied on, other than what follows from the above.
Results may differ from a plain program's by a relative error of at most 0.015.
The roundings to bfloat16 on the way count: a program that leaves them out, or rounds other values in their place, can miss the bound.
Values may be sent and summed in bfloat16 or wider, within the bound.
No kernel may reach another device: no remote copies, remote signals or barrier semaphores. Data moves between devices by JAX's collectives and lax.ppermute only.
A program may use at most 64 MiB of HBM per device.

v0:
```python
import math

import jax
import jax.numpy as jnp
from jax import lax
from jax.sharding import PartitionSpec as P

HALO = 128
KF = 128
LS_STEPS = 3


STEEPNESS = 4.0
THRESHOLD = 1.0
SPEED_GAIN = 4.0
SMOOTHING = 0.24
GRAD_FLOOR = 0.25


def with_halo(block, sides, width):
    for axis, dim in sides:
        count = lax.axis_size(axis)
        forward = [(i, i + 1) for i in range(count - 1)]
        backward = [(target, source) for source, target in forward]
        low = lax.ppermute(
            lax.slice_in_dim(block, block.shape[dim] - width, None, axis=dim), axis, forward
        )
        high = lax.ppermute(lax.slice_in_dim(block, 0, width, axis=dim), axis, backward)
        block = jnp.concatenate([low, block, high], axis=dim)
    return block


def make_tables(window, freqs, margin, tile):
    shifts = jnp.arange(freqs, dtype=jnp.int32) - freqs // 2
    places = jnp.arange(window, dtype=jnp.int32)
    phases = shifts[:, None] * places[None, :] % window
    angles = 2.0 * math.pi / window * phases.astype(jnp.float32)
    scaled = 1.0 / math.sqrt(window)
    fwd_cos = (jnp.cos(angles) * scaled).astype(jnp.bfloat16)
    fwd_sin = (-jnp.sin(angles) * scaled).astype(jnp.bfloat16)
    inner = angles[:, margin : margin + tile].T
    inv_cos = (jnp.cos(inner) * scaled).astype(jnp.bfloat16)
    inv_sin = (jnp.sin(inner) * scaled).astype(jnp.bfloat16)
    return (fwd_cos, fwd_sin, inv_cos, inv_sin)


def matmul(left, right):
    return jnp.dot(left, right, preferred_element_type=jnp.float32)


def batched(form, left, right):
    return jnp.einsum(form, left, right, preferred_element_type=jnp.float32)


def tile_pass(win_data, goal, kernel_re, kernel_im, doses_col, tables):
    fwd_cos, fwd_sin, inv_cos, inv_sin = tables
    freqs = fwd_cos.shape[0]
    lift = matmul(jnp.concatenate([fwd_cos, fwd_sin], axis=0), win_data).astype(jnp.bfloat16)
    lift_re = lift[:freqs]
    lift_im = lift[freqs:]
    spec_re = matmul(lift_re, fwd_cos.T) - matmul(lift_im, fwd_sin.T)
    spec_im = matmul(lift_re, fwd_sin.T) + matmul(lift_im, fwd_cos.T)
    blur_re = (kernel_re * spec_re - kernel_im * spec_im).astype(jnp.bfloat16)
    blur_im = (kernel_re * spec_im + kernel_im * spec_re).astype(jnp.bfloat16)
    proj_re = (
        batched("rj,gjk->grk", inv_cos, blur_re) - batched("rj,gjk->grk", inv_sin, blur_im)
    ).astype(jnp.bfloat16)
    proj_im = (
        batched("rj,gjk->grk", inv_cos, blur_im) + batched("rj,gjk->grk", inv_sin, blur_re)
    ).astype(jnp.bfloat16)
    field_re = batched("grj,cj->grc", proj_re, inv_cos) - batched("grj,cj->grc", proj_im, inv_sin)
    field_im = batched("grj,cj->grc", proj_re, inv_sin) + batched("grj,cj->grc", proj_im, inv_cos)
    groups = doses_col.shape[0]
    tile = field_re.shape[1]
    grouped = (groups, -1, tile, tile)
    power = (field_re * field_re + field_im * field_im).reshape(grouped)
    intensity = jnp.sum(power, axis=1)
    dose_col = doses_col[:, None, None]
    resist = jax.nn.sigmoid(STEEPNESS * (dose_col * intensity - THRESHOLD))
    sens = 2.0 * (resist - goal) * STEEPNESS * dose_col * resist * (1.0 - resist)
    adj_re = (
        (2.0 * sens[:, None] * field_re.reshape(grouped))
        .reshape(field_re.shape)
        .astype(jnp.bfloat16)
    )
    adj_im = (
        (2.0 * sens[:, None] * field_im.reshape(grouped))
        .reshape(field_im.shape)
        .astype(jnp.bfloat16)
    )
    back_re = (
        batched("grc,cj->grj", adj_re, inv_cos) + batched("grc,cj->grj", adj_im, inv_sin)
    ).astype(jnp.bfloat16)
    back_im = (
        batched("grc,cj->grj", adj_im, inv_cos) - batched("grc,cj->grj", adj_re, inv_sin)
    ).astype(jnp.bfloat16)
    grad_blur_re = batched("rj,grk->gjk", inv_cos, back_re) + batched(
        "rj,grk->gjk", inv_sin, back_im
    )
    grad_blur_im = batched("rj,grk->gjk", inv_cos, back_im) - batched(
        "rj,grk->gjk", inv_sin, back_re
    )
    grad_spec_re = jnp.sum(kernel_re * grad_blur_re + kernel_im * grad_blur_im, axis=0)
    grad_spec_im = jnp.sum(kernel_re * grad_blur_im - kernel_im * grad_blur_re, axis=0)
    return (resist, grad_spec_re, grad_spec_im)


def window_grad(grad_spec_re, grad_spec_im, tables):
    fwd_cos, fwd_sin = (tables[0], tables[1])
    spec_low_re = grad_spec_re.astype(jnp.bfloat16)
    spec_low_im = grad_spec_im.astype(jnp.bfloat16)
    grad_lift_re = (matmul(spec_low_re, fwd_cos) + matmul(spec_low_im, fwd_sin)).astype(
        jnp.bfloat16
    )
    grad_lift_im = (matmul(spec_low_im, fwd_cos) - matmul(spec_low_re, fwd_sin)).astype(
        jnp.bfloat16
    )
    stacked = jnp.concatenate([fwd_cos, fwd_sin], axis=0)
    grad_lift = jnp.concatenate([grad_lift_re, grad_lift_im], axis=0)
    result = lax.dot_general(
        stacked, grad_lift, (((0,), (0,)), ((), ())), preferred_element_type=jnp.float32
    )
    return result.astype(jnp.bfloat16)


def fold_axis(values, tile, margin, axis):
    centre = lax.slice_in_dim(values, 2 * margin, 2 * margin + tile, axis=axis)
    upper_rim = lax.slice_in_dim(values, 0, margin, axis=axis)
    lower_rim = lax.slice_in_dim(values, tile + 3 * margin, tile + 4 * margin, axis=axis)
    leading = [(0, 0), (0, 0)]
    trailing = [(0, 0), (0, 0)]
    leading[axis] = (0, tile - margin)
    trailing[axis] = (tile - margin, 0)
    return centre + jnp.pad(upper_rim, leading) + jnp.pad(lower_rim, trailing)


def advance(padded, speed):
    centre = padded[1:-1, 1:-1]
    above_cells = padded[:-2, 1:-1]
    below_cells = padded[2:, 1:-1]
    left_cells = padded[1:-1, :-2]
    right_cells = padded[1:-1, 2:]
    slope_y = 0.5 * (below_cells - above_cells)
    slope_x = 0.5 * (right_cells - left_cells)
    spread = above_cells + below_cells + left_cells + right_cells - 4.0 * centre
    return (
        centre
        - SPEED_GAIN * speed * jnp.sqrt(GRAD_FLOOR + slope_y * slope_y + slope_x * slope_x)
        + SMOOTHING * spread
    )


def body(level_init, target, kernels, corner_doses):
    tile = level_init.shape[0]
    margin = HALO
    freqs = KF
    window = tile + 2 * margin
    tables = make_tables(window, freqs, margin, tile)
    level = level_init.astype(jnp.float32) * 0.125
    trans = jnp.tanh(0.25 * level)
    level_rim = with_halo(level.astype(jnp.bfloat16), (("ty", 0), ("tx", 1)), margin).astype(
        level.dtype
    )
    win_data = jnp.tanh(0.25 * level_rim).astype(jnp.bfloat16)
    kernel_re = kernels[:, :, 0].reshape(-1, freqs, freqs)
    kernel_im = kernels[:, :, 1].reshape(-1, freqs, freqs)
    resist, grad_spec_re, grad_spec_im = tile_pass(
        win_data, target.astype(jnp.float32), kernel_re, kernel_im, corner_doses, tables
    )
    grad_spec_re, grad_spec_im = (
        lax.psum(grad_spec_re.astype(jnp.bfloat16), "corner").astype(jnp.float32),
        lax.psum(grad_spec_im.astype(jnp.bfloat16), "corner").astype(jnp.float32),
    )
    grad_window = window_grad(grad_spec_re, grad_spec_im, tables)
    framed_grad = with_halo(grad_window, (("ty", 0), ("tx", 1)), margin).astype(jnp.float32)
    grad_trans = fold_axis(fold_axis(framed_grad, tile, margin, 0), tile, margin, 1)
    speed = grad_trans * 0.25 * (1.0 - trans * trans)
    stacked = jnp.stack([level, speed], axis=1)
    grown = with_halo(stacked.astype(jnp.bfloat16), (("ty", 0), ("tx", 2)), LS_STEPS).astype(
        stacked.dtype
    )
    level_ext = grown[:, 0, :]
    speed_ext = grown[:, 1, :]
    extent = tile + 2 * LS_STEPS
    offsets = jnp.arange(extent, dtype=jnp.int32) - LS_STEPS
    rows_at = lax.axis_index("ty") * tile + offsets
    cols_at = lax.axis_index("tx") * tile + offsets
    inside_rows = (rows_at >= 0) & (rows_at < tile * lax.axis_size("ty"))
    inside_cols = (cols_at >= 0) & (cols_at < tile * lax.axis_size("tx"))
    inside = (inside_rows[:, None] & inside_cols[None, :]).astype(jnp.float32)
    for repeat in range(LS_STEPS):
        speed_ext = speed_ext[1:-1, 1:-1]
        level_ext = (
            advance(level_ext, speed_ext)
            * inside[repeat + 1 : extent - repeat - 1, repeat + 1 : extent - repeat - 1]
        )
    level = level_ext
    return (resist, level)


def solution(mesh):
    in_specs = (P("ty", "tx"), P("ty", "tx"), P("corner", None, None, None, None), P("corner"))
    out_specs = (P("corner", "ty", "tx"), P("ty", "tx"))
    return jax.shard_map(body, mesh=mesh, in_specs=in_specs, out_specs=out_specs, check_vma=False)
```

profile of v0, /device:TPU:0, one launch (start us, length us, event | category | flops | bytes accessed | tf_op | source)
XLA Modules:
  0.0 120.3 jit_solution(7993260280615964932)
XLA Ops:
  8.2 4.9 %collective-permute-start = (bf16[128,256]{1,0:T(8,128)(2,1)S(1)}, bf16[128,256]{1,0:T(8,128)(2,1)S(1)}, u32[]{:S(2)}, u32[]{:S(2)}) collective-permute-start(bf16[128,256]{1,0:T(8,128)(2,1)S(1)} %get-tuple-element.26), channel_id=1, source_target_pairs={{0,8},{8,16},{16,24},{1,9},{9,17},{17,25},{2,10},{10,18},{18,26},{... | collective-permute-start | bytes 196616 | tf_op jit(solution)/shard_map/ppermute | solution.py:25
  13.1 1.3 %collective-permute-start.1 = (bf16[128,256]{1,0:T(8,128)(2,1)S(1)}, bf16[128,256]{1,0:T(8,128)(2,1)S(1)}, u32[]{:S(2)}, u32[]{:S(2)}) collective-permute-start(bf16[128,256]{1,0:T(8,128)(2,1)S(1)} %get-tuple-element.27), channel_id=1, source_target_pairs={{8,0},{16,8},{24,16},{9,1},{17,9},{25,17},{10,2},{18,10},{26,18},{... | collective-permute-start | bytes 196616 | tf_op jit(solution)/shard_map/ppermute | solution.py:28
  14.4 1.1 fusion.118
  15.5 1.1 fusion.38
  17.7 1.6 %collective-permute-done.1 = bf16[128,256]{1,0:T(8,128)(2,1)S(1)} collective-permute-done((bf16[128,256]{1,0:T(8,128)(2,1)S(1)}, bf16[128,256]{1,0:T(8,128)(2,1)S(1)}, u32[]{:S(2)}, u32[]{:S(2)}) %collective-permute-start.1) | collective-permute-done | bytes 65568 | tf_op jit(solution)/shard_map/ppermute | solution.py:28
  19.3 3.5 %collective-permute-start.2 = (bf16[512,128]{1,0:T(8,128)(2,1)S(1)}, bf16[512,128]{1,0:T(8,128)(2,1)S(1)}, u32[]{:S(2)}, u32[]{:S(2)}) collective-permute-start(bf16[512,128]{1,0:T(8,128)(2,1)S(1)} %get-tuple-element.24), channel_id=1, source_target_pairs={{0,2},{2,4},{4,6},{1,3},{3,5},{5,7},{8,10},{10,12},{12,14},{9,11},... | collective-permute-start | bytes 393224 | tf_op jit(solution)/shard_map/ppermute | solution.py:25
  22.8 1.3 %collective-permute-start.3 = (bf16[512,128]{1,0:T(8,128)(2,1)S(1)}, bf16[512,128]{1,0:T(8,128)(2,1)S(1)}, u32[]{:S(2)}, u32[]{:S(2)}) collective-permute-start(bf16[512,128]{1,0:T(8,128)(2,1)S(1)} %get-tuple-element.25), channel_id=1, source_target_pairs={{2,0},{4,2},{6,4},{3,1},{5,3},{7,5},{10,8},{12,10},{14,12},{11,9},... | collective-permute-start | bytes 393224 | tf_op jit(solution)/shard_map/ppermute | solution.py:28
  25.3 4.4 %collective-permute-done.3 = bf16[512,128]{1,0:T(8,128)(2,1)S(1)} collective-permute-done((bf16[512,128]{1,0:T(8,128)(2,1)S(1)}, bf16[512,128]{1,0:T(8,128)(2,1)S(1)}, u32[]{:S(2)}, u32[]{:S(2)}) %collective-permute-start.3) | collective-permute-done | bytes 131104 | tf_op jit(solution)/shard_map/ppermute | solution.py:28
  30.0 1.2 fusion.55
  31.2 1.2 %fusion.56 = f32[128,128]{1,0:T(8,128)S(1)} fusion(s32[128]{0:T(128)S(1)} %iota_add_fusion.1, bf16[256,512]{1,0:T(8,128)(2,1)S(1)} %convolution_convert_fusion.1), kind=kOutput, calls=%fused_computation.112 | convolution fusion | flops 17891328 | bytes 197120 | tf_op jit(solution)/shard_map/dot_general | solution.py:48
  32.4 1.2 %convolution_subtract_fusion.5 = f32[128,128]{1,0:T(8,128)S(1)} fusion(f32[128,128]{1,0:T(8,128)S(1)} %fusion.55, s32[128]{0:T(128)S(1)} %iota_add_fusion.1, bf16[256,512]{1,0:T(8,128)(2,1)S(1)} %convolution_convert_fusion.1), kind=kOutput, calls=%fused_computation.27 | convolution fusion | flops 17907712 | bytes 262656 | tf_op jit(solution)/shard_map/dot_general | solution.py:48
  33.7 1.2 convolution_add_fusion.5
  42.2 18.1 %all-reduce.5.cloned.1.call-done = (bf16[128,128]{0,1:T(8,128)(2,1)}, bf16[128,128]{0,1:T(8,128)(2,1)}) async-done(((bf16[128,128]{0,1:T(8,128)(2,1)}, bf16[128,128]{0,1:T(8,128)(2,1)}), (bf16[128,128]{0,1:T(8,128)(2,1)}, bf16[128,128]{0,1:T(8,128)(2,1)})) %all-reduce.5.cloned.1.call-update) | async-done | bytes 65552 | tf_op jit(solution)/shard_map/psum | solution.py:172
  60.3 2.0 %fusion.54 = f32[128,512]{1,0:T(8,128)S(1)} fusion(bf16[128,128]{0,1:T(8,128)(2,1)} %get-tuple-element.5, s32[128]{0:T(128)S(1)} %iota_add_fusion.1), kind=kOutput, calls=%fused_computation.110 | convolution fusion | flops 17825792 | bytes 295424 | tf_op jit(solution)/shard_map/dot_general | solution.py:48
  62.3 2.0 %fusion.53 = f32[128,512]{1,0:T(8,128)S(1)} fusion(bf16[128,128]{0,1:T(8,128)(2,1)} %get-tuple-element.4, s32[128]{0:T(128)S(1)} %iota_add_fusion.1), kind=kOutput, calls=%fused_computation.109 | convolution fusion | flops 17825792 | bytes 295424 | tf_op jit(solution)/shard_map/dot_general | solution.py:48
  64.3 1.4 %fusion.8 = bf16[128,512]{1,0:T(8,128)(2,1)S(1)} fusion(f32[128,512]{1,0:T(8,128)S(1)} %fusion.54, bf16[128,128]{0,1:T(8,128)(2,1)S(1)} %copy-done.4, s32[128]{0:T(128)S(1)} %iota_add_fusion.1), kind=kOutput, calls=%fused_computation.24 | convolution fusion | flops 18022400 | bytes 426496 | tf_op jit(solution)/shard_map/dot_general | solution.py:48
  65.7 1.2 fusion.9
  67.2 3.7 %collective-permute-start.4 = (bf16[128,512]{1,0:T(8,128)(2,1)S(1)}, bf16[128,512]{1,0:T(8,128)(2,1)S(1)}, u32[]{:S(2)}, u32[]{:S(2)}) collective-permute-start(bf16[128,512]{1,0:T(8,128)(2,1)S(1)} %get-tuple-element.14), channel_id=1, source_target_pairs={{0,8},{8,16},{16,24},{1,9},{9,17},{17,25},{2,10},{10,18},{18,26},{... | collective-permute-start | bytes 393224 | tf_op jit(solution)/shard_map/ppermute | solution.py:25
  70.9 1.3 %collective-permute-start.5 = (bf16[128,512]{1,0:T(8,128)(2,1)S(1)}, bf16[128,512]{1,0:T(8,128)(2,1)S(1)}, u32[]{:S(2)}, u32[]{:S(2)}) collective-permute-start(bf16[128,512]{1,0:T(8,128)(2,1)S(1)} %get-tuple-element.15), channel_id=1, source_target_pairs={{8,0},{16,8},{24,16},{9,1},{17,9},{25,17},{10,2},{18,10},{26,18},{... | collective-permute-start | bytes 393224 | tf_op jit(solution)/shard_map/ppermute | solution.py:28
  72.2 1.8 %collective-permute-done.4 = bf16[128,512]{1,0:T(8,128)(2,1)S(1)} collective-permute-done((bf16[128,512]{1,0:T(8,128)(2,1)S(1)}, bf16[128,512]{1,0:T(8,128)(2,1)S(1)}, u32[]{:S(2)}, u32[]{:S(2)}) %collective-permute-start.4) | collective-permute-done | bytes 131104 | tf_op jit(solution)/shard_map/ppermute | solution.py:25
  74.1 4.7 %collective-permute-done.5 = bf16[128,512]{1,0:T(8,128)(2,1)S(1)} collective-permute-done((bf16[128,512]{1,0:T(8,128)(2,1)S(1)}, bf16[128,512]{1,0:T(8,128)(2,1)S(1)}, u32[]{:S(2)}, u32[]{:S(2)}) %collective-permute-start.5) | collective-permute-done | bytes 131104 | tf_op jit(solution)/shard_map/ppermute | solution.py:28
  78.8 3.4 %collective-permute-start.6 = (bf16[768,128]{1,0:T(8,128)(2,1)S(1)}, bf16[768,128]{1,0:T(8,128)(2,1)S(1)}, u32[]{:S(2)}, u32[]{:S(2)}) collective-permute-start(bf16[768,128]{1,0:T(8,128)(2,1)S(1)} %get-tuple-element.8), channel_id=1, source_target_pairs={{0,2},{2,4},{4,6},{1,3},{3,5},{5,7},{8,10},{10,12},{12,14},{9,11},... | collective-permute-start | bytes 589832 | tf_op jit(solution)/shard_map/ppermute | solution.py:25
  82.2 1.3 %collective-permute-start.7 = (bf16[768,128]{1,0:T(8,128)(2,1)S(1)}, bf16[768,128]{1,0:T(8,128)(2,1)S(1)}, u32[]{:S(2)}, u32[]{:S(2)}) collective-permute-start(bf16[768,128]{1,0:T(8,128)(2,1)S(1)} %get-tuple-element.9), channel_id=1, source_target_pairs={{2,0},{4,2},{6,4},{3,1},{5,3},{7,5},{10,8},{12,10},{14,12},{11,9},... | collective-permute-start | bytes 589832 | tf_op jit(solution)/shard_map/ppermute | solution.py:28
  83.6 2.5 %collective-permute-done.6 = bf16[768,128]{1,0:T(8,128)(2,1)S(1)} collective-permute-done((bf16[768,128]{1,0:T(8,128)(2,1)S(1)}, bf16[768,128]{1,0:T(8,128)(2,1)S(1)}, u32[]{:S(2)}, u32[]{:S(2)}) %collective-permute-start.6) | collective-permute-done | bytes 196640 | tf_op jit(solution)/shard_map/ppermute | solution.py:25
  86.0 4.1 %collective-permute-done.7 = bf16[768,128]{1,0:T(8,128)(2,1)S(1)} collective-permute-done((bf16[768,128]{1,0:T(8,128)(2,1)S(1)}, bf16[768,128]{1,0:T(8,128)(2,1)S(1)}, u32[]{:S(2)}, u32[]{:S(2)}) %collective-permute-start.7) | collective-permute-done | bytes 196640 | tf_op jit(solution)/shard_map/ppermute | solution.py:28
  91.2 3.3 %collective-permute-start.8 = (bf16[3,2,256]{2,0,1:T(4,128)(2,1)S(1)}, bf16[3,2,256]{2,0,1:T(4,128)(2,1)S(1)}, u32[]{:S(2)}, u32[]{:S(2)}) collective-permute-start(bf16[3,2,256]{2,0,1:T(4,128)(2,1)S(1)} %get-tuple-element.18), channel_id=1, source_target_pairs={{0,8},{8,16},{16,24},{1,9},{9,17},{17,25},{2,10},{10,18},{18,26},{... | collective-permute-start | bytes 9224 | tf_op jit(solution)/shard_map/ppermute | solution.py:25
  94.5 1.3 %collective-permute-start.9 = (bf16[3,2,256]{2,0,1:T(4,128)(2,1)S(1)}, bf16[3,2,256]{2,0,1:T(4,128)(2,1)S(1)}, u32[]{:S(2)}, u32[]{:S(2)}) collective-permute-start(bf16[3,2,256]{2,0,1:T(4,128)(2,1)S(1)} %get-tuple-element.19), channel_id=1, source_target_pairs={{8,0},{16,8},{24,16},{9,1},{17,9},{25,17},{10,2},{18,10},{26,18},{... | collective-permute-start | bytes 9224 | tf_op jit(solution)/shard_map/ppermute | solution.py:28
  95.8 4.2 %collective-permute-done.9 = bf16[3,2,256]{2,0,1:T(4,128)(2,1)S(1)} collective-permute-done((bf16[3,2,256]{2,0,1:T(4,128)(2,1)S(1)}, bf16[3,2,256]{2,0,1:T(4,128)(2,1)S(1)}, u32[]{:S(2)}, u32[]{:S(2)}) %collective-permute-start.9) | collective-permute-done | bytes 3104 | tf_op jit(solution)/shard_map/ppermute | solution.py:28
  100.2 3.4 %collective-permute-start.10 = (bf16[262,2,3]{2,0,1:T(8,128)(2,1)S(1)}, bf16[262,2,3]{2,0,1:T(8,128)(2,1)S(1)}, u32[]{:S(2)}, u32[]{:S(2)}) collective-permute-start(bf16[262,2,3]{2,0,1:T(8,128)(2,1)S(1)} %get-tuple-element.16), channel_id=1, source_target_pairs={{0,2},{2,4},{4,6},{1,3},{3,5},{5,7},{8,10},{10,12},{12,14},{9,11},... | collective-permute-start | bytes 9440 | tf_op jit(solution)/shard_map/ppermute | solution.py:25
  103.6 1.3 %collective-permute-start.11 = (bf16[262,2,3]{2,0,1:T(8,128)(2,1)S(1)}, bf16[262,2,3]{2,0,1:T(8,128)(2,1)S(1)}, u32[]{:S(2)}, u32[]{:S(2)}) collective-permute-start(bf16[262,2,3]{2,0,1:T(8,128)(2,1)S(1)} %get-tuple-element.17), channel_id=1, source_target_pairs={{2,0},{4,2},{6,4},{3,1},{5,3},{7,5},{10,8},{12,10},{14,12},{11,9},... | collective-permute-start | bytes 9440 | tf_op jit(solution)/shard_map/ppermute | solution.py:28
  106.1 4.4 %collective-permute-done.11 = bf16[262,2,3]{2,0,1:T(8,128)(2,1)S(1)} collective-permute-done((bf16[262,2,3]{2,0,1:T(8,128)(2,1)S(1)}, bf16[262,2,3]{2,0,1:T(8,128)(2,1)S(1)}, u32[]{:S(2)}, u32[]{:S(2)}) %collective-permute-start.11) | collective-permute-done | bytes 3176 | tf_op jit(solution)/shard_map/ppermute | solution.py:28
  112.3 1.2 slice_multiply_fusion.4
  (63 shorter events, 14.7 us)
Async XLA Ops:
  7.2 53.2 %all-reduce.5.cloned.1.call-start = ((), (), s32[]{:S(2)}) async-start(), calls=%async_computation | async-start | bytes 131072 | tf_op jit(solution)/shard_map/psum | solution.py:172
  8.2 9.5 %collective-permute-start = (bf16[128,256]{1,0:T(8,128)(2,1)S(1)}, bf16[128,256]{1,0:T(8,128)(2,1)S(1)}, u32[]{:S(2)}, u32[]{:S(2)}) collective-permute-start(bf16[128,256]{1,0:T(8,128)(2,1)S(1)} %get-tuple-element.26), channel_id=1, source_target_pairs={{0,8},{8,16},{16,24},{1,9},{9,17},{17,25},{2,10},{10,18},{18,26},{... | collective-permute-start | bytes 196616 | tf_op jit(solution)/shard_map/ppermute | solution.py:25
  13.1 6.2 %collective-permute-start.1 = (bf16[128,256]{1,0:T(8,128)(2,1)S(1)}, bf16[128,256]{1,0:T(8,128)(2,1)S(1)}, u32[]{:S(2)}, u32[]{:S(2)}) collective-permute-start(bf16[128,256]{1,0:T(8,128)(2,1)S(1)} %get-tuple-element.27), channel_id=1, source_target_pairs={{8,0},{16,8},{24,16},{9,1},{17,9},{25,17},{10,2},{18,10},{26,18},{... | collective-permute-start | bytes 196616 | tf_op jit(solution)/shard_map/ppermute | solution.py:28
  19.3 6.0 %collective-permute-start.2 = (bf16[512,128]{1,0:T(8,128)(2,1)S(1)}, bf16[512,128]{1,0:T(8,128)(2,1)S(1)}, u32[]{:S(2)}, u32[]{:S(2)}) collective-permute-start(bf16[512,128]{1,0:T(8,128)(2,1)S(1)} %get-tuple-element.24), channel_id=1, source_target_pairs={{0,2},{2,4},{4,6},{1,3},{3,5},{5,7},{8,10},{10,12},{12,14},{9,11},... | collective-permute-start | bytes 393224 | tf_op jit(solution)/shard_map/ppermute | solution.py:25
  22.8 6.9 %collective-permute-start.3 = (bf16[512,128]{1,0:T(8,128)(2,1)S(1)}, bf16[512,128]{1,0:T(8,128)(2,1)S(1)}, u32[]{:S(2)}, u32[]{:S(2)}) collective-permute-start(bf16[512,128]{1,0:T(8,128)(2,1)S(1)} %get-tuple-element.25), channel_id=1, source_target_pairs={{2,0},{4,2},{6,4},{3,1},{5,3},{7,5},{10,8},{12,10},{14,12},{11,9},... | collective-permute-start | bytes 393224 | tf_op jit(solution)/shard_map/ppermute | solution.py:28
  37.1 1.0 copy-start.1
  60.3 3.9 %copy-start.4 = (bf16[128,128]{0,1:T(8,128)(2,1)S(1)}, bf16[128,128]{0,1:T(8,128)(2,1)}, u32[]{:S(2)}) copy-start(bf16[128,128]{0,1:T(8,128)(2,1)} %get-tuple-element.4) | copy-start | bytes 98308
  62.3 3.4 %copy-start.3 = (bf16[128,128]{0,1:T(8,128)(2,1)S(1)}, bf16[128,128]{0,1:T(8,128)(2,1)}, u32[]{:S(2)}) copy-start(bf16[128,128]{0,1:T(8,128)(2,1)} %get-tuple-element.5) | copy-start | bytes 98308
  66.9 16.7 %copy-start = (s32[256,256]{1,0:T(8,128)S(1)}, s32[256,256]{1,0:T(8,128)}, u32[]{:S(2)}) copy-start(s32[256,256]{1,0:T(8,128)} %param.4) | copy-start | bytes 786436
  67.2 6.8 %collective-permute-start.4 = (bf16[128,512]{1,0:T(8,128)(2,1)S(1)}, bf16[128,512]{1,0:T(8,128)(2,1)S(1)}, u32[]{:S(2)}, u32[]{:S(2)}) collective-permute-start(bf16[128,512]{1,0:T(8,128)(2,1)S(1)} %get-tuple-element.14), channel_id=1, source_target_pairs={{0,8},{8,16},{16,24},{1,9},{9,17},{17,25},{2,10},{10,18},{18,26},{... | collective-permute-start | bytes 393224 | tf_op jit(solution)/shard_map/ppermute | solution.py:25
  70.9 7.9 %collective-permute-start.5 = (bf16[128,512]{1,0:T(8,128)(2,1)S(1)}, bf16[128,512]{1,0:T(8,128)(2,1)S(1)}, u32[]{:S(2)}, u32[]{:S(2)}) collective-permute-start(bf16[128,512]{1,0:T(8,128)(2,1)S(1)} %get-tuple-element.15), channel_id=1, source_target_pairs={{8,0},{16,8},{24,16},{9,1},{17,9},{25,17},{10,2},{18,10},{26,18},{... | collective-permute-start | bytes 393224 | tf_op jit(solution)/shard_map/ppermute | solution.py:28
  78.8 7.2 %collective-permute-start.6 = (bf16[768,128]{1,0:T(8,128)(2,1)S(1)}, bf16[768,128]{1,0:T(8,128)(2,1)S(1)}, u32[]{:S(2)}, u32[]{:S(2)}) collective-permute-start(bf16[768,128]{1,0:T(8,128)(2,1)S(1)} %get-tuple-element.8), channel_id=1, source_target_pairs={{0,2},{2,4},{4,6},{1,3},{3,5},{5,7},{8,10},{10,12},{12,14},{9,11},... | collective-permute-start | bytes 589832 | tf_op jit(solution)/shard_map/ppermute | solution.py:25
  82.2 7.9 %collective-permute-start.7 = (bf16[768,128]{1,0:T(8,128)(2,1)S(1)}, bf16[768,128]{1,0:T(8,128)(2,1)S(1)}, u32[]{:S(2)}, u32[]{:S(2)}) collective-permute-start(bf16[768,128]{1,0:T(8,128)(2,1)S(1)} %get-tuple-element.9), channel_id=1, source_target_pairs={{2,0},{4,2},{6,4},{3,1},{5,3},{7,5},{10,8},{12,10},{14,12},{11,9},... | collective-permute-start | bytes 589832 | tf_op jit(solution)/shard_map/ppermute | solution.py:28
  90.2 0.7 copy-start.2
  91.2 4.6 %collective-permute-start.8 = (bf16[3,2,256]{2,0,1:T(4,128)(2,1)S(1)}, bf16[3,2,256]{2,0,1:T(4,128)(2,1)S(1)}, u32[]{:S(2)}, u32[]{:S(2)}) collective-permute-start(bf16[3,2,256]{2,0,1:T(4,128)(2,1)S(1)} %get-tuple-element.18), channel_id=1, source_target_pairs={{0,8},{8,16},{16,24},{1,9},{9,17},{17,25},{2,10},{10,18},{18,26},{... | collective-permute-start | bytes 9224 | tf_op jit(solution)/shard_map/ppermute | solution.py:25
  94.5 5.5 %collective-permute-start.9 = (bf16[3,2,256]{2,0,1:T(4,128)(2,1)S(1)}, bf16[3,2,256]{2,0,1:T(4,128)(2,1)S(1)}, u32[]{:S(2)}, u32[]{:S(2)}) collective-permute-start(bf16[3,2,256]{2,0,1:T(4,128)(2,1)S(1)} %get-tuple-element.19), channel_id=1, source_target_pairs={{8,0},{16,8},{24,16},{9,1},{17,9},{25,17},{10,2},{18,10},{26,18},{... | collective-permute-start | bytes 9224 | tf_op jit(solution)/shard_map/ppermute | solution.py:28
  100.2 5.9 %collective-permute-start.10 = (bf16[262,2,3]{2,0,1:T(8,128)(2,1)S(1)}, bf16[262,2,3]{2,0,1:T(8,128)(2,1)S(1)}, u32[]{:S(2)}, u32[]{:S(2)}) collective-permute-start(bf16[262,2,3]{2,0,1:T(8,128)(2,1)S(1)} %get-tuple-element.16), channel_id=1, source_target_pairs={{0,2},{2,4},{4,6},{1,3},{3,5},{5,7},{8,10},{10,12},{12,14},{9,11},... | collective-permute-start | bytes 9440 | tf_op jit(solution)/shard_map/ppermute | solution.py:25
  103.6 6.9 %collective-permute-start.11 = (bf16[262,2,3]{2,0,1:T(8,128)(2,1)S(1)}, bf16[262,2,3]{2,0,1:T(8,128)(2,1)S(1)}, u32[]{:S(2)}, u32[]{:S(2)}) collective-permute-start(bf16[262,2,3]{2,0,1:T(8,128)(2,1)S(1)} %get-tuple-element.17), channel_id=1, source_target_pairs={{2,0},{4,2},{6,4},{3,1},{5,3},{7,5},{10,8},{12,10},{14,12},{11,9},... | collective-permute-start | bytes 9440 | tf_op jit(solution)/shard_map/ppermute | solution.py:28
Sparse Core Ops, SparseCore 0:
  42.3 17.9 all-reduce.4
where the time goes:
time: 121 us; the launch traced here: 120 us
  waiting for transfers between devices  47.6 us (39%)
  starting transfers between devices  29.9 us (25%)
  matrix products  17.6 us (15%)
  between operations  15.2 us (13%)
  other arithmetic  7.13 us (6%)
  local copies, waits for them, and re-layouts  2.89 us (2%)
    ppermute x6, waiting for transfers between devices, with_halo(): lax.ppermute(lax.slice_in_dim(block, 0, width, axis=dim), axis, backward)  23.3 us
    ppermute x6, starting transfers between devices, with_halo(): lax.ppermute(lax.slice_in_dim(block, block.shape[dim] - width, None, axis...  22.1 us
    psum x1, waiting for transfers between devices, body(): lax.psum(grad_spec_im.astype(jnp.bfloat16), 'corner').astype(jnp.float32)  18.1 us
    dot_general x9, matrix products, matmul(): return jnp.dot(left, right, preferred_element_type=jnp.float32)  11.6 us
    ppermute x6, starting transfers between devices, with_halo(): lax.ppermute(lax.slice_in_dim(block, 0, width, axis=dim), axis, backward)  7.75 us
    ppermute x6, waiting for transfers between devices, with_halo(): lax.ppermute(lax.slice_in_dim(block, block.shape[dim] - width, None, axis...  6.14 us
    dot_general x16, matrix products, batched(): return jnp.einsum(form, left, right, preferred_element_type=jnp.float32)  5.61 us
    mul x3, other arithmetic, body(): advance(level_ext, speed_ext)  2.64 us
  transfers between devices with their start and end apart: 13, of which 11 were waited for; matrix products, arithmetic and copies ran while one was open for 3% of the time, Pallas kernels for 0%

commit v1 on v0

v1 whole, which is shorter than its diff:
```python
import functools
import math

import jax
import jax.numpy as jnp
import numpy as np
from jax import lax
from jax.experimental import pallas as pl
from jax.experimental.pallas import tpu as pltpu
from jax.sharding import PartitionSpec as P

HALO = 128
KF = 128
LS_STEPS = 3

STEEPNESS = 4.0
THRESHOLD = 1.0
SPEED_GAIN = 4.0
SMOOTHING = 0.24
GRAD_FLOOR = 0.25

RIM = 16


def make_tables(tile, margin, freqs):
    window = tile + 2 * margin
    shifts = np.arange(freqs) - freqs // 2
    places = np.arange(window)
    angles = 2.0 * math.pi / window * (shifts[:, None] * places[None, :] % window)
    scaled = 1.0 / math.sqrt(window)
    cos = np.cos(angles) * scaled
    sin = np.sin(angles) * scaled
    stacked = np.concatenate([cos, -sin], axis=0)
    inv_cos = cos[:, margin : margin + tile].T
    inv_sin = sin[:, margin : margin + tile].T
    inverse = np.block([[inv_cos, -inv_sin], [inv_sin, inv_cos]])

    def rim(width, offset):
        out = np.zeros((2 * freqs, width))
        for step in range(LS_STEPS):
            for place, at in ((tile + step, step), (step - LS_STEPS, width - LS_STEPS + step)):
                if 0 <= place + offset < window:
                    out[:, at] = stacked[:, place + offset]
        return out

    offsets = (margin + tile, margin, margin - tile)
    rim_cols = np.stack([rim(margin, offset) for offset in offsets])
    rim_rows = [rim(RIM, offset).T for offset in offsets]
    own_rows = np.concatenate([stacked[:, margin : margin + tile].T, rim_rows[1]])
    send_rows = np.stack(
        [
            np.concatenate([stacked[:, tile + margin :].T, rim_rows[0]]),
            np.concatenate([stacked[:, :margin].T, rim_rows[2]]),
        ]
    )
    as_const = lambda values: np.asarray(values, np.float32).astype(jnp.bfloat16)
    return {
        "fwd": as_const(stacked),
        "fwd_t": as_const(stacked.T),
        "inv": as_const(inverse),
        "inv_t": as_const(inverse.T),
        "rim_cols": as_const(rim_cols),
        "own_rows": as_const(own_rows),
        "send_rows": as_const(send_rows),
    }


def dot(left, right):
    return jnp.dot(left, right, preferred_element_type=jnp.float32)


def dot_general(left, right, left_dim, right_dim):
    return lax.dot_general(
        left, right, (((left_dim,), (right_dim,)), ((), ())), preferred_element_type=jnp.float32
    )


def by_core(core, first, second):
    return jnp.where(core == 0, first, second)


def lift_kernel(level_ref, mine_ref, other_ref, fwd_ref, lift_ref, send_ref):
    core = lax.axis_index("corner")
    tile = level_ref.shape[0]
    margin = mine_ref.shape[0]
    level = level_ref[...].astype(jnp.float32) * 0.125
    mine = mine_ref[...].astype(jnp.float32)
    other = other_ref[...].astype(jnp.float32)
    above = by_core(core, mine, other)
    below = by_core(core, other, mine)
    squash = lambda values: jnp.tanh(0.25 * values).astype(jnp.bfloat16)
    lift = (
        dot(fwd_ref[:, :margin], squash(above))
        + dot(fwd_ref[:, margin : margin + tile], squash(level))
        + dot(fwd_ref[:, margin + tile :], squash(below))
    ).astype(jnp.bfloat16)
    lift_ref[...] = lift
    rows = lift.shape[0]
    send_ref[:rows, :] = by_core(core, lift[:, tile - margin :], lift[:, :margin])
    at = lax.broadcasted_iota(jnp.int32, (RIM, margin), 0)
    lane = lax.broadcasted_iota(jnp.int32, (RIM, margin), 1)
    first = by_core(core, margin - LS_STEPS, 0)
    pick = ((lane == first + at) & (at < LS_STEPS)).astype(jnp.bfloat16)
    rim = jnp.where(
        lax.broadcasted_iota(jnp.int32, (RIM, tile), 0) < RIM // 2,
        below[:RIM],
        above[margin - RIM :],
    )
    strip = by_core(core, level[:, tile - margin :], level[:, :margin]).astype(jnp.bfloat16)
    rim_strip = by_core(core, rim[:, tile - margin :], rim[:, :margin]).astype(jnp.bfloat16)
    for block in range(tile // margin):
        picked = dot_general(pick, strip[block * margin : (block + 1) * margin], 1, 1)
        send_ref[rows + block * RIM : rows + (block + 1) * RIM, :] = picked.astype(jnp.bfloat16)
    padded = jnp.concatenate([rim_strip, jnp.zeros((margin - RIM, margin), jnp.bfloat16)], axis=0)
    block = tile // margin
    send_ref[rows + block * RIM : rows + (block + 1) * RIM, :] = dot_general(
        pick, padded, 1, 1
    ).astype(jnp.bfloat16)


def corner_kernel(
    dose_ref,
    lift_ref,
    mine_ref,
    other_ref,
    kernels_ref,
    target_ref,
    fwd_t_ref,
    inv_ref,
    inv_t_ref,
    resist_ref,
    grad_ref,
    blur_ref,
    proj_ref,
    field_ref,
    back_ref,
):
    core = lax.axis_index("corner")
    tile = target_ref.shape[0]
    rows = lift_ref.shape[0]
    freqs = rows // 2
    margin = mine_ref.shape[1]
    count = kernels_ref.shape[0]
    mine = mine_ref[:rows, :]
    other = other_ref[:rows, :]
    mixed = (
        dot(by_core(core, mine, other), fwd_t_ref[:margin, :])
        + dot(lift_ref[...], fwd_t_ref[margin : margin + tile, :])
        + dot(by_core(core, other, mine), fwd_t_ref[margin + tile :, :])
    )
    spec_re = mixed[:freqs, :freqs] - mixed[freqs:, freqs:]
    spec_im = mixed[:freqs, freqs:] + mixed[freqs:, :freqs]
    for g in range(count):
        kernel_re = kernels_ref[g, 0]
        kernel_im = kernels_ref[g, 1]
        cols = slice(g * freqs, (g + 1) * freqs)
        blur_ref[:freqs, cols] = (kernel_re * spec_re - kernel_im * spec_im).astype(jnp.bfloat16)
        blur_ref[freqs:, cols] = (kernel_re * spec_im + kernel_im * spec_re).astype(jnp.bfloat16)
    proj_ref[...] = dot(inv_ref[...], blur_ref[...]).astype(jnp.bfloat16)
    power = jnp.zeros((tile, tile), jnp.float32)
    for g in range(count):
        cols = slice(g * freqs, (g + 1) * freqs)
        pair = jnp.concatenate([proj_ref[:tile, cols], proj_ref[tile:, cols]], axis=1)
        field = dot(pair, inv_t_ref[...])
        field_ref[g] = field
        power = power + (field[:, :tile] * field[:, :tile] + field[:, tile:] * field[:, tile:])
    dose = dose_ref[0]
    resist = jax.nn.sigmoid(STEEPNESS * (dose * power - THRESHOLD))
    resist_ref[...] = resist
    goal = target_ref[...].astype(jnp.float32)
    sens = 2.0 * (resist - goal) * STEEPNESS * dose * resist * (1.0 - resist)
    twice = 2.0 * sens
    twice = jnp.concatenate([twice, twice], axis=1)
    for g in range(count):
        cols = slice(g * freqs, (g + 1) * freqs)
        back = dot((twice * field_ref[g]).astype(jnp.bfloat16), inv_ref[...]).astype(jnp.bfloat16)
        back_ref[:tile, cols] = back[:, :freqs]
        back_ref[tile:, cols] = back[:, freqs:]
    blurred = dot(inv_t_ref[...], back_ref[...])
    grad_re = jnp.zeros((freqs, freqs), jnp.float32)
    grad_im = jnp.zeros((freqs, freqs), jnp.float32)
    for g in range(count):
        kernel_re = kernels_ref[g, 0]
        kernel_im = kernels_ref[g, 1]
        cols = slice(g * freqs, (g + 1) * freqs)
        blur_re = blurred[:freqs, cols]
        blur_im = blurred[freqs:, cols]
        grad_re = grad_re + (kernel_re * blur_re + kernel_im * blur_im)
        grad_im = grad_im + (kernel_re * blur_im - kernel_im * blur_re)
    grad_ref[:freqs, :] = grad_re
    grad_ref[freqs:, :] = grad_im


def lift_grad_kernel(
    grad_ref, mine_ref, other_ref, fwd_ref, rim_ref, send_rows_ref, lift_ref, send_ref
):
    core = lax.axis_index("corner")
    freqs = grad_ref.shape[0] // 2
    margin = rim_ref.shape[2]
    tile = fwd_ref.shape[1] - 2 * margin
    last = tile + margin

    def both(values):
        low_re = values[:freqs]
        low_im = values[freqs:]
        upper = jnp.concatenate([low_re, low_im], axis=1)
        lower = jnp.concatenate([low_im, -low_re], axis=1)
        return jnp.concatenate([upper, lower], axis=0)

    mine = mine_ref[...]
    other = other_ref[...]
    before = both(by_core(core, mine, other))
    here = both(grad_ref[...])
    after = both(by_core(core, other, mine))
    middle = dot(here, fwd_ref[:, margin : margin + tile])
    lift_ref[:, :margin] = (middle[:, :margin] + dot(before, fwd_ref[:, last:])).astype(
        jnp.bfloat16
    )
    lift_ref[:, tile - margin : tile] = (
        middle[:, tile - margin :] + dot(after, fwd_ref[:, :margin])
    ).astype(jnp.bfloat16)
    lift_ref[:, tile:] = (
        dot(before, rim_ref[0]) + dot(here, rim_ref[1]) + dot(after, rim_ref[2])
    ).astype(jnp.bfloat16)
    send_ref[...] = dot(send_rows_ref[core], lift_ref[...]).astype(jnp.bfloat16)


def frame_kernel(
    lift_ref, own_rows_ref, level_ref, above_ref, below_ref, left_ref, right_ref,
    grad_ref, frame_ref, slope_ref,
):
    core = lax.axis_index("corner")
    tile = level_ref.shape[0]
    margin = above_ref.shape[0]
    rows = lift_ref.shape[0]
    grad_ref[...] = dot(own_rows_ref[...], lift_ref[...])
    mine = above_ref[...].astype(jnp.float32)
    other = below_ref[...].astype(jnp.float32)
    above = by_core(core, mine, other)
    below = by_core(core, other, mine)
    frame_ref[:tile, :tile] = level_ref[...].astype(jnp.float32) * 0.125
    frame_ref[tile:, :tile] = jnp.where(
        lax.broadcasted_iota(jnp.int32, (RIM, tile), 0) < RIM // 2,
        below[:RIM],
        above[margin - RIM :],
    )
    at = lax.broadcasted_iota(jnp.int32, (RIM, margin), 0)
    lane = lax.broadcasted_iota(jnp.int32, (RIM, margin), 1)
    place_left = ((lane == margin - LS_STEPS + at) & (at < LS_STEPS)).astype(jnp.bfloat16)
    place_right = ((lane == at) & (at < LS_STEPS)).astype(jnp.bfloat16)
    for block in range(tile // margin + 1):
        part = slice(rows + block * RIM, rows + (block + 1) * RIM)
        left = by_core(core, left_ref[part, :], right_ref[part, :])
        right = by_core(core, right_ref[part, :], left_ref[part, :])
        placed = dot_general(left, place_left, 0, 0) + dot_general(right, place_right, 0, 0)
        size = margin if block < tile // margin else RIM
        frame_ref[block * margin : block * margin + size, tile:] = placed[:size]
    trans = jnp.tanh(0.25 * frame_ref[...])
    slope_ref[...] = 0.25 * (1.0 - trans * trans)


def advance_kernel(extent, grad_ref, mine_ref, other_ref, frame_ref, slope_ref, out_ref):
    core = lax.axis_index("corner")
    tile = out_ref.shape[0]
    rows, cols = frame_ref.shape
    margin = cols - tile
    mine = mine_ref[...].astype(jnp.float32)
    other = other_ref[...].astype(jnp.float32)
    before = by_core(core, mine, other)
    after = by_core(core, other, mine)
    grad = grad_ref[...] + jnp.concatenate(
        [before[:margin], after[:margin], before[margin:] + after[margin:]], axis=0
    )
    speed = SPEED_GAIN * (grad * slope_ref[...])

    def inside(axis, dim, size, count):
        at = lax.broadcasted_iota(jnp.int32, (rows, cols), dim)
        index = lax.axis_index(axis)
        behind = (at >= tile + LS_STEPS) & (index > 0)
        ahead = (at >= tile) & (at < tile + LS_STEPS) & (index < count - 1)
        return (at < tile) | behind | ahead

    keep = inside("ty", 0, rows, extent[0]) & inside("tx", 1, cols, extent[1])
    level = frame_ref[...]
    for _ in range(LS_STEPS):
        up = pltpu.roll(level, 1, 0)
        down = pltpu.roll(level, rows - 1, 0)
        left = pltpu.roll(level, 1, 1)
        right = pltpu.roll(level, cols - 1, 1)
        slope_y = 0.5 * (down - up)
        slope_x = 0.5 * (right - left)
        spread = up + down + left + right - 4.0 * level
        level = (
            level
            - speed * jnp.sqrt(GRAD_FLOOR + slope_y * slope_y + slope_x * slope_x)
            + SMOOTHING * spread
        )
        level = jnp.where(keep, level, 0.0)
    out_ref[...] = level[:tile, :tile]


def call(kernel, out_shape, *args, scratch=(), smem=0, name=None):
    vmem = pl.BlockSpec(memory_space=pltpu.VMEM)
    in_specs = [pl.BlockSpec(memory_space=pltpu.SMEM)] * smem + [vmem] * (len(args) - smem)
    return pl.pallas_call(
        kernel,
        out_shape=[jax.ShapeDtypeStruct(*item) for item in out_shape],
        in_specs=in_specs,
        out_specs=[vmem] * len(out_shape),
        scratch_shapes=list(scratch),
        compiler_params=pltpu.CompilerParams(vmem_limit_bytes=24 << 20),
        name=name,
    )(*args)


def along(axis, values):
    count = lax.axis_size(axis)
    pairs = []
    for index in range(count - 1):
        pairs.append((index * 2, (index + 1) * 2))
        pairs.append(((index + 1) * 2 + 1, index * 2 + 1))
    return lax.ppermute(values, (axis, "corner"), pairs)


def across(values):
    return lax.ppermute(values, "corner", [(0, 1), (1, 0)])


def body(level_init, target, kernels, corner_doses):
    tile = level_init.shape[0]
    margin = HALO
    freqs = KF
    count = kernels.shape[1]
    tables = make_tables(tile, margin, freqs)
    core = lax.axis_index("corner")
    bf16, f32 = jnp.bfloat16, jnp.float32
    extent = (lax.axis_size("ty"), lax.axis_size("tx"))

    edge = lax.dynamic_slice_in_dim(level_init, (1 - core) * (tile - margin), margin, axis=0)
    rows_mine = along("ty", (edge.astype(f32) * 0.125).astype(bf16))
    rows_other = across(rows_mine)
    strip_rows = (tile // margin + 1) * RIM
    lift, send = call(
        lift_kernel,
        [((2 * freqs, tile), bf16), ((2 * freqs + strip_rows, margin), bf16)],
        level_init, rows_mine, rows_other, tables["fwd"],
        name="lift",
    )
    cols_mine = along("tx", send)
    cols_other = across(cols_mine)
    resist, grad = call(
        corner_kernel,
        [((tile, tile), f32), ((2 * freqs, freqs), f32)],
        corner_doses, lift, cols_mine, cols_other, kernels[0], target,
        tables["fwd_t"], tables["inv"], tables["inv_t"],
        smem=1,
        scratch=[
            pltpu.VMEM((2 * freqs, count * freqs), bf16),
            pltpu.VMEM((2 * tile, count * freqs), bf16),
            pltpu.VMEM((count, tile, 2 * tile), f32),
            pltpu.VMEM((2 * tile, count * freqs), bf16),
        ],
        name="corner",
    )
    grad = (grad + across(grad)).astype(bf16)
    grad_mine = along("tx", grad)
    grad_other = across(grad_mine)
    grad_lift, piece = call(
        lift_grad_kernel,
        [((2 * freqs, tile + margin), bf16), ((margin + RIM, tile + margin), bf16)],
        grad, grad_mine, grad_other, tables["fwd"], tables["rim_cols"], tables["send_rows"],
        name="lift_grad",
    )
    piece_mine = along("ty", piece)
    piece_other = across(piece_mine)
    framed = (tile + RIM, tile + margin)
    own, frame, slope = call(
        frame_kernel,
        [(framed, f32)] * 3,
        grad_lift, tables["own_rows"], level_init, rows_mine, rows_other, cols_mine, cols_other,
        name="frame",
    )
    (level,) = call(
        functools.partial(advance_kernel, extent),
        [((tile, tile), f32)],
        own, piece_mine, piece_other, frame, slope,
        name="advance",
    )
    return (resist[None], level)


def solution(mesh):
    in_specs = (P("ty", "tx"), P("ty", "tx"), P("corner", None, None, None, None), P("corner"))
    out_specs = (P("corner", "ty", "tx"), P("ty", "tx"))
    return jax.shard_map(body, mesh=mesh, in_specs=in_specs, out_specs=out_specs, check_vma=False)
```

time: 121 us -> 46.9 us (0.39)
  the two profiles are of different devices: /device:TPU:0 before, /device:TPU:21 now
where the time goes in v1:
time: 46.9 us; the launch traced here: 46.5 us
  starting transfers between devices  17.8 us (38%)
  waiting for transfers between devices  15.2 us (32%)
  local copies, waits for them, and re-layouts  5.73 us (12%)
  Pallas kernels  5.44 us (12%)
  between operations  1.39 us (3%)
  other arithmetic  0.94 us (2%)
    ppermute x4, waiting for transfers between devices, along(): return lax.ppermute(values, (axis, 'corner'), pairs)  11.5 us
    ppermute x4, starting transfers between devices, along(): return lax.ppermute(values, (axis, 'corner'), pairs)  9.51 us
    ppermute x5, starting transfers between devices, across(): return lax.ppermute(values, 'corner', [(0, 1), (1, 0)])  8.28 us
    unnamed x24, local copies, waits for them, and re-layouts  5.73 us
    pallas_call x5, Pallas kernels, call(): pl.pallas_call(kernel, out_shape=[jax.ShapeDtypeStruct(*item) for item in...  5.44 us
    ppermute x5, waiting for transfers between devices, across(): return lax.ppermute(values, 'corner', [(0, 1), (1, 0)])  3.7 us
  transfers between devices with their start and end apart: 9, of which 9 were waited for; matrix products, arithmetic and copies ran while one was open for 0% of the time, Pallas kernels for 1%

profile of v1, /device:TPU:21, one launch (start us, length us, event | category | flops | bytes accessed | tf_op | source)
XLA Modules:
  0.0 46.5 jit_solution(16291053032994669677)
XLA Ops:
  0.6 0.9 %multiply_convert_fusion = bf16[128,256]{1,0:T(8,128)(2,1)S(1)} fusion(s32[256,256]{1,0:T(8,128)} %level_ref.3, s32[]{:T(128)S(6)} %select_n.3), kind=kLoop, calls=%fused_computation.1 | loop fusion | flops 98304 | bytes 196612 | tf_op jit(solution)/shard_map/convert_element_type | solution.py:340
  1.6 3.1 %collective-permute-start = (bf16[128,256]{1,0:T(8,128)(2,1)S(1)}, bf16[128,256]{1,0:T(8,128)(2,1)S(1)}, u32[]{:S(2)}, u32[]{:S(2)}) collective-permute-start(bf16[128,256]{1,0:T(8,128)(2,1)S(1)} %multiply_convert_fusion), channel_id=1, source_target_pairs={{0,8},{9,1},{8,16},{17,9},{16,24},{25,17},{2,10},{11,3},{10,18},{1... | collective-permute-start | bytes 196616 | tf_op jit(solution)/shard_map/ppermute | solution.py:322
  4.6 1.9 %collective-permute-done.mine_ref.above_ref = bf16[128,256]{1,0:T(8,128)(2,1)S(1)} collective-permute-done((bf16[128,256]{1,0:T(8,128)(2,1)S(1)}, bf16[128,256]{1,0:T(8,128)(2,1)S(1)}, u32[]{:S(2)}, u32[]{:S(2)}) %collective-permute-start) | collective-permute-done | bytes 65568 | tf_op jit(solution)/shard_map/ppermute | solution.py:322
  6.6 2.7 %collective-permute-start.1 = (bf16[128,256]{1,0:T(8,128)(2,1)S(1)}, bf16[128,256]{1,0:T(8,128)(2,1)S(1)}, u32[]{:S(2)}, u32[]{:S(2)}) collective-permute-start(bf16[128,256]{1,0:T(8,128)(2,1)S(1)} %collective-permute-done.mine_ref.above_ref), channel_id=1, source_target_pairs={{0,1},{1,0},{2,3},{3,2},{4,5},{5,4},{6,7},{7,6},{8,9},{9,8},{10,11... | collective-permute-start | bytes 196616 | tf_op jit(solution)/shard_map/ppermute | solution.py:326
  9.3 0.9 %collective-permute-done.1.other_ref.below_ref = bf16[128,256]{1,0:T(8,128)(2,1)S(1)} collective-permute-done((bf16[128,256]{1,0:T(8,128)(2,1)S(1)}, bf16[128,256]{1,0:T(8,128)(2,1)S(1)}, u32[]{:S(2)}, u32[]{:S(2)}) %collective-permute-start.1) | collective-permute-done | bytes 65568 | tf_op jit(solution)/shard_map/ppermute | solution.py:326
  10.2 0.9 %copy-done = s32[256,256]{1,0:T(8,128)S(1)} copy-done((s32[256,256]{1,0:T(8,128)S(1)}, s32[256,256]{1,0:T(8,128)}, u32[]{:S(2)}) %copy-start) | copy-done | bytes 262168
  11.1 0.9 %copy-done.2 = bf16[256,512]{1,0:T(8,128)(2,1)S(1)} copy-done((bf16[256,512]{1,0:T(8,128)(2,1)S(1)}, bf16[256,512]{1,0:T(8,128)(2,1)}, u32[]{:S(2)}) %copy-start.2) | copy-done | bytes 262168
  12.1 0.3 lift.1
  12.4 2.1 %collective-permute-start.2 = (bf16[304,128]{1,0:T(8,128)(2,1)S(1)}, bf16[304,128]{1,0:T(8,128)(2,1)S(1)}, u32[]{:S(2)}, u32[]{:S(2)}) collective-permute-start(bf16[304,128]{1,0:T(8,128)(2,1)S(1)} %get-tuple-element.12), channel_id=1, source_target_pairs={{0,2},{3,1},{2,4},{5,3},{4,6},{7,5},{8,10},{11,9},{10,12},{13,11},... | collective-permute-start | bytes 233480 | tf_op jit(solution)/shard_map/ppermute | solution.py:322
  14.5 3.4 %collective-permute-done.2.mine_ref.left_ref = bf16[304,128]{1,0:T(8,128)(2,1)S(1)} collective-permute-done((bf16[304,128]{1,0:T(8,128)(2,1)S(1)}, bf16[304,128]{1,0:T(8,128)(2,1)S(1)}, u32[]{:S(2)}, u32[]{:S(2)}) %collective-permute-start.2) | collective-permute-done | bytes 77856 | tf_op jit(solution)/shard_map/ppermute | solution.py:322
  17.9 1.2 %collective-permute-start.3 = (bf16[304,128]{1,0:T(8,128)(2,1)S(1)}, bf16[304,128]{1,0:T(8,128)(2,1)S(1)}, u32[]{:S(2)}, u32[]{:S(2)}) collective-permute-start(bf16[304,128]{1,0:T(8,128)(2,1)S(1)} %collective-permute-done.2.mine_ref.left_ref), channel_id=1, source_target_pairs={{0,1},{1,0},{2,3},{3,2},{4,5},{5,4},{6,7},{7,6},{8,9},{9,8},{10,11... | collective-permute-start | bytes 233480 | tf_op jit(solution)/shard_map/ppermute | solution.py:326
  19.7 0.3 collective-permute-done.3.other_ref.right_ref
  20.0 0.9 %copy-done.5 = s32[256,256]{1,0:T(8,128)S(1)} copy-done((s32[256,256]{1,0:T(8,128)S(1)}, s32[256,256]{1,0:T(8,128)}, u32[]{:S(2)}) %copy-start.5) | copy-done | bytes 262168
  20.9 0.9 %copy-done.6 = bf16[512,256]{1,0:T(8,128)(2,1)S(1)} copy-done((bf16[512,256]{1,0:T(8,128)(2,1)S(1)}, bf16[512,256]{1,0:T(8,128)(2,1)}, u32[]{:S(2)}) %copy-start.6) | copy-done | bytes 262168
  21.9 0.9 %copy-done.7 = bf16[512,256]{1,0:T(8,128)(2,1)S(1)} copy-done((bf16[512,256]{1,0:T(8,128)(2,1)S(1)}, bf16[512,256]{1,0:T(8,128)(2,1)}, u32[]{:S(2)}) %copy-start.7) | copy-done | bytes 262168
  22.8 0.9 %copy-done.8 = bf16[256,512]{1,0:T(8,128)(2,1)S(1)} copy-done((bf16[256,512]{1,0:T(8,128)(2,1)S(1)}, bf16[256,512]{1,0:T(8,128)(2,1)}, u32[]{:S(2)}) %copy-start.8) | copy-done | bytes 262168
  23.8 2.2 %corner.1 = (f32[256,256]{1,0:T(8,128)}, f32[256,128]{1,0:T(8,128)S(1)}) custom-call(f32[1]{0:T(128)S(6)} %copy.13.dose_ref, bf16[256,256]{1,0:T(8,128)(2,1)S(1)} %get-tuple-element.11.lift_ref, bf16[304,128]{1,0:T(8,128)(2,1)S(1)} %collective-permute-done.2.mine_ref.left_ref, bf16[304,128]{1,0:T(8,128)(2,1)S(1)} %collective-permute-done.3.other_ref.right_ref, ...), custom_call_target="tpu_custom_call" | custom-call | tf_op jit(solution)/shard_map/corner/pallas_call | solution.py:305
  26.0 0.0 copy-start.3
  26.0 0.4 collective-permute-start.4
  26.5 1.0 %collective-permute-done.4 = f32[256,128]{1,0:T(8,128)S(1)} collective-permute-done((f32[256,128]{1,0:T(8,128)S(1)}, f32[256,128]{1,0:T(8,128)S(1)}, u32[]{:S(2)}, u32[]{:S(2)}) %collective-permute-start.4) | collective-permute-done | bytes 131104 | tf_op jit(solution)/shard_map/ppermute | solution.py:326
  27.5 0.0 copy-start.11
  27.5 2.2 %collective-permute-start.5 = (bf16[256,128]{1,0:T(8,128)(2,1)S(1)}, bf16[256,128]{1,0:T(8,128)(2,1)S(1)}, u32[]{:S(2)}, u32[]{:S(2)}) collective-permute-start(bf16[256,128]{1,0:T(8,128)(2,1)S(1)} %add_convert_fusion.grad_ref), channel_id=1, source_target_pairs={{0,2},{3,1},{2,4},{5,3},{4,6},{7,5},{8,10},{11,9},{10,12},{13,11},... | collective-permute-start | bytes 196616 | tf_op jit(solution)/shard_map/ppermute | solution.py:322
  29.7 2.9 %collective-permute-done.5.mine_ref = bf16[256,128]{1,0:T(8,128)(2,1)S(1)} collective-permute-done((bf16[256,128]{1,0:T(8,128)(2,1)S(1)}, bf16[256,128]{1,0:T(8,128)(2,1)S(1)}, u32[]{:S(2)}, u32[]{:S(2)}) %collective-permute-start.5) | collective-permute-done | bytes 65568 | tf_op jit(solution)/shard_map/ppermute | solution.py:322
  32.6 1.5 %collective-permute-start.6 = (bf16[256,128]{1,0:T(8,128)(2,1)S(1)}, bf16[256,128]{1,0:T(8,128)(2,1)S(1)}, u32[]{:S(2)}, u32[]{:S(2)}) collective-permute-start(bf16[256,128]{1,0:T(8,128)(2,1)S(1)} %collective-permute-done.5.mine_ref), channel_id=1, source_target_pairs={{0,1},{1,0},{2,3},{3,2},{4,5},{5,4},{6,7},{7,6},{8,9},{9,8},{10,11... | collective-permute-start | bytes 196616 | tf_op jit(solution)/shard_map/ppermute | solution.py:326
  34.1 0.9 %collective-permute-done.6.other_ref = bf16[256,128]{1,0:T(8,128)(2,1)S(1)} collective-permute-done((bf16[256,128]{1,0:T(8,128)(2,1)S(1)}, bf16[256,128]{1,0:T(8,128)(2,1)S(1)}, u32[]{:S(2)}, u32[]{:S(2)}) %collective-permute-start.6) | collective-permute-done | bytes 65568 | tf_op jit(solution)/shard_map/ppermute | solution.py:326
  35.1 0.6 %lift_grad.1 = (bf16[256,384]{1,0:T(8,128)(2,1)S(1)}, bf16[144,384]{1,0:T(8,128)(2,1)S(1)}) custom-call(bf16[256,128]{1,0:T(8,128)(2,1)S(1)} %add_convert_fusion.grad_ref, bf16[256,128]{1,0:T(8,128)(2,1)S(1)} %collective-permute-done.5.mine_ref, bf16[256,128]{1,0:T(8,128)(2,1)S(1)} %collective-permute-done.6.other_ref, bf16[256,512]{1,0:T(8,128)(2,1)S(1)} %copy-done.3, ...), custom_call_target="tpu_custom_call" | custom-call | tf_op jit(solution)/shard_map/lift_grad/pallas_call | solution.py:305
  35.6 2.2 %collective-permute-start.7 = (bf16[144,384]{1,0:T(8,128)(2,1)S(1)}, bf16[144,384]{1,0:T(8,128)(2,1)S(1)}, u32[]{:S(2)}, u32[]{:S(2)}) collective-permute-start(bf16[144,384]{1,0:T(8,128)(2,1)S(1)} %get-tuple-element.17), channel_id=1, source_target_pairs={{0,8},{9,1},{8,16},{17,9},{16,24},{25,17},{2,10},{11,3},{10,18},{1... | collective-permute-start | bytes 331784 | tf_op jit(solution)/shard_map/ppermute | solution.py:322
  37.8 3.3 %collective-permute-done.7.mine_ref = bf16[144,384]{1,0:T(8,128)(2,1)S(1)} collective-permute-done((bf16[144,384]{1,0:T(8,128)(2,1)S(1)}, bf16[144,384]{1,0:T(8,128)(2,1)S(1)}, u32[]{:S(2)}, u32[]{:S(2)}) %collective-permute-start.7) | collective-permute-done | bytes 110624 | tf_op jit(solution)/shard_map/ppermute | solution.py:322
  41.1 2.4 %collective-permute-start.8 = (bf16[144,384]{1,0:T(8,128)(2,1)S(1)}, bf16[144,384]{1,0:T(8,128)(2,1)S(1)}, u32[]{:S(2)}, u32[]{:S(2)}) collective-permute-start(bf16[144,384]{1,0:T(8,128)(2,1)S(1)} %collective-permute-done.7.mine_ref), channel_id=1, source_target_pairs={{0,1},{1,0},{2,3},{3,2},{4,5},{5,4},{6,7},{7,6},{8,9},{9,8},{10,11... | collective-permute-start | bytes 331784 | tf_op jit(solution)/shard_map/ppermute | solution.py:326
  43.5 0.3 frame.1
  43.9 0.6 %collective-permute-done.8.other_ref = bf16[144,384]{1,0:T(8,128)(2,1)S(1)} collective-permute-done((bf16[144,384]{1,0:T(8,128)(2,1)S(1)}, bf16[144,384]{1,0:T(8,128)(2,1)S(1)}, u32[]{:S(2)}, u32[]{:S(2)}) %collective-permute-start.8) | collective-permute-done | bytes 110624 | tf_op jit(solution)/shard_map/ppermute | solution.py:326
  44.5 2.0 %advance.1 = f32[256,256]{1,0:T(8,128)} custom-call(f32[272,384]{1,0:T(8,128)S(1)} %get-tuple-element.16.grad_ref, bf16[144,384]{1,0:T(8,128)(2,1)S(1)} %collective-permute-done.7.mine_ref, bf16[144,384]{1,0:T(8,128)(2,1)S(1)} %collective-permute-done.8.other_ref, f32[272,384]{1,0:T(8,128)S(1)} %get-tuple-element.18.frame_ref, ...), custom_call_target="tpu_custom_call" | custom-call | tf_op jit(solution)/shard_map/advance/pallas_call | solution.py:305
  (17 shorter events, 0.0 us)
Async XLA Ops:
  1.6 5.0 %collective-permute-start = (bf16[128,256]{1,0:T(8,128)(2,1)S(1)}, bf16[128,256]{1,0:T(8,128)(2,1)S(1)}, u32[]{:S(2)}, u32[]{:S(2)}) collective-permute-start(bf16[128,256]{1,0:T(8,128)(2,1)S(1)} %multiply_convert_fusion), channel_id=1, source_target_pairs={{0,8},{9,1},{8,16},{17,9},{16,24},{25,17},{2,10},{11,3},{10,18},{1... | collective-permute-start | bytes 196616 | tf_op jit(solution)/shard_map/ppermute | solution.py:322
  6.6 3.6 %collective-permute-start.1 = (bf16[128,256]{1,0:T(8,128)(2,1)S(1)}, bf16[128,256]{1,0:T(8,128)(2,1)S(1)}, u32[]{:S(2)}, u32[]{:S(2)}) collective-permute-start(bf16[128,256]{1,0:T(8,128)(2,1)S(1)} %collective-permute-done.mine_ref.above_ref), channel_id=1, source_target_pairs={{0,1},{1,0},{2,3},{3,2},{4,5},{5,4},{6,7},{7,6},{8,9},{9,8},{10,11... | collective-permute-start | bytes 196616 | tf_op jit(solution)/shard_map/ppermute | solution.py:326
  10.2 0.9 %copy-start = (s32[256,256]{1,0:T(8,128)S(1)}, s32[256,256]{1,0:T(8,128)}, u32[]{:S(2)}) copy-start(s32[256,256]{1,0:T(8,128)} %level_ref.3) | copy-start | bytes 786436
  11.1 0.9 %copy-start.2 = (bf16[256,512]{1,0:T(8,128)(2,1)S(1)}, bf16[256,512]{1,0:T(8,128)(2,1)}, u32[]{:S(2)}) copy-start(bf16[256,512]{1,0:T(8,128)(2,1)} %constant.28.clone.fwd_ref) | copy-start | bytes 786436
  12.1 7.9 %copy-start.4 = (f32[1,5,2,128,128]{4,3,2,1,0:T(8,128)S(1)}, f32[1,5,2,128,128]{4,3,2,1,0:T(8,128)}, u32[]{:S(2)}) copy-start(f32[1,5,2,128,128]{4,3,2,1,0:T(8,128)} %param.13) | copy-start | bytes 1966084
  12.4 5.4 %collective-permute-start.2 = (bf16[304,128]{1,0:T(8,128)(2,1)S(1)}, bf16[304,128]{1,0:T(8,128)(2,1)S(1)}, u32[]{:S(2)}, u32[]{:S(2)}) collective-permute-start(bf16[304,128]{1,0:T(8,128)(2,1)S(1)} %get-tuple-element.12), channel_id=1, source_target_pairs={{0,2},{3,1},{2,4},{5,3},{4,6},{7,5},{8,10},{11,9},{10,12},{13,11},... | collective-permute-start | bytes 233480 | tf_op jit(solution)/shard_map/ppermute | solution.py:322
  17.9 2.1 %collective-permute-start.3 = (bf16[304,128]{1,0:T(8,128)(2,1)S(1)}, bf16[304,128]{1,0:T(8,128)(2,1)S(1)}, u32[]{:S(2)}, u32[]{:S(2)}) collective-permute-start(bf16[304,128]{1,0:T(8,128)(2,1)S(1)} %collective-permute-done.2.mine_ref.left_ref), channel_id=1, source_target_pairs={{0,1},{1,0},{2,3},{3,2},{4,5},{5,4},{6,7},{7,6},{8,9},{9,8},{10,11... | collective-permute-start | bytes 233480 | tf_op jit(solution)/shard_map/ppermute | solution.py:326
  20.0 1.0 %copy-start.5 = (s32[256,256]{1,0:T(8,128)S(1)}, s32[256,256]{1,0:T(8,128)}, u32[]{:S(2)}) copy-start(s32[256,256]{1,0:T(8,128)} %target_ref.1) | copy-start | bytes 786436
  20.9 0.9 %copy-start.6 = (bf16[512,256]{1,0:T(8,128)(2,1)S(1)}, bf16[512,256]{1,0:T(8,128)(2,1)}, u32[]{:S(2)}) copy-start(bf16[512,256]{1,0:T(8,128)(2,1)} %constant.29.clone.fwd_t_ref) | copy-start | bytes 786436
  21.9 0.9 %copy-start.7 = (bf16[512,256]{1,0:T(8,128)(2,1)S(1)}, bf16[512,256]{1,0:T(8,128)(2,1)}, u32[]{:S(2)}) copy-start(bf16[512,256]{1,0:T(8,128)(2,1)} %constant.30.clone.inv_ref) | copy-start | bytes 786436
  22.8 0.9 %copy-start.8 = (bf16[256,512]{1,0:T(8,128)(2,1)S(1)}, bf16[256,512]{1,0:T(8,128)(2,1)}, u32[]{:S(2)}) copy-start(bf16[256,512]{1,0:T(8,128)(2,1)} %constant.31.clone.inv_t_ref) | copy-start | bytes 786436
  23.8 11.3 %copy-start.9 = (bf16[3,256,128]{2,1,0:T(8,128)(2,1)S(1)}, bf16[3,256,128]{2,1,0:T(8,128)(2,1)}, u32[]{:S(2)}) copy-start(bf16[3,256,128]{2,1,0:T(8,128)(2,1)} %constant.32.clone.rim_ref) | copy-start | bytes 589828
  23.8 11.3 %copy-start.10 = (bf16[2,144,256]{2,1,0:T(8,128)(2,1)S(1)}, bf16[2,144,256]{2,1,0:T(8,128)(2,1)}, u32[]{:S(2)}) copy-start(bf16[2,144,256]{2,1,0:T(8,128)(2,1)} %constant.33.clone.send_rows_ref) | copy-start | bytes 442372
  26.0 9.0 %copy-start.3 = (bf16[256,512]{1,0:T(8,128)(2,1)S(1)}, bf16[256,512]{1,0:T(8,128)(2,1)}, u32[]{:S(2)}) copy-start(bf16[256,512]{1,0:T(8,128)(2,1)} %constant.28.clone.fwd_ref) | copy-start | bytes 786436
  26.0 1.4 %collective-permute-start.4 = (f32[256,128]{1,0:T(8,128)S(1)}, f32[256,128]{1,0:T(8,128)S(1)}, u32[]{:S(2)}, u32[]{:S(2)}) collective-permute-start(f32[256,128]{1,0:T(8,128)S(1)} %get-tuple-element.14), channel_id=1, source_target_pairs={{0,1},{1,0},{2,3},{3,2},{4,5},{5,4},{6,7},{7,6},{8,9},{9,8},{10,11... | collective-permute-start | bytes 393224 | tf_op jit(solution)/shard_map/ppermute | solution.py:326
  27.5 16.1 %copy-start.1 = (s32[256,256]{1,0:T(8,128)S(1)}, s32[256,256]{1,0:T(8,128)}, u32[]{:S(2)}) copy-start(s32[256,256]{1,0:T(8,128)} %level_ref.3) | copy-start | bytes 786436
  27.5 16.1 %copy-start.11 = (bf16[272,256]{1,0:T(8,128)(2,1)S(1)}, bf16[272,256]{1,0:T(8,128)(2,1)}, u32[]{:S(2)}) copy-start(bf16[272,256]{1,0:T(8,128)(2,1)} %constant.34.clone.own_rows_ref) | copy-start | bytes 417796
  27.5 5.1 %collective-permute-start.5 = (bf16[256,128]{1,0:T(8,128)(2,1)S(1)}, bf16[256,128]{1,0:T(8,128)(2,1)S(1)}, u32[]{:S(2)}, u32[]{:S(2)}) collective-permute-start(bf16[256,128]{1,0:T(8,128)(2,1)S(1)} %add_convert_fusion.grad_ref), channel_id=1, source_target_pairs={{0,2},{3,1},{2,4},{5,3},{4,6},{7,5},{8,10},{11,9},{10,12},{13,11},... | collective-permute-start | bytes 196616 | tf_op jit(solution)/shard_map/ppermute | solution.py:322
  32.6 2.4 %collective-permute-start.6 = (bf16[256,128]{1,0:T(8,128)(2,1)S(1)}, bf16[256,128]{1,0:T(8,128)(2,1)S(1)}, u32[]{:S(2)}, u32[]{:S(2)}) collective-permute-start(bf16[256,128]{1,0:T(8,128)(2,1)S(1)} %collective-permute-done.5.mine_ref), channel_id=1, source_target_pairs={{0,1},{1,0},{2,3},{3,2},{4,5},{5,4},{6,7},{7,6},{8,9},{9,8},{10,11... | collective-permute-start | bytes 196616 | tf_op jit(solution)/shard_map/ppermute | solution.py:326
  35.6 5.5 %collective-permute-start.7 = (bf16[144,384]{1,0:T(8,128)(2,1)S(1)}, bf16[144,384]{1,0:T(8,128)(2,1)S(1)}, u32[]{:S(2)}, u32[]{:S(2)}) collective-permute-start(bf16[144,384]{1,0:T(8,128)(2,1)S(1)} %get-tuple-element.17), channel_id=1, source_target_pairs={{0,8},{9,1},{8,16},{17,9},{16,24},{25,17},{2,10},{11,3},{10,18},{1... | collective-permute-start | bytes 331784 | tf_op jit(solution)/shard_map/ppermute | solution.py:322
  41.1 3.4 %collective-permute-start.8 = (bf16[144,384]{1,0:T(8,128)(2,1)S(1)}, bf16[144,384]{1,0:T(8,128)(2,1)S(1)}, u32[]{:S(2)}, u32[]{:S(2)}) collective-permute-start(bf16[144,384]{1,0:T(8,128)(2,1)S(1)} %collective-permute-done.7.mine_ref), channel_id=1, source_target_pairs={{0,1},{1,0},{2,3},{3,2},{4,5},{5,4},{6,7},{7,6},{8,9},{9,8},{10,11... | collective-permute-start | bytes 331784 | tf_op jit(solution)/shard_map/ppermute | solution.py:326

commit v2 on v1

--- a/solution.py
+++ b/solution.py
@@ -20,6 +20,7 @@
 GRAD_FLOOR = 0.25
 
 RIM = 16
+PAD = 8
 
 
 def make_tables(tile, margin, freqs):
@@ -49,8 +50,8 @@
     own_rows = np.concatenate([stacked[:, margin : margin + tile].T, rim_rows[1]])
     send_rows = np.stack(
         [
+            np.concatenate([stacked[:, :margin].T, rim_rows[2]]),
             np.concatenate([stacked[:, tile + margin :].T, rim_rows[0]]),
-            np.concatenate([stacked[:, :margin].T, rim_rows[2]]),
         ]
     )
     as_const = lambda values: np.asarray(values, np.float32).astype(jnp.bfloat16)
@@ -96,18 +97,18 @@
     ).astype(jnp.bfloat16)
     lift_ref[...] = lift
     rows = lift.shape[0]
-    send_ref[:rows, :] = by_core(core, lift[:, tile - margin :], lift[:, :margin])
+    send_ref[:rows, :] = by_core(core, lift[:, :margin], lift[:, tile - margin :])
     at = lax.broadcasted_iota(jnp.int32, (RIM, margin), 0)
     lane = lax.broadcasted_iota(jnp.int32, (RIM, margin), 1)
-    first = by_core(core, margin - LS_STEPS, 0)
+    first = by_core(core, 0, margin - LS_STEPS)
     pick = ((lane == first + at) & (at < LS_STEPS)).astype(jnp.bfloat16)
     rim = jnp.where(
         lax.broadcasted_iota(jnp.int32, (RIM, tile), 0) < RIM // 2,
         below[:RIM],
         above[margin - RIM :],
     )
-    strip = by_core(core, level[:, tile - margin :], level[:, :margin]).astype(jnp.bfloat16)
-    rim_strip = by_core(core, rim[:, tile - margin :], rim[:, :margin]).astype(jnp.bfloat16)
+    strip = by_core(core, level[:, :margin], level[:, tile - margin :]).astype(jnp.bfloat16)
+    rim_strip = by_core(core, rim[:, :margin], rim[:, tile - margin :]).astype(jnp.bfloat16)
     for block in range(tile // margin):
         picked = dot_general(pick, strip[block * margin : (block + 1) * margin], 1, 1)
         send_ref[rows + block * RIM : rows + (block + 1) * RIM, :] = picked.astype(jnp.bfloat16)
@@ -236,14 +237,9 @@
     grad_ref[...] = dot(own_rows_ref[...], lift_ref[...])
     mine = above_ref[...].astype(jnp.float32)
     other = below_ref[...].astype(jnp.float32)
-    above = by_core(core, mine, other)
-    below = by_core(core, other, mine)
-    frame_ref[:tile, :tile] = level_ref[...].astype(jnp.float32) * 0.125
-    frame_ref[tile:, :tile] = jnp.where(
-        lax.broadcasted_iota(jnp.int32, (RIM, tile), 0) < RIM // 2,
-        below[:RIM],
-        above[margin - RIM :],
-    )
+    frame_ref[:PAD, :tile] = 0.5 * by_core(core, mine, other)[margin - PAD :]
+    frame_ref[PAD : PAD + tile, :tile] = level_ref[...].astype(jnp.float32) * 0.0625
+    frame_ref[PAD + tile :, :tile] = 0.5 * by_core(core, other, mine)[:PAD]
     at = lax.broadcasted_iota(jnp.int32, (RIM, margin), 0)
     lane = lax.broadcasted_iota(jnp.int32, (RIM, margin), 1)
     place_left = ((lane == margin - LS_STEPS + at) & (at < LS_STEPS)).astype(jnp.bfloat16)
@@ -253,53 +249,112 @@
         left = by_core(core, left_ref[part, :], right_ref[part, :])
         right = by_core(core, right_ref[part, :], left_ref[part, :])
         placed = dot_general(left, place_left, 0, 0) + dot_general(right, place_right, 0, 0)
-        size = margin if block < tile // margin else RIM
-        frame_ref[block * margin : block * margin + size, tile:] = placed[:size]
-    trans = jnp.tanh(0.25 * frame_ref[...])
-    slope_ref[...] = 0.25 * (1.0 - trans * trans)
-
-
-def advance_kernel(extent, grad_ref, mine_ref, other_ref, frame_ref, slope_ref, out_ref):
+        placed = 0.5 * placed
+        if block < tile // margin:
+            start = PAD + block * margin
+            frame_ref[start : start + margin, tile:] = placed
+        else:
+            frame_ref[PAD + tile :, tile:] = placed[:PAD]
+            frame_ref[:PAD, tile:] = placed[PAD:RIM]
+    trans = jnp.tanh(0.5 * frame_ref[...])
+    slope_ref[...] = (SPEED_GAIN * 0.5 * 0.25) * (1.0 - trans * trans)
+
+
+def advance_kernel(
+    extent, grad_ref, mine_ref, other_ref, frame_ref, slope_ref, out_ref, speed_ref, *level_refs
+):
     core = lax.axis_index("corner")
     tile = out_ref.shape[0]
     rows, cols = frame_ref.shape
     margin = cols - tile
-    mine = mine_ref[...].astype(jnp.float32)
-    other = other_ref[...].astype(jnp.float32)
-    before = by_core(core, mine, other)
-    after = by_core(core, other, mine)
-    grad = grad_ref[...] + jnp.concatenate(
-        [before[:margin], after[:margin], before[margin:] + after[margin:]], axis=0
-    )
-    speed = SPEED_GAIN * (grad * slope_ref[...])
-
-    def inside(axis, dim, size, count):
-        at = lax.broadcasted_iota(jnp.int32, (rows, cols), dim)
-        index = lax.axis_index(axis)
-        behind = (at >= tile + LS_STEPS) & (index > 0)
-        ahead = (at >= tile) & (at < tile + LS_STEPS) & (index < count - 1)
-        return (at < tile) | behind | ahead
-
-    keep = inside("ty", 0, rows, extent[0]) & inside("tx", 1, cols, extent[1])
-    level = frame_ref[...]
-    for _ in range(LS_STEPS):
-        up = pltpu.roll(level, 1, 0)
-        down = pltpu.roll(level, rows - 1, 0)
-        left = pltpu.roll(level, 1, 1)
-        right = pltpu.roll(level, cols - 1, 1)
-        slope_y = 0.5 * (down - up)
-        slope_x = 0.5 * (right - left)
-        spread = up + down + left + right - 4.0 * level
-        level = (
-            level
-            - speed * jnp.sqrt(GRAD_FLOOR + slope_y * slope_y + slope_x * slope_x)
-            + SMOOTHING * spread
-        )
-        level = jnp.where(keep, level, 0.0)
-    out_ref[...] = level[:tile, :tile]
-
-
-def call(kernel, out_shape, *args, scratch=(), smem=0, name=None):
+    blocks = cols // margin
+    first, last = level_refs[:blocks], level_refs[blocks:]
+
+    lane = lax.broadcasted_iota(jnp.int32, (PAD, margin), 1)
+    at_ty, at_tx = lax.axis_index("ty"), lax.axis_index("tx")
+    all_lanes = lane >= 0
+    keep_above = all_lanes & (at_ty > 0)
+    keep_below = all_lanes & (at_ty < extent[0] - 1)
+    keep_cols = ((lane >= margin // 2) & (at_tx > 0)) | (
+        (lane < margin // 2) & (at_tx < extent[1] - 1)
+    )
+
+    before = by_core(core, mine_ref[...].astype(jnp.float32), other_ref[...].astype(jnp.float32))
+    after = by_core(core, other_ref[...].astype(jnp.float32), mine_ref[...].astype(jnp.float32))
+    rim = before[margin:] + after[margin:] + grad_ref[tile:]
+    speed_ref[:PAD] = rim[PAD:] * slope_ref[:PAD]
+    speed_ref[PAD + tile :] = rim[:PAD] * slope_ref[PAD + tile :]
+    for half, part in ((0, before), (1, after)):
+        at = half * margin
+        speed_ref[PAD + at : PAD + at + margin] = (
+            grad_ref[at : at + margin] + part[:margin]
+        ) * slope_ref[PAD + at : PAD + at + margin]
+    for ref in level_refs:
+        ref[:PAD] = jnp.zeros((PAD, margin), jnp.float32)
+        ref[PAD + rows :] = jnp.zeros((PAD, margin), jnp.float32)
+    for block in range(blocks):
+        first[block][PAD : PAD + rows] = frame_ref[:, block * margin : (block + 1) * margin]
+
+    source, target = first, last
+    for step in range(LS_STEPS):
+        final = step == LS_STEPS - 1
+        for at in range(PAD if final else 0, rows - PAD if final else rows, PAD):
+            here = [ref[PAD + at : 2 * PAD + at] for ref in source]
+            back = [pltpu.roll(part, 1, 1) for part in here]
+            ahead = [pltpu.roll(part, margin - 1, 1) for part in here]
+            for block in range(blocks - 1 if final else blocks):
+                up = source[block][PAD + at - 1 : 2 * PAD + at - 1]
+                down = source[block][PAD + at + 1 : 2 * PAD + at + 1]
+                left = jnp.where(lane == 0, back[block - 1], back[block])
+                right = jnp.where(lane == margin - 1, ahead[(block + 1) % blocks], ahead[block])
+                slope_y = down - up
+                slope_x = right - left
+                square = GRAD_FLOOR + slope_y * slope_y + slope_x * slope_x
+                level = (
+                    (1.0 - 4.0 * SMOOTHING) * here[block]
+                    + SMOOTHING * ((up + down) + (left + right))
+                    - speed_ref[at : at + PAD, block * margin : (block + 1) * margin]
+                    * (square * lax.rsqrt(square))
+                )
+                if final:
+                    out_ref[at - PAD : at, block * margin : (block + 1) * margin] = 2.0 * level
+                    continue
+                if at == 0:
+                    level = jnp.where(keep_above, level, 0.0)
+                if at == rows - PAD:
+                    level = jnp.where(keep_below, level, 0.0)
+                if block == blocks - 1:
+                    level = jnp.where(keep_cols, level, 0.0)
+                target[block][PAD + at : 2 * PAD + at] = level
+        source, target = target, source
+
+
+def load_kernel(*refs):
+    count = len(refs) // 2
+    sems = refs[-1]
+    copies = [
+        pltpu.make_async_copy(refs[i], refs[count + i], sems.at[i]) for i in range(count)
+    ]
+    for copy in copies:
+        copy.start()
+    for copy in copies:
+        copy.wait()
+
+
+def load(*arrays):
+    return pl.pallas_call(
+        load_kernel,
+        out_shape=[jax.ShapeDtypeStruct(item.shape, item.dtype) for item in arrays],
+        in_specs=[pl.BlockSpec(memory_space=pltpu.HBM)] * len(arrays),
+        out_specs=[pl.BlockSpec(memory_space=pltpu.VMEM)] * len(arrays),
+        scratch_shapes=[pltpu.SemaphoreType.DMA((len(arrays),))],
+        compiler_params=pltpu.CompilerParams(vmem_limit_bytes=24 << 20),
+        cost_estimate=pl.CostEstimate(flops=0, bytes_accessed=8 << 20, transcendentals=0),
+        name="load",
+    )(*[pltpu.with_memory_space_constraint(item, pltpu.HBM) for item in arrays])
+
+
+def call(kernel, out_shape, *args, scratch=(), smem=0):
     vmem = pl.BlockSpec(memory_space=pltpu.VMEM)
     in_specs = [pl.BlockSpec(memory_space=pltpu.SMEM)] * smem + [vmem] * (len(args) - smem)
     return pl.pallas_call(
@@ -309,7 +364,6 @@
         out_specs=[vmem] * len(out_shape),
         scratch_shapes=list(scratch),
         compiler_params=pltpu.CompilerParams(vmem_limit_bytes=24 << 20),
-        name=name,
     )(*args)
 
 
@@ -317,8 +371,8 @@
     count = lax.axis_size(axis)
     pairs = []
     for index in range(count - 1):
-        pairs.append((index * 2, (index + 1) * 2))
-        pairs.append(((index + 1) * 2 + 1, index * 2 + 1))
+        pairs.append((index * 2 + 1, (index + 1) * 2))
+        pairs.append(((index + 1) * 2, index * 2 + 1))
     return lax.ppermute(values, (axis, "corner"), pairs)
 
 
@@ -326,7 +380,7 @@
     return lax.ppermute(values, "corner", [(0, 1), (1, 0)])
 
 
-def body(level_init, target, kernels, corner_doses):
+def step(level_init, target, kernels, corner_doses):
     tile = level_init.shape[0]
     margin = HALO
     freqs = KF
@@ -336,22 +390,27 @@
     bf16, f32 = jnp.bfloat16, jnp.float32
     extent = (lax.axis_size("ty"), lax.axis_size("tx"))
 
-    edge = lax.dynamic_slice_in_dim(level_init, (1 - core) * (tile - margin), margin, axis=0)
-    rows_mine = along("ty", (edge.astype(f32) * 0.125).astype(bf16))
+    edge = lax.dynamic_slice_in_dim(level_init, core * (tile - margin), margin, axis=0)
+    edge = (edge.astype(f32) * 0.125).astype(bf16)
+    rows_mine = along("ty", edge)
     rows_other = across(rows_mine)
+    names = sorted(tables)
+    level_init, target, kernels, *loaded = load(
+        level_init, target, kernels[0], *(tables[name] for name in names)
+    )
+    tables = dict(zip(names, loaded))
     strip_rows = (tile // margin + 1) * RIM
     lift, send = call(
         lift_kernel,
         [((2 * freqs, tile), bf16), ((2 * freqs + strip_rows, margin), bf16)],
         level_init, rows_mine, rows_other, tables["fwd"],
-        name="lift",
     )
     cols_mine = along("tx", send)
     cols_other = across(cols_mine)
     resist, grad = call(
         corner_kernel,
         [((tile, tile), f32), ((2 * freqs, freqs), f32)],
-        corner_doses, lift, cols_mine, cols_other, kernels[0], target,
+        corner_doses, lift, cols_mine, cols_other, kernels, target,
         tables["fwd_t"], tables["inv"], tables["inv_t"],
         smem=1,
         scratch=[
@@ -360,7 +419,6 @@
             pltpu.VMEM((count, tile, 2 * tile), f32),
             pltpu.VMEM((2 * tile, count * freqs), bf16),
         ],
-        name="corner",
     )
     grad = (grad + across(grad)).astype(bf16)
     grad_mine = along("tx", grad)
@@ -369,7 +427,6 @@
         lift_grad_kernel,
         [((2 * freqs, tile + margin), bf16), ((margin + RIM, tile + margin), bf16)],
         grad, grad_mine, grad_other, tables["fwd"], tables["rim_cols"], tables["send_rows"],
-        name="lift_grad",
     )
     piece_mine = along("ty", piece)
     piece_other = across(piece_mine)
@@ -378,13 +435,13 @@
         frame_kernel,
         [(framed, f32)] * 3,
         grad_lift, tables["own_rows"], level_init, rows_mine, rows_other, cols_mine, cols_other,
-        name="frame",
     )
     (level,) = call(
         functools.partial(advance_kernel, extent),
         [((tile, tile), f32)],
         own, piece_mine, piece_other, frame, slope,
-        name="advance",
+        scratch=[pltpu.VMEM(framed, f32)]
+        + [pltpu.VMEM((framed[0] + 2 * PAD, margin), f32)] * (2 * framed[1] // margin),
     )
     return (resist[None], level)
 
@@ -392,4 +449,4 @@
 def solution(mesh):
     in_specs = (P("ty", "tx"), P("ty", "tx"), P("corner", None, None, None, None), P("corner"))
     out_specs = (P("corner", "ty", "tx"), P("ty", "tx"))
-    return jax.shard_map(body, mesh=mesh, in_specs=in_specs, out_specs=out_specs, check_vma=False)
+    return jax.shard_map(step, mesh=mesh, in_specs=in_specs, out_specs=out_specs, check_vma=False)

time: 46.9 us -> 39.5 us (0.84)
  the two profiles are of different devices: /device:TPU:21 before, /device:TPU:19 now
where the time goes in v2:
time: 39.5 us; the launch traced here: 39.2 us
  waiting for transfers between devices  15.2 us (38%)
  starting transfers between devices  14.9 us (38%)
  Pallas kernels  6.76 us (17%)
  between operations  1.37 us (3%)
  other arithmetic  0.94 us (2%)
    ppermute x4, starting transfers between devices, along(): return lax.ppermute(values, (axis, 'corner'), pairs)  13.7 us
    ppermute x4, waiting for transfers between devices, along(): return lax.ppermute(values, (axis, 'corner'), pairs)  12.1 us
    pallas_call x5, Pallas kernels, call(): pl.pallas_call(kernel, out_shape=[jax.ShapeDtypeStruct(*item) for item in...  4.99 us
    ppermute x5, waiting for transfers between devices, across(): return lax.ppermute(values, 'corner', [(0, 1), (1, 0)])  3.15 us
    pallas_call x1, Pallas kernels, load(): pl.pallas_call(load_kernel, out_shape=[jax.ShapeDtypeStruct(item.shape, i...  1.77 us
    ppermute x5, starting transfers between devices, across(): return lax.ppermute(values, 'corner', [(0, 1), (1, 0)])  1.18 us
    convert_element_type x1, other arithmetic, step(): edge = (edge.astype(f32) * 0.125).astype(bf16)  0.92 us
  transfers between devices with their start and end apart: 9, of which 8 were waited for; matrix products, arithmetic and copies ran while one was open for 0% of the time, Pallas kernels for 5%

profile of v2, /device:TPU:19, one launch (start us, length us, event | category | flops | bytes accessed | tf_op | source)
XLA Modules:
  0.0 39.2 jit_solution(6784894069551844867)
XLA Ops:
  0.6 0.9 %multiply_convert_fusion = bf16[128,256]{1,0:T(8,128)(2,1)S(1)} fusion(s32[256,256]{1,0:T(8,128)} %refs_0_.1, s32[]{:T(128)S(6)} %select_n.3), kind=kLoop, calls=%fused_computation.1 | loop fusion | flops 98304 | bytes 196612 | tf_op jit(solution)/shard_map/convert_element_type | solution.py:394
  1.6 3.7 %collective-permute-start = (bf16[128,256]{1,0:T(8,128)(2,1)S(1)}, bf16[128,256]{1,0:T(8,128)(2,1)S(1)}, u32[]{:S(2)}, u32[]{:S(2)}) collective-permute-start(bf16[128,256]{1,0:T(8,128)(2,1)S(1)} %multiply_convert_fusion), channel_id=1, source_target_pairs={{1,8},{8,1},{9,16},{16,9},{17,24},{24,17},{3,10},{10,3},{11,18},{1... | collective-permute-start | bytes 196616 | tf_op jit(solution)/shard_map/ppermute | solution.py:376
  5.2 3.5 %collective-permute-done.mine_ref.above_ref = bf16[128,256]{1,0:T(8,128)(2,1)S(1)} collective-permute-done((bf16[128,256]{1,0:T(8,128)(2,1)S(1)}, bf16[128,256]{1,0:T(8,128)(2,1)S(1)}, u32[]{:S(2)}, u32[]{:S(2)}) %collective-permute-start) | collective-permute-done | bytes 65568 | tf_op jit(solution)/shard_map/ppermute | solution.py:376
  8.7 0.0 collective-permute-start.1
  8.7 1.8 %load.1 = (s32[256,256]{1,0:T(8,128)S(1)}, s32[256,256]{1,0:T(8,128)S(1)}, f32[5,2,128,128]{3,2,1,0:T(8,128)S(1)}, bf16[256,512]{1,0:T(8,128)(2,1)S(1)}, bf16[51...) custom-call(s32[256,256]{1,0:T(8,128)} %refs_0_.1, ...), custom_call_target="tpu_custom_call" | custom-call | bytes 8388608 | tf_op jit(solution)/shard_map/load/pallas_call | solution.py:345
  10.5 0.0 collective-permute-done.1.other_ref.below_ref
  10.5 0.3 shard_map.122
  10.8 3.6 %collective-permute-start.2 = (bf16[304,128]{1,0:T(8,128)(2,1)S(1)}, bf16[304,128]{1,0:T(8,128)(2,1)S(1)}, u32[]{:S(2)}, u32[]{:S(2)}) collective-permute-start(bf16[304,128]{1,0:T(8,128)(2,1)S(1)} %get-tuple-element.24), channel_id=1, source_target_pairs={{1,2},{2,1},{3,4},{4,3},{5,6},{6,5},{9,10},{10,9},{11,12},{12,11},... | collective-permute-start | bytes 233480 | tf_op jit(solution)/shard_map/ppermute | solution.py:376
  14.4 2.2 %collective-permute-done.2.mine_ref.left_ref = bf16[304,128]{1,0:T(8,128)(2,1)S(1)} collective-permute-done((bf16[304,128]{1,0:T(8,128)(2,1)S(1)}, bf16[304,128]{1,0:T(8,128)(2,1)S(1)}, u32[]{:S(2)}, u32[]{:S(2)}) %collective-permute-start.2) | collective-permute-done | bytes 77856 | tf_op jit(solution)/shard_map/ppermute | solution.py:376
  16.6 0.4 %collective-permute-start.3 = (bf16[304,128]{1,0:T(8,128)(2,1)S(1)}, bf16[304,128]{1,0:T(8,128)(2,1)S(1)}, u32[]{:S(2)}, u32[]{:S(2)}) collective-permute-start(bf16[304,128]{1,0:T(8,128)(2,1)S(1)} %collective-permute-done.2.mine_ref.left_ref), channel_id=1, source_target_pairs={{0,1},{1,0},{2,3},{3,2},{4,5},{5,4},{6,7},{7,6},{8,9},{9,8},{10,11... | collective-permute-start | bytes 233480 | tf_op jit(solution)/shard_map/ppermute | solution.py:380
  17.7 0.3 collective-permute-done.3.other_ref.right_ref
  17.9 2.3 %shard_map.123 = (f32[256,256]{1,0:T(8,128)}, f32[256,128]{1,0:T(8,128)S(1)}) custom-call(f32[1]{0:T(128)S(6)} %copy.13.dose_ref, bf16[256,256]{1,0:T(8,128)(2,1)S(1)} %get-tuple-element.23.lift_ref, bf16[304,128]{1,0:T(8,128)(2,1)S(1)} %collective-permute-done.2.mine_ref.left_ref, bf16[304,128]{1,0:T(8,128)(2,1)S(1)} %collective-permute-done.3.other_ref.right_ref, ...), custom_call_target="tpu_custom_call" | custom-call | tf_op jit(solution)/shard_map/pallas_call | solution.py:360
  20.2 0.4 %collective-permute-start.4 = (f32[256,128]{1,0:T(8,128)S(1)}, f32[256,128]{1,0:T(8,128)S(1)}, u32[]{:S(2)}, u32[]{:S(2)}) collective-permute-start(f32[256,128]{1,0:T(8,128)S(1)} %get-tuple-element.31), channel_id=1, source_target_pairs={{0,1},{1,0},{2,3},{3,2},{4,5},{5,4},{6,7},{7,6},{8,9},{9,8},{10,11... | collective-permute-start | bytes 393224 | tf_op jit(solution)/shard_map/ppermute | solution.py:380
  20.7 1.0 %collective-permute-done.4 = f32[256,128]{1,0:T(8,128)S(1)} collective-permute-done((f32[256,128]{1,0:T(8,128)S(1)}, f32[256,128]{1,0:T(8,128)S(1)}, u32[]{:S(2)}, u32[]{:S(2)}) %collective-permute-start.4) | collective-permute-done | bytes 131104 | tf_op jit(solution)/shard_map/ppermute | solution.py:380
  21.7 3.4 %collective-permute-start.5 = (bf16[256,128]{1,0:T(8,128)(2,1)S(1)}, bf16[256,128]{1,0:T(8,128)(2,1)S(1)}, u32[]{:S(2)}, u32[]{:S(2)}) collective-permute-start(bf16[256,128]{1,0:T(8,128)(2,1)S(1)} %add_convert_fusion.grad_ref), channel_id=1, source_target_pairs={{1,2},{2,1},{3,4},{4,3},{5,6},{6,5},{9,10},{10,9},{11,12},{12,11},... | collective-permute-start | bytes 196616 | tf_op jit(solution)/shard_map/ppermute | solution.py:376
  25.1 2.1 %collective-permute-done.5.mine_ref = bf16[256,128]{1,0:T(8,128)(2,1)S(1)} collective-permute-done((bf16[256,128]{1,0:T(8,128)(2,1)S(1)}, bf16[256,128]{1,0:T(8,128)(2,1)S(1)}, u32[]{:S(2)}, u32[]{:S(2)}) %collective-permute-start.5) | collective-permute-done | bytes 65568 | tf_op jit(solution)/shard_map/ppermute | solution.py:376
  27.3 0.4 collective-permute-start.6
  27.6 0.9 %collective-permute-done.6.other_ref = bf16[256,128]{1,0:T(8,128)(2,1)S(1)} collective-permute-done((bf16[256,128]{1,0:T(8,128)(2,1)S(1)}, bf16[256,128]{1,0:T(8,128)(2,1)S(1)}, u32[]{:S(2)}, u32[]{:S(2)}) %collective-permute-start.6) | collective-permute-done | bytes 65568 | tf_op jit(solution)/shard_map/ppermute | solution.py:380
  28.5 0.6 %shard_map.124 = (bf16[256,384]{1,0:T(8,128)(2,1)S(1)}, bf16[144,384]{1,0:T(8,128)(2,1)S(1)}) custom-call(bf16[256,128]{1,0:T(8,128)(2,1)S(1)} %add_convert_fusion.grad_ref, bf16[256,128]{1,0:T(8,128)(2,1)S(1)} %collective-permute-done.5.mine_ref, bf16[256,128]{1,0:T(8,128)(2,1)S(1)} %collective-permute-done.6.other_ref, ...), custom_call_target="tpu_custom_call" | custom-call | tf_op jit(solution)/shard_map/pallas_call | solution.py:360
  29.1 3.0 %collective-permute-start.7 = (bf16[144,384]{1,0:T(8,128)(2,1)S(1)}, bf16[144,384]{1,0:T(8,128)(2,1)S(1)}, u32[]{:S(2)}, u32[]{:S(2)}) collective-permute-start(bf16[144,384]{1,0:T(8,128)(2,1)S(1)} %get-tuple-element.37), channel_id=1, source_target_pairs={{1,8},{8,1},{9,16},{16,9},{17,24},{24,17},{3,10},{10,3},{11,18},{1... | collective-permute-start | bytes 331784 | tf_op jit(solution)/shard_map/ppermute | solution.py:376
  32.1 4.3 %collective-permute-done.7.mine_ref = bf16[144,384]{1,0:T(8,128)(2,1)S(1)} collective-permute-done((bf16[144,384]{1,0:T(8,128)(2,1)S(1)}, bf16[144,384]{1,0:T(8,128)(2,1)S(1)}, u32[]{:S(2)}, u32[]{:S(2)}) %collective-permute-start.7) | collective-permute-done | bytes 110624 | tf_op jit(solution)/shard_map/ppermute | solution.py:376
  36.4 0.0 collective-permute-start.8
  36.4 0.3 shard_map.125
  36.7 1.0 %collective-permute-done.8.other_ref = bf16[144,384]{1,0:T(8,128)(2,1)S(1)} collective-permute-done((bf16[144,384]{1,0:T(8,128)(2,1)S(1)}, bf16[144,384]{1,0:T(8,128)(2,1)S(1)}, u32[]{:S(2)}, u32[]{:S(2)}) %collective-permute-start.8) | collective-permute-done | bytes 110624 | tf_op jit(solution)/shard_map/ppermute | solution.py:380
  37.7 1.5 %shard_map.126 = f32[256,256]{1,0:T(8,128)} custom-call(f32[272,384]{1,0:T(8,128)S(1)} %get-tuple-element.36.grad_ref, bf16[144,384]{1,0:T(8,128)(2,1)S(1)} %collective-permute-done.7.mine_ref, bf16[144,384]{1,0:T(8,128)(2,1)S(1)} %collective-permute-done.8.other_ref, f32[272,384]{1,0:T(8,128)S(1)} %get-tuple-element.38.frame_ref, ...), custom_call_target="tpu_custom_call" | custom-call | tf_op jit(solution)/shard_map/pallas_call | solution.py:360
  (1 shorter events, 0.0 us)
Async XLA Ops:
  1.6 7.1 %collective-permute-start = (bf16[128,256]{1,0:T(8,128)(2,1)S(1)}, bf16[128,256]{1,0:T(8,128)(2,1)S(1)}, u32[]{:S(2)}, u32[]{:S(2)}) collective-permute-start(bf16[128,256]{1,0:T(8,128)(2,1)S(1)} %multiply_convert_fusion), channel_id=1, source_target_pairs={{1,8},{8,1},{9,16},{16,9},{17,24},{24,17},{3,10},{10,3},{11,18},{1... | collective-permute-start | bytes 196616 | tf_op jit(solution)/shard_map/ppermute | solution.py:376
  8.7 1.8 %collective-permute-start.1 = (bf16[128,256]{1,0:T(8,128)(2,1)S(1)}, bf16[128,256]{1,0:T(8,128)(2,1)S(1)}, u32[]{:S(2)}, u32[]{:S(2)}) collective-permute-start(bf16[128,256]{1,0:T(8,128)(2,1)S(1)} %collective-permute-done.mine_ref.above_ref), channel_id=1, source_target_pairs={{0,1},{1,0},{2,3},{3,2},{4,5},{5,4},{6,7},{7,6},{8,9},{9,8},{10,11... | collective-permute-start | bytes 196616 | tf_op jit(solution)/shard_map/ppermute | solution.py:380
  10.8 5.8 %collective-permute-start.2 = (bf16[304,128]{1,0:T(8,128)(2,1)S(1)}, bf16[304,128]{1,0:T(8,128)(2,1)S(1)}, u32[]{:S(2)}, u32[]{:S(2)}) collective-permute-start(bf16[304,128]{1,0:T(8,128)(2,1)S(1)} %get-tuple-element.24), channel_id=1, source_target_pairs={{1,2},{2,1},{3,4},{4,3},{5,6},{6,5},{9,10},{10,9},{11,12},{12,11},... | collective-permute-start | bytes 233480 | tf_op jit(solution)/shard_map/ppermute | solution.py:376
  16.6 1.3 %collective-permute-start.3 = (bf16[304,128]{1,0:T(8,128)(2,1)S(1)}, bf16[304,128]{1,0:T(8,128)(2,1)S(1)}, u32[]{:S(2)}, u32[]{:S(2)}) collective-permute-start(bf16[304,128]{1,0:T(8,128)(2,1)S(1)} %collective-permute-done.2.mine_ref.left_ref), channel_id=1, source_target_pairs={{0,1},{1,0},{2,3},{3,2},{4,5},{5,4},{6,7},{7,6},{8,9},{9,8},{10,11... | collective-permute-start | bytes 233480 | tf_op jit(solution)/shard_map/ppermute | solution.py:380
  20.2 1.4 %collective-permute-start.4 = (f32[256,128]{1,0:T(8,128)S(1)}, f32[256,128]{1,0:T(8,128)S(1)}, u32[]{:S(2)}, u32[]{:S(2)}) collective-permute-start(f32[256,128]{1,0:T(8,128)S(1)} %get-tuple-element.31), channel_id=1, source_target_pairs={{0,1},{1,0},{2,3},{3,2},{4,5},{5,4},{6,7},{7,6},{8,9},{9,8},{10,11... | collective-permute-start | bytes 393224 | tf_op jit(solution)/shard_map/ppermute | solution.py:380
  21.7 5.6 %collective-permute-start.5 = (bf16[256,128]{1,0:T(8,128)(2,1)S(1)}, bf16[256,128]{1,0:T(8,128)(2,1)S(1)}, u32[]{:S(2)}, u32[]{:S(2)}) collective-permute-start(bf16[256,128]{1,0:T(8,128)(2,1)S(1)} %add_convert_fusion.grad_ref), channel_id=1, source_target_pairs={{1,2},{2,1},{3,4},{4,3},{5,6},{6,5},{9,10},{10,9},{11,12},{12,11},... | collective-permute-start | bytes 196616 | tf_op jit(solution)/shard_map/ppermute | solution.py:376
  27.3 1.3 %collective-permute-start.6 = (bf16[256,128]{1,0:T(8,128)(2,1)S(1)}, bf16[256,128]{1,0:T(8,128)(2,1)S(1)}, u32[]{:S(2)}, u32[]{:S(2)}) collective-permute-start(bf16[256,128]{1,0:T(8,128)(2,1)S(1)} %collective-permute-done.5.mine_ref), channel_id=1, source_target_pairs={{0,1},{1,0},{2,3},{3,2},{4,5},{5,4},{6,7},{7,6},{8,9},{9,8},{10,11... | collective-permute-start | bytes 196616 | tf_op jit(solution)/shard_map/ppermute | solution.py:380
  29.1 7.3 %collective-permute-start.7 = (bf16[144,384]{1,0:T(8,128)(2,1)S(1)}, bf16[144,384]{1,0:T(8,128)(2,1)S(1)}, u32[]{:S(2)}, u32[]{:S(2)}) collective-permute-start(bf16[144,384]{1,0:T(8,128)(2,1)S(1)} %get-tuple-element.37), channel_id=1, source_target_pairs={{1,8},{8,1},{9,16},{16,9},{17,24},{24,17},{3,10},{10,3},{11,18},{1... | collective-permute-start | bytes 331784 | tf_op jit(solution)/shard_map/ppermute | solution.py:376
  36.4 1.3 %collective-permute-start.8 = (bf16[144,384]{1,0:T(8,128)(2,1)S(1)}, bf16[144,384]{1,0:T(8,128)(2,1)S(1)}, u32[]{:S(2)}, u32[]{:S(2)}) collective-permute-start(bf16[144,384]{1,0:T(8,128)(2,1)S(1)} %collective-permute-done.7.mine_ref), channel_id=1, source_target_pairs={{0,1},{1,0},{2,3},{3,2},{4,5},{5,4},{6,7},{7,6},{8,9},{9,8},{10,11... | collective-permute-start | bytes 331784 | tf_op jit(solution)/shard_map/ppermute | solution.py:380

commit v3 on v2

--- a/solution.py
+++ b/solution.py
@@ -80,15 +80,14 @@
     return jnp.where(core == 0, first, second)
 
 
-def lift_kernel(level_ref, mine_ref, other_ref, fwd_ref, lift_ref, send_ref):
+def lift_kernel(counts, level_ref, mine_ref, other_ref, fwd_ref, lift_ref, send_ref):
     core = lax.axis_index("corner")
     tile = level_ref.shape[0]
     margin = mine_ref.shape[0]
     level = level_ref[...].astype(jnp.float32) * 0.125
-    mine = mine_ref[...].astype(jnp.float32)
-    other = other_ref[...].astype(jnp.float32)
-    above = by_core(core, mine, other)
-    below = by_core(core, other, mine)
+    above, below = ordered("ty", counts, mine_ref[...], other_ref[...])
+    above = above.astype(jnp.float32)
+    below = below.astype(jnp.float32)
     squash = lambda values: jnp.tanh(0.25 * values).astype(jnp.bfloat16)
     lift = (
         dot(fwd_ref[:, :margin], squash(above))
@@ -120,6 +119,7 @@
 
 
 def corner_kernel(
+    counts,
     dose_ref,
     lift_ref,
     mine_ref,
@@ -136,18 +136,16 @@
     field_ref,
     back_ref,
 ):
-    core = lax.axis_index("corner")
     tile = target_ref.shape[0]
     rows = lift_ref.shape[0]
     freqs = rows // 2
     margin = mine_ref.shape[1]
     count = kernels_ref.shape[0]
-    mine = mine_ref[:rows, :]
-    other = other_ref[:rows, :]
+    left, right = ordered("tx", counts, mine_ref[:rows, :], other_ref[:rows, :])
     mixed = (
-        dot(by_core(core, mine, other), fwd_t_ref[:margin, :])
+        dot(left, fwd_t_ref[:margin, :])
         + dot(lift_ref[...], fwd_t_ref[margin : margin + tile, :])
-        + dot(by_core(core, other, mine), fwd_t_ref[margin + tile :, :])
+        + dot(right, fwd_t_ref[margin + tile :, :])
     )
     spec_re = mixed[:freqs, :freqs] - mixed[freqs:, freqs:]
     spec_im = mixed[:freqs, freqs:] + mixed[freqs:, :freqs]
@@ -193,9 +191,10 @@
 
 
 def lift_grad_kernel(
+    counts,
     grad_ref, mine_ref, other_ref, fwd_ref, rim_ref, send_rows_ref, lift_ref, send_ref
 ):
-    core = lax.axis_index("corner")
+    to_after = 1 - lax.rem(lax.axis_index("corner") + lax.axis_index("ty"), 2)
     freqs = grad_ref.shape[0] // 2
     margin = rim_ref.shape[2]
     tile = fwd_ref.shape[1] - 2 * margin
@@ -208,11 +207,10 @@
         lower = jnp.concatenate([low_im, -low_re], axis=1)
         return jnp.concatenate([upper, lower], axis=0)
 
-    mine = mine_ref[...]
-    other = other_ref[...]
-    before = both(by_core(core, mine, other))
+    before, after = ordered("tx", counts, mine_ref[...], other_ref[...])
+    before = both(before)
     here = both(grad_ref[...])
-    after = both(by_core(core, other, mine))
+    after = both(after)
     middle = dot(here, fwd_ref[:, margin : margin + tile])
     lift_ref[:, :margin] = (middle[:, :margin] + dot(before, fwd_ref[:, last:])).astype(
         jnp.bfloat16
@@ -223,31 +221,29 @@
     lift_ref[:, tile:] = (
         dot(before, rim_ref[0]) + dot(here, rim_ref[1]) + dot(after, rim_ref[2])
     ).astype(jnp.bfloat16)
-    send_ref[...] = dot(send_rows_ref[core], lift_ref[...]).astype(jnp.bfloat16)
+    send_ref[...] = dot(send_rows_ref[to_after], lift_ref[...]).astype(jnp.bfloat16)
 
 
 def frame_kernel(
-    lift_ref, own_rows_ref, level_ref, above_ref, below_ref, left_ref, right_ref,
+    counts,
+    lift_ref, own_rows_ref, level_ref, mine_ref, other_ref, cols_mine_ref, cols_other_ref,
     grad_ref, frame_ref, slope_ref,
 ):
-    core = lax.axis_index("corner")
     tile = level_ref.shape[0]
-    margin = above_ref.shape[0]
+    margin = mine_ref.shape[0]
     rows = lift_ref.shape[0]
     grad_ref[...] = dot(own_rows_ref[...], lift_ref[...])
-    mine = above_ref[...].astype(jnp.float32)
-    other = below_ref[...].astype(jnp.float32)
-    frame_ref[:PAD, :tile] = 0.5 * by_core(core, mine, other)[margin - PAD :]
+    above, below = ordered("ty", counts, mine_ref[...], other_ref[...])
+    frame_ref[:PAD, :tile] = 0.5 * above.astype(jnp.float32)[margin - PAD :]
     frame_ref[PAD : PAD + tile, :tile] = level_ref[...].astype(jnp.float32) * 0.0625
-    frame_ref[PAD + tile :, :tile] = 0.5 * by_core(core, other, mine)[:PAD]
+    frame_ref[PAD + tile :, :tile] = 0.5 * below.astype(jnp.float32)[:PAD]
     at = lax.broadcasted_iota(jnp.int32, (RIM, margin), 0)
     lane = lax.broadcasted_iota(jnp.int32, (RIM, margin), 1)
     place_left = ((lane == margin - LS_STEPS + at) & (at < LS_STEPS)).astype(jnp.bfloat16)
     place_right = ((lane == at) & (at < LS_STEPS)).astype(jnp.bfloat16)
     for block in range(tile // margin + 1):
         part = slice(rows + block * RIM, rows + (block + 1) * RIM)
-        left = by_core(core, left_ref[part, :], right_ref[part, :])
-        right = by_core(core, right_ref[part, :], left_ref[part, :])
+        left, right = ordered("tx", counts, cols_mine_ref[part, :], cols_other_ref[part, :])
         placed = dot_general(left, place_left, 0, 0) + dot_general(right, place_right, 0, 0)
         placed = 0.5 * placed
         if block < tile // margin:
@@ -261,9 +257,8 @@
 
 
 def advance_kernel(
-    extent, grad_ref, mine_ref, other_ref, frame_ref, slope_ref, out_ref, speed_ref, *level_refs
+    counts, grad_ref, mine_ref, other_ref, frame_ref, slope_ref, out_ref, speed_ref, *level_refs
 ):
-    core = lax.axis_index("corner")
     tile = out_ref.shape[0]
     rows, cols = frame_ref.shape
     margin = cols - tile
@@ -274,13 +269,14 @@
     at_ty, at_tx = lax.axis_index("ty"), lax.axis_index("tx")
     all_lanes = lane >= 0
     keep_above = all_lanes & (at_ty > 0)
-    keep_below = all_lanes & (at_ty < extent[0] - 1)
+    keep_below = all_lanes & (at_ty < counts["ty"] - 1)
     keep_cols = ((lane >= margin // 2) & (at_tx > 0)) | (
-        (lane < margin // 2) & (at_tx < extent[1] - 1)
-    )
-
-    before = by_core(core, mine_ref[...].astype(jnp.float32), other_ref[...].astype(jnp.float32))
-    after = by_core(core, other_ref[...].astype(jnp.float32), mine_ref[...].astype(jnp.float32))
+        (lane < margin // 2) & (at_tx < counts["tx"] - 1)
+    )
+
+    before, after = ordered("ty", counts, mine_ref[...], other_ref[...])
+    before = before.astype(jnp.float32)
+    after = after.astype(jnp.float32)
     rim = before[margin:] + after[margin:] + grad_ref[tile:]
     speed_ref[:PAD] = rim[PAD:] * slope_ref[:PAD]
     speed_ref[PAD + tile :] = rim[:PAD] * slope_ref[PAD + tile :]
@@ -368,12 +364,36 @@
 
 
 def along(axis, values):
-    count = lax.axis_size(axis)
+    rows, cols = lax.axis_size("ty"), lax.axis_size("tx")
+    count, others = (rows, cols) if axis == "ty" else (cols, rows)
+
+    def device(place, other, core):
+        row, col = (place, other) if axis == "ty" else (other, place)
+        return (row * cols + col) * 2 + core
+
     pairs = []
-    for index in range(count - 1):
-        pairs.append((index * 2 + 1, (index + 1) * 2))
-        pairs.append(((index + 1) * 2, index * 2 + 1))
-    return lax.ppermute(values, (axis, "corner"), pairs)
+    for other in range(others):
+        free = {device(place, other, core) for place in (0, count - 1) for core in range(2)}
+        for place in range(count - 1):
+            cores = (place % 2, place % 2) if axis == "ty" else (1, 0)
+            one, two = device(place, other, cores[0]), device(place + 1, other, cores[1])
+            pairs += [(one, two), (two, one)]
+            free -= {one, two}
+        if other % 2 == 0 and other + 1 < others:
+            step = device(0, 1, 0) - device(0, 0, 0)
+            for one in sorted(free):
+                pairs += [(one, one + step), (one + step, one)]
+    return lax.ppermute(values, ("ty", "tx", "corner"), pairs)
+
+
+def ordered(axis, counts, mine, other):
+    index, core = lax.axis_index(axis), lax.axis_index("corner")
+    count = counts[axis]
+    from_before = (core != lax.rem(index, 2)) if axis == "ty" else core == 0
+    before = jnp.where(from_before, mine, other)
+    after = jnp.where(from_before, other, mine)
+    zero = jnp.zeros_like(mine)
+    return jnp.where(index > 0, before, zero), jnp.where(index < count - 1, after, zero)
 
 
 def across(values):
@@ -386,11 +406,11 @@
     freqs = KF
     count = kernels.shape[1]
     tables = make_tables(tile, margin, freqs)
-    core = lax.axis_index("corner")
+    to_after = 1 - lax.rem(lax.axis_index("corner") + lax.axis_index("ty"), 2)
     bf16, f32 = jnp.bfloat16, jnp.float32
-    extent = (lax.axis_size("ty"), lax.axis_size("tx"))
-
-    edge = lax.dynamic_slice_in_dim(level_init, core * (tile - margin), margin, axis=0)
+    counts = {"ty": lax.axis_size("ty"), "tx": lax.axis_size("tx")}
+
+    edge = lax.dynamic_slice_in_dim(level_init, to_after * (tile - margin), margin, axis=0)
     edge = (edge.astype(f32) * 0.125).astype(bf16)
     rows_mine = along("ty", edge)
     rows_other = across(rows_mine)
@@ -401,14 +421,14 @@
     tables = dict(zip(names, loaded))
     strip_rows = (tile // margin + 1) * RIM
     lift, send = call(
-        lift_kernel,
+        functools.partial(lift_kernel, counts),
         [((2 * freqs, tile), bf16), ((2 * freqs + strip_rows, margin), bf16)],
         level_init, rows_mine, rows_other, tables["fwd"],
     )
     cols_mine = along("tx", send)
     cols_other = across(cols_mine)
     resist, grad = call(
-        corner_kernel,
+        functools.partial(corner_kernel, counts),
         [((tile, tile), f32), ((2 * freqs, freqs), f32)],
         corner_doses, lift, cols_mine, cols_other, kernels, target,
         tables["fwd_t"], tables["inv"], tables["inv_t"],
@@ -424,7 +444,7 @@
     grad_mine = along("tx", grad)
     grad_other = across(grad_mine)
     grad_lift, piece = call(
-        lift_grad_kernel,
+        functools.partial(lift_grad_kernel, counts),
         [((2 * freqs, tile + margin), bf16), ((margin + RIM, tile + margin), bf16)],
         grad, grad_mine, grad_other, tables["fwd"], tables["rim_cols"], tables["send_rows"],
     )
@@ -432,12 +452,12 @@
     piece_other = across(piece_mine)
     framed = (tile + RIM, tile + margin)
     own, frame, slope = call(
-        frame_kernel,
+        functools.partial(frame_kernel, counts),
         [(framed, f32)] * 3,
         grad_lift, tables["own_rows"], level_init, rows_mine, rows_other, cols_mine, cols_other,
     )
     (level,) = call(
-        functools.partial(advance_kernel, extent),
+        functools.partial(advance_kernel, counts),
         [((tile, tile), f32)],
         own, piece_mine, piece_other, frame, slope,
         scratch=[pltpu.VMEM(framed, f32)]

time: 39.5 us -> 33.6 us (0.85)
  the two profiles are of different devices: /device:TPU:19 before, /device:TPU:0 now
where the time goes in v3:
time: 33.6 us; the launch traced here: 33.4 us
  waiting for transfers between devices  15.8 us (47%)
  starting transfers between devices  8.57 us (26%)
  Pallas kernels  6.76 us (20%)
  between operations  1.35 us (4%)
  other arithmetic  0.94 us (3%)
    ppermute x4, waiting for transfers between devices, along(): return lax.ppermute(values, ('ty', 'tx', 'corner'), pairs)  11.9 us
    ppermute x4, starting transfers between devices, along(): return lax.ppermute(values, ('ty', 'tx', 'corner'), pairs)  8.23 us
    pallas_call x5, Pallas kernels, call(): pl.pallas_call(kernel, out_shape=[jax.ShapeDtypeStruct(*item) for item in...  4.99 us
    ppermute x5, waiting for transfers between devices, across(): return lax.ppermute(values, 'corner', [(0, 1), (1, 0)])  3.95 us
    pallas_call x1, Pallas kernels, load(): pl.pallas_call(load_kernel, out_shape=[jax.ShapeDtypeStruct(item.shape, i...  1.77 us
    convert_element_type x1, other arithmetic, step(): edge = (edge.astype(f32) * 0.125).astype(bf16)  0.92 us
  transfers between devices with their start and end apart: 9, of which 8 were waited for; matrix products, arithmetic and copies ran while one was open for 0% of the time, Pallas kernels for 6%

profile of v3, /device:TPU:0, one launch (start us, length us, event | category | flops | bytes accessed | tf_op | source)
XLA Modules:
  0.0 33.4 jit_solution(18374922635094435093)
XLA Ops:
  0.6 0.9 %multiply_convert_fusion = bf16[128,256]{1,0:T(8,128)(2,1)S(1)} fusion(s32[256,256]{1,0:T(8,128)} %refs_0_.1, s32[]{:T(128)S(6)} %select_n.3), kind=kLoop, calls=%fused_computation.1 | loop fusion | flops 98304 | bytes 196612 | tf_op jit(solution)/shard_map/convert_element_type | solution.py:414
  1.6 3.0 %collective-permute-start = (bf16[128,256]{1,0:T(8,128)(2,1)S(1)}, bf16[128,256]{1,0:T(8,128)(2,1)S(1)}, u32[]{:S(2)}, u32[]{:S(2)}) collective-permute-start(bf16[128,256]{1,0:T(8,128)(2,1)S(1)} %multiply_convert_fusion), channel_id=1, source_target_pairs={{0,8},{8,0},{9,17},{17,9},{16,24},{24,16},{1,3},{3,1},{25,27},{27,... | collective-permute-start | bytes 196616 | tf_op jit(solution)/shard_map/ppermute | solution.py:386
  4.6 2.6 %collective-permute-done.mine_ref = bf16[128,256]{1,0:T(8,128)(2,1)S(1)} collective-permute-done((bf16[128,256]{1,0:T(8,128)(2,1)S(1)}, bf16[128,256]{1,0:T(8,128)(2,1)S(1)}, u32[]{:S(2)}, u32[]{:S(2)}) %collective-permute-start) | collective-permute-done | bytes 65568 | tf_op jit(solution)/shard_map/ppermute | solution.py:386
  7.2 0.0 collective-permute-start.1
  7.2 1.8 %load.1 = (s32[256,256]{1,0:T(8,128)S(1)}, s32[256,256]{1,0:T(8,128)S(1)}, f32[5,2,128,128]{3,2,1,0:T(8,128)S(1)}, bf16[256,512]{1,0:T(8,128)(2,1)S(1)}, bf16[51...) custom-call(s32[256,256]{1,0:T(8,128)} %refs_0_.1, ...), custom_call_target="tpu_custom_call" | custom-call | bytes 8388608 | tf_op jit(solution)/shard_map/load/pallas_call | solution.py:341
  9.0 0.0 collective-permute-done.1.other_ref
  9.0 0.3 shard_map.122
  9.3 1.7 %collective-permute-start.2 = (bf16[304,128]{1,0:T(8,128)(2,1)S(1)}, bf16[304,128]{1,0:T(8,128)(2,1)S(1)}, u32[]{:S(2)}, u32[]{:S(2)}) collective-permute-start(bf16[304,128]{1,0:T(8,128)(2,1)S(1)} %get-tuple-element.24), channel_id=1, source_target_pairs={{1,2},{2,1},{3,4},{4,3},{5,6},{6,5},{0,8},{8,0},{7,15},{15,7},{9,1... | collective-permute-start | bytes 233480 | tf_op jit(solution)/shard_map/ppermute | solution.py:386
  11.0 2.7 %collective-permute-done.2.mine_ref.cols_mine_ref = bf16[304,128]{1,0:T(8,128)(2,1)S(1)} collective-permute-done((bf16[304,128]{1,0:T(8,128)(2,1)S(1)}, bf16[304,128]{1,0:T(8,128)(2,1)S(1)}, u32[]{:S(2)}, u32[]{:S(2)}) %collective-permute-start.2) | collective-permute-done | bytes 77856 | tf_op jit(solution)/shard_map/ppermute | solution.py:386
  13.8 0.1 collective-permute-start.3
  14.5 0.5 %collective-permute-done.3.other_ref.cols_other_ref = bf16[304,128]{1,0:T(8,128)(2,1)S(1)} collective-permute-done((bf16[304,128]{1,0:T(8,128)(2,1)S(1)}, bf16[304,128]{1,0:T(8,128)(2,1)S(1)}, u32[]{:S(2)}, u32[]{:S(2)}) %collective-permute-start.3) | collective-permute-done | bytes 77856 | tf_op jit(solution)/shard_map/ppermute | solution.py:400
  15.0 2.3 %shard_map.123 = (f32[256,256]{1,0:T(8,128)}, f32[256,128]{1,0:T(8,128)S(1)}) custom-call(f32[1]{0:T(128)S(6)} %copy.13.dose_ref, bf16[256,256]{1,0:T(8,128)(2,1)S(1)} %get-tuple-element.23.lift_ref, bf16[304,128]{1,0:T(8,128)(2,1)S(1)} %collective-permute-done.2.mine_ref.cols_mine_ref, bf16[304,128]{1,0:T(8,128)(2,1)S(1)} %collective-permute-done.3.other_ref.cols_other_ref, ...), custom_call_target="tpu_custom_call" | custom-call | tf_op jit(solution)/shard_map/pallas_call | solution.py:356
  17.3 0.2 collective-permute-start.4
  17.5 1.2 %collective-permute-done.4 = f32[256,128]{1,0:T(8,128)S(1)} collective-permute-done((f32[256,128]{1,0:T(8,128)S(1)}, f32[256,128]{1,0:T(8,128)S(1)}, u32[]{:S(2)}, u32[]{:S(2)}) %collective-permute-start.4) | collective-permute-done | bytes 131104 | tf_op jit(solution)/shard_map/ppermute | solution.py:400
  18.7 1.7 %collective-permute-start.5 = (bf16[256,128]{1,0:T(8,128)(2,1)S(1)}, bf16[256,128]{1,0:T(8,128)(2,1)S(1)}, u32[]{:S(2)}, u32[]{:S(2)}) collective-permute-start(bf16[256,128]{1,0:T(8,128)(2,1)S(1)} %add_convert_fusion.grad_ref), channel_id=1, source_target_pairs={{1,2},{2,1},{3,4},{4,3},{5,6},{6,5},{0,8},{8,0},{7,15},{15,7},{9,1... | collective-permute-start | bytes 196616 | tf_op jit(solution)/shard_map/ppermute | solution.py:386
  20.5 2.6 %collective-permute-done.5.mine_ref = bf16[256,128]{1,0:T(8,128)(2,1)S(1)} collective-permute-done((bf16[256,128]{1,0:T(8,128)(2,1)S(1)}, bf16[256,128]{1,0:T(8,128)(2,1)S(1)}, u32[]{:S(2)}, u32[]{:S(2)}) %collective-permute-start.5) | collective-permute-done | bytes 65568 | tf_op jit(solution)/shard_map/ppermute | solution.py:386
  23.1 0.0 collective-permute-start.6
  23.1 1.3 %collective-permute-done.6.other_ref = bf16[256,128]{1,0:T(8,128)(2,1)S(1)} collective-permute-done((bf16[256,128]{1,0:T(8,128)(2,1)S(1)}, bf16[256,128]{1,0:T(8,128)(2,1)S(1)}, u32[]{:S(2)}, u32[]{:S(2)}) %collective-permute-start.6) | collective-permute-done | bytes 65568 | tf_op jit(solution)/shard_map/ppermute | solution.py:400
  24.3 0.6 %shard_map.124 = (bf16[256,384]{1,0:T(8,128)(2,1)S(1)}, bf16[144,384]{1,0:T(8,128)(2,1)S(1)}) custom-call(bf16[256,128]{1,0:T(8,128)(2,1)S(1)} %add_convert_fusion.grad_ref, bf16[256,128]{1,0:T(8,128)(2,1)S(1)} %collective-permute-done.5.mine_ref, bf16[256,128]{1,0:T(8,128)(2,1)S(1)} %collective-permute-done.6.other_ref, ...), custom_call_target="tpu_custom_call" | custom-call | tf_op jit(solution)/shard_map/pallas_call | solution.py:356
  24.9 1.7 %collective-permute-start.7 = (bf16[144,384]{1,0:T(8,128)(2,1)S(1)}, bf16[144,384]{1,0:T(8,128)(2,1)S(1)}, u32[]{:S(2)}, u32[]{:S(2)}) collective-permute-start(bf16[144,384]{1,0:T(8,128)(2,1)S(1)} %get-tuple-element.37), channel_id=1, source_target_pairs={{0,8},{8,0},{9,17},{17,9},{16,24},{24,16},{1,3},{3,1},{25,27},{27,... | collective-permute-start | bytes 331784 | tf_op jit(solution)/shard_map/ppermute | solution.py:386
  26.6 3.9 %collective-permute-done.7.mine_ref = bf16[144,384]{1,0:T(8,128)(2,1)S(1)} collective-permute-done((bf16[144,384]{1,0:T(8,128)(2,1)S(1)}, bf16[144,384]{1,0:T(8,128)(2,1)S(1)}, u32[]{:S(2)}, u32[]{:S(2)}) %collective-permute-start.7) | collective-permute-done | bytes 110624 | tf_op jit(solution)/shard_map/ppermute | solution.py:386
  30.6 0.0 collective-permute-start.8
  30.6 0.3 shard_map.125
  30.9 1.0 %collective-permute-done.8.other_ref = bf16[144,384]{1,0:T(8,128)(2,1)S(1)} collective-permute-done((bf16[144,384]{1,0:T(8,128)(2,1)S(1)}, bf16[144,384]{1,0:T(8,128)(2,1)S(1)}, u32[]{:S(2)}, u32[]{:S(2)}) %collective-permute-start.8) | collective-permute-done | bytes 110624 | tf_op jit(solution)/shard_map/ppermute | solution.py:400
  31.9 1.5 %shard_map.126 = f32[256,256]{1,0:T(8,128)} custom-call(f32[272,384]{1,0:T(8,128)S(1)} %get-tuple-element.36.grad_ref, bf16[144,384]{1,0:T(8,128)(2,1)S(1)} %collective-permute-done.7.mine_ref, bf16[144,384]{1,0:T(8,128)(2,1)S(1)} %collective-permute-done.8.other_ref, f32[272,384]{1,0:T(8,128)S(1)} %get-tuple-element.38.frame_ref, ...), custom_call_target="tpu_custom_call" | custom-call | tf_op jit(solution)/shard_map/pallas_call | solution.py:356
  (1 shorter events, 0.0 us)
Async XLA Ops:
  1.6 5.6 %collective-permute-start = (bf16[128,256]{1,0:T(8,128)(2,1)S(1)}, bf16[128,256]{1,0:T(8,128)(2,1)S(1)}, u32[]{:S(2)}, u32[]{:S(2)}) collective-permute-start(bf16[128,256]{1,0:T(8,128)(2,1)S(1)} %multiply_convert_fusion), channel_id=1, source_target_pairs={{0,8},{8,0},{9,17},{17,9},{16,24},{24,16},{1,3},{3,1},{25,27},{27,... | collective-permute-start | bytes 196616 | tf_op jit(solution)/shard_map/ppermute | solution.py:386
  7.2 1.8 %collective-permute-start.1 = (bf16[128,256]{1,0:T(8,128)(2,1)S(1)}, bf16[128,256]{1,0:T(8,128)(2,1)S(1)}, u32[]{:S(2)}, u32[]{:S(2)}) collective-permute-start(bf16[128,256]{1,0:T(8,128)(2,1)S(1)} %collective-permute-done.mine_ref), channel_id=1, source_target_pairs={{0,1},{1,0},{2,3},{3,2},{4,5},{5,4},{6,7},{7,6},{8,9},{9,8},{10,11... | collective-permute-start | bytes 196616 | tf_op jit(solution)/shard_map/ppermute | solution.py:400
  9.3 4.5 %collective-permute-start.2 = (bf16[304,128]{1,0:T(8,128)(2,1)S(1)}, bf16[304,128]{1,0:T(8,128)(2,1)S(1)}, u32[]{:S(2)}, u32[]{:S(2)}) collective-permute-start(bf16[304,128]{1,0:T(8,128)(2,1)S(1)} %get-tuple-element.24), channel_id=1, source_target_pairs={{1,2},{2,1},{3,4},{4,3},{5,6},{6,5},{0,8},{8,0},{7,15},{15,7},{9,1... | collective-permute-start | bytes 233480 | tf_op jit(solution)/shard_map/ppermute | solution.py:386
  13.8 1.3 %collective-permute-start.3 = (bf16[304,128]{1,0:T(8,128)(2,1)S(1)}, bf16[304,128]{1,0:T(8,128)(2,1)S(1)}, u32[]{:S(2)}, u32[]{:S(2)}) collective-permute-start(bf16[304,128]{1,0:T(8,128)(2,1)S(1)} %collective-permute-done.2.mine_ref.cols_mine_ref), channel_id=1, source_target_pairs={{0,1},{1,0},{2,3},{3,2},{4,5},{5,4},{6,7},{7,6},{8,9},{9,8},{10,11... | collective-permute-start | bytes 233480 | tf_op jit(solution)/shard_map/ppermute | solution.py:400
  17.3 1.4 %collective-permute-start.4 = (f32[256,128]{1,0:T(8,128)S(1)}, f32[256,128]{1,0:T(8,128)S(1)}, u32[]{:S(2)}, u32[]{:S(2)}) collective-permute-start(f32[256,128]{1,0:T(8,128)S(1)} %get-tuple-element.31), channel_id=1, source_target_pairs={{0,1},{1,0},{2,3},{3,2},{4,5},{5,4},{6,7},{7,6},{8,9},{9,8},{10,11... | collective-permute-start | bytes 393224 | tf_op jit(solution)/shard_map/ppermute | solution.py:400
  18.7 4.3 %collective-permute-start.5 = (bf16[256,128]{1,0:T(8,128)(2,1)S(1)}, bf16[256,128]{1,0:T(8,128)(2,1)S(1)}, u32[]{:S(2)}, u32[]{:S(2)}) collective-permute-start(bf16[256,128]{1,0:T(8,128)(2,1)S(1)} %add_convert_fusion.grad_ref), channel_id=1, source_target_pairs={{1,2},{2,1},{3,4},{4,3},{5,6},{6,5},{0,8},{8,0},{7,15},{15,7},{9,1... | collective-permute-start | bytes 196616 | tf_op jit(solution)/shard_map/ppermute | solution.py:386
  23.1 1.3 %collective-permute-start.6 = (bf16[256,128]{1,0:T(8,128)(2,1)S(1)}, bf16[256,128]{1,0:T(8,128)(2,1)S(1)}, u32[]{:S(2)}, u32[]{:S(2)}) collective-permute-start(bf16[256,128]{1,0:T(8,128)(2,1)S(1)} %collective-permute-done.5.mine_ref), channel_id=1, source_target_pairs={{0,1},{1,0},{2,3},{3,2},{4,5},{5,4},{6,7},{7,6},{8,9},{9,8},{10,11... | collective-permute-start | bytes 196616 | tf_op jit(solution)/shard_map/ppermute | solution.py:400
  24.9 5.7 %collective-permute-start.7 = (bf16[144,384]{1,0:T(8,128)(2,1)S(1)}, bf16[144,384]{1,0:T(8,128)(2,1)S(1)}, u32[]{:S(2)}, u32[]{:S(2)}) collective-permute-start(bf16[144,384]{1,0:T(8,128)(2,1)S(1)} %get-tuple-element.37), channel_id=1, source_target_pairs={{0,8},{8,0},{9,17},{17,9},{16,24},{24,16},{1,3},{3,1},{25,27},{27,... | collective-permute-start | bytes 331784 | tf_op jit(solution)/shard_map/ppermute | solution.py:386
  30.6 1.3 %collective-permute-start.8 = (bf16[144,384]{1,0:T(8,128)(2,1)S(1)}, bf16[144,384]{1,0:T(8,128)(2,1)S(1)}, u32[]{:S(2)}, u32[]{:S(2)}) collective-permute-start(bf16[144,384]{1,0:T(8,128)(2,1)S(1)} %collective-permute-done.7.mine_ref), channel_id=1, source_target_pairs={{0,1},{1,0},{2,3},{3,2},{4,5},{5,4},{6,7},{7,6},{8,9},{9,8},{10,11... | collective-permute-start | bytes 331784 | tf_op jit(solution)/shard_map/ppermute | solution.py:400

commit v4 on v3

--- a/solution.py
+++ b/solution.py
@@ -21,6 +21,9 @@
 
 RIM = 16
 PAD = 8
+CHUNKS = 4
+BLOCKS = 1
+EDGE_PARTS = 4
 
 
 def make_tables(tile, margin, freqs):
@@ -78,6 +81,23 @@
 
 def by_core(core, first, second):
     return jnp.where(core == 0, first, second)
+
+
+def edge_kernel(level_ref, edge_ref, buffer_ref, sems):
+    margin = edge_ref.shape[0]
+    part = margin // EDGE_PARTS
+    place = 1 - lax.rem(lax.axis_index("corner") + lax.axis_index("ty"), 2)
+    copies = []
+    for at in range(EDGE_PARTS):
+        rows = pl.ds(pl.multiple_of(place * margin + at * part, part), part)
+        copies.append(
+            pltpu.make_async_copy(level_ref.at[rows, :], buffer_ref.at[at], sems.at[at])
+        )
+        copies[-1].start()
+    for at, copy in enumerate(copies):
+        copy.wait()
+        values = buffer_ref[at].astype(jnp.float32) * 0.125
+        edge_ref[at * part : (at + 1) * part] = values.astype(jnp.bfloat16)
 
 
 def lift_kernel(counts, level_ref, mine_ref, other_ref, fwd_ref, lift_ref, send_ref):
@@ -135,6 +155,8 @@
     proj_ref,
     field_ref,
     back_ref,
+    done_ref,
+    sems,
 ):
     tile = target_ref.shape[0]
     rows = lift_ref.shape[0]
@@ -149,45 +171,85 @@
     )
     spec_re = mixed[:freqs, :freqs] - mixed[freqs:, freqs:]
     spec_im = mixed[:freqs, freqs:] + mixed[freqs:, :freqs]
+    lanes = [slice(g * freqs, (g + 1) * freqs) for g in range(count)]
+    groups = [range(g, min(g + 2, count)) for g in range(0, count, 2)]
+    dose = dose_ref[0]
+    size = tile // BLOCKS
+    copies = []
+
+    def project(group):
+        for g in group:
+            kernel_re = kernels_ref[g, 0]
+            kernel_im = kernels_ref[g, 1]
+            blur_re = (kernel_re * spec_re - kernel_im * spec_im).astype(jnp.bfloat16)
+            blur_im = (kernel_re * spec_im + kernel_im * spec_re).astype(jnp.bfloat16)
+            blur_ref[:freqs, lanes[g]] = blur_re
+            blur_ref[freqs:, lanes[g]] = blur_im
+        cols = slice(group[0] * freqs, (group[-1] + 1) * freqs)
+        proj = dot(inv_ref[...], blur_ref[:, cols]).astype(jnp.bfloat16)
+        for at, g in enumerate(group):
+            for part in range(2):
+                lane = (2 * g + part) * freqs
+                proj_ref[:, lane : lane + freqs] = proj[part * tile : (part + 1) * tile, lanes[at]]
+
+    def forward(block, g):
+        at = slice(block * size, (block + 1) * size)
+        pair = proj_ref[at, 2 * g * freqs : 2 * (g + 1) * freqs]
+        field_ref[g, at] = dot(pair, inv_t_ref[...])
+
+    def sensitivity(block):
+        at = slice(block * size, (block + 1) * size)
+        power = None
+        for g in range(count):
+            field = field_ref[g, at]
+            term = field[:, :tile] * field[:, :tile] + field[:, tile:] * field[:, tile:]
+            power = term if power is None else power + term
+        resist = jax.nn.sigmoid(STEEPNESS * (dose * power - THRESHOLD))
+        done_ref[at] = resist
+        copies.append(
+            pltpu.make_async_copy(done_ref.at[at, :], resist_ref.at[at, :], sems.at[block])
+        )
+        copies[-1].start()
+        goal = target_ref[at].astype(jnp.float32)
+        return (4.0 * STEEPNESS * dose) * (resist - goal) * (resist * (1.0 - resist))
+
+    def backward(block, g, twice):
+        at = slice(block * size, (block + 1) * size)
+        adj_re = (twice * field_ref[g, at, :tile]).astype(jnp.bfloat16)
+        adj_im = (twice * field_ref[g, at, tile:]).astype(jnp.bfloat16)
+        adj = jnp.concatenate([adj_re, adj_im], axis=1)
+        back = dot(adj, inv_ref[...]).astype(jnp.bfloat16)
+        back_ref[block * size : (block + 1) * size, lanes[g]] = back[:, :freqs]
+        back_ref[tile + block * size : tile + (block + 1) * size, lanes[g]] = back[:, freqs:]
+
+    for group in groups:
+        project(group)
     for g in range(count):
-        kernel_re = kernels_ref[g, 0]
-        kernel_im = kernels_ref[g, 1]
-        cols = slice(g * freqs, (g + 1) * freqs)
-        blur_ref[:freqs, cols] = (kernel_re * spec_re - kernel_im * spec_im).astype(jnp.bfloat16)
-        blur_ref[freqs:, cols] = (kernel_re * spec_im + kernel_im * spec_re).astype(jnp.bfloat16)
-    proj_ref[...] = dot(inv_ref[...], blur_ref[...]).astype(jnp.bfloat16)
-    power = jnp.zeros((tile, tile), jnp.float32)
-    for g in range(count):
-        cols = slice(g * freqs, (g + 1) * freqs)
-        pair = jnp.concatenate([proj_ref[:tile, cols], proj_ref[tile:, cols]], axis=1)
-        field = dot(pair, inv_t_ref[...])
-        field_ref[g] = field
-        power = power + (field[:, :tile] * field[:, :tile] + field[:, tile:] * field[:, tile:])
-    dose = dose_ref[0]
-    resist = jax.nn.sigmoid(STEEPNESS * (dose * power - THRESHOLD))
-    resist_ref[...] = resist
-    goal = target_ref[...].astype(jnp.float32)
-    sens = 2.0 * (resist - goal) * STEEPNESS * dose * resist * (1.0 - resist)
-    twice = 2.0 * sens
-    twice = jnp.concatenate([twice, twice], axis=1)
-    for g in range(count):
-        cols = slice(g * freqs, (g + 1) * freqs)
-        back = dot((twice * field_ref[g]).astype(jnp.bfloat16), inv_ref[...]).astype(jnp.bfloat16)
-        back_ref[:tile, cols] = back[:, :freqs]
-        back_ref[tile:, cols] = back[:, freqs:]
-    blurred = dot(inv_t_ref[...], back_ref[...])
-    grad_re = jnp.zeros((freqs, freqs), jnp.float32)
-    grad_im = jnp.zeros((freqs, freqs), jnp.float32)
-    for g in range(count):
-        kernel_re = kernels_ref[g, 0]
-        kernel_im = kernels_ref[g, 1]
-        cols = slice(g * freqs, (g + 1) * freqs)
-        blur_re = blurred[:freqs, cols]
-        blur_im = blurred[freqs:, cols]
-        grad_re = grad_re + (kernel_re * blur_re + kernel_im * blur_im)
-        grad_im = grad_im + (kernel_re * blur_im - kernel_im * blur_re)
+        forward(0, g)
+    for block in range(BLOCKS):
+        twice = sensitivity(block)
+        for g in range(count):
+            if block + 1 < BLOCKS:
+                forward(block + 1, g)
+        for g in range(count):
+            backward(block, g, twice)
+    grad_re = None
+    for group in groups:
+        cols = slice(group[0] * freqs, (group[-1] + 1) * freqs)
+        blurred = dot(inv_t_ref[...], back_ref[:, cols])
+        for at, g in enumerate(group):
+            kernel_re = kernels_ref[g, 0]
+            kernel_im = kernels_ref[g, 1]
+            blur_re = blurred[:freqs, lanes[at]]
+            blur_im = blurred[freqs:, lanes[at]]
+            term_re = kernel_re * blur_re + kernel_im * blur_im
+            term_im = kernel_re * blur_im - kernel_im * blur_re
+            grad_re = term_re if grad_re is None else grad_re + term_re
+            grad_im = term_im if g == 0 else grad_im + term_im
     grad_ref[:freqs, :] = grad_re
     grad_ref[freqs:, :] = grad_im
+    for copy in copies:
+        copy.wait()
 
 
 def lift_grad_kernel(
@@ -224,56 +286,106 @@
     send_ref[...] = dot(send_rows_ref[to_after], lift_ref[...]).astype(jnp.bfloat16)
 
 
+def grid_masks(counts, margin):
+    lane = lax.broadcasted_iota(jnp.int32, (PAD, margin), 1)
+    at_ty, at_tx = lax.axis_index("ty"), lax.axis_index("tx")
+    every = lane >= 0
+    above = every & (at_ty > 0)
+    below = every & (at_ty < counts["ty"] - 1)
+    beside = ((lane >= margin // 2) & (at_tx > 0)) | (
+        (lane < margin // 2) & (at_tx < counts["tx"] - 1)
+    )
+    return above, below, beside
+
+
+def within(keeps, rows, blocks, at, block, level):
+    above, below, beside = keeps
+    if at == 0:
+        level = jnp.where(above, level, 0.0)
+    if at == rows - PAD:
+        level = jnp.where(below, level, 0.0)
+    if block == blocks - 1:
+        level = jnp.where(beside, level, 0.0)
+    return level
+
+
+def stencil(source, at, wanted, margin):
+    blocks = len(source)
+    lane = lax.broadcasted_iota(jnp.int32, (PAD, margin), 1)
+    here = [ref[PAD + at : 2 * PAD + at] for ref in source]
+    back = [pltpu.roll(part, 1, 1) for part in here]
+    ahead = [pltpu.roll(part, margin - 1, 1) for part in here]
+    for block in range(wanted):
+        up = source[block][PAD + at - 1 : 2 * PAD + at - 1]
+        down = source[block][PAD + at + 1 : 2 * PAD + at + 1]
+        left = jnp.where(lane == 0, back[block - 1], back[block])
+        right = jnp.where(lane == margin - 1, ahead[(block + 1) % blocks], ahead[block])
+        slope_y = down - up
+        slope_x = right - left
+        square = GRAD_FLOOR + slope_y * slope_y + slope_x * slope_x
+        base = (1.0 - 4.0 * SMOOTHING) * here[block] + SMOOTHING * ((up + down) + (left + right))
+        yield base, square * lax.rsqrt(square)
+
+
 def frame_kernel(
     counts,
     lift_ref, own_rows_ref, level_ref, mine_ref, other_ref, cols_mine_ref, cols_other_ref,
-    grad_ref, frame_ref, slope_ref,
+    grad_ref, slope_ref, base_ref, root_ref, *level_refs,
 ):
     tile = level_ref.shape[0]
     margin = mine_ref.shape[0]
     rows = lift_ref.shape[0]
     grad_ref[...] = dot(own_rows_ref[...], lift_ref[...])
     above, below = ordered("ty", counts, mine_ref[...], other_ref[...])
-    frame_ref[:PAD, :tile] = 0.5 * above.astype(jnp.float32)[margin - PAD :]
-    frame_ref[PAD : PAD + tile, :tile] = level_ref[...].astype(jnp.float32) * 0.0625
-    frame_ref[PAD + tile :, :tile] = 0.5 * below.astype(jnp.float32)[:PAD]
+    blocks = len(level_refs)
+    extent = slope_ref.shape[0]
+    level = level_ref[...].astype(jnp.float32) * 0.0625
+    above = 0.5 * above.astype(jnp.float32)[margin - PAD :]
+    below = 0.5 * below.astype(jnp.float32)[:PAD]
+    zero = jnp.zeros((PAD, margin), jnp.float32)
+    for block, ref in enumerate(level_refs):
+        ref[:PAD] = zero
+        ref[PAD + extent :] = zero
+        if block < blocks - 1:
+            lanes = slice(block * margin, (block + 1) * margin)
+            ref[PAD : 2 * PAD] = above[:, lanes]
+            ref[2 * PAD : 2 * PAD + tile] = level[:, lanes]
+            ref[2 * PAD + tile : PAD + extent] = below[:, lanes]
     at = lax.broadcasted_iota(jnp.int32, (RIM, margin), 0)
     lane = lax.broadcasted_iota(jnp.int32, (RIM, margin), 1)
     place_left = ((lane == margin - LS_STEPS + at) & (at < LS_STEPS)).astype(jnp.bfloat16)
     place_right = ((lane == at) & (at < LS_STEPS)).astype(jnp.bfloat16)
+    side = level_refs[-1]
     for block in range(tile // margin + 1):
         part = slice(rows + block * RIM, rows + (block + 1) * RIM)
         left, right = ordered("tx", counts, cols_mine_ref[part, :], cols_other_ref[part, :])
         placed = dot_general(left, place_left, 0, 0) + dot_general(right, place_right, 0, 0)
         placed = 0.5 * placed
         if block < tile // margin:
-            start = PAD + block * margin
-            frame_ref[start : start + margin, tile:] = placed
+            start = 2 * PAD + block * margin
+            side[start : start + margin] = placed
         else:
-            frame_ref[PAD + tile :, tile:] = placed[:PAD]
-            frame_ref[:PAD, tile:] = placed[PAD:RIM]
-    trans = jnp.tanh(0.5 * frame_ref[...])
-    slope_ref[...] = (SPEED_GAIN * 0.5 * 0.25) * (1.0 - trans * trans)
+            side[2 * PAD + tile : PAD + extent] = placed[:PAD]
+            side[PAD : 2 * PAD] = placed[PAD:RIM]
+    for at in range(0, extent, PAD):
+        for block, (base, root) in enumerate(stencil(level_refs, at, blocks, margin)):
+            lanes = slice(block * margin, (block + 1) * margin)
+            trans = jnp.tanh(0.5 * level_refs[block][PAD + at : 2 * PAD + at])
+            base_ref[at : at + PAD, lanes] = base
+            root_ref[at : at + PAD, lanes] = root
+            slope_ref[at : at + PAD, lanes] = (SPEED_GAIN * 0.5 * 0.25) * (1.0 - trans * trans)
 
 
 def advance_kernel(
-    counts, grad_ref, mine_ref, other_ref, frame_ref, slope_ref, out_ref, speed_ref, *level_refs
+    counts, grad_ref, mine_ref, other_ref, slope_ref, base_ref, root_ref, out_ref,
+    speed_ref, done_ref, sems, *level_refs,
 ):
+    rows, cols = slope_ref.shape
     tile = out_ref.shape[0]
-    rows, cols = frame_ref.shape
     margin = cols - tile
     blocks = cols // margin
     first, last = level_refs[:blocks], level_refs[blocks:]
-
-    lane = lax.broadcasted_iota(jnp.int32, (PAD, margin), 1)
-    at_ty, at_tx = lax.axis_index("ty"), lax.axis_index("tx")
-    all_lanes = lane >= 0
-    keep_above = all_lanes & (at_ty > 0)
-    keep_below = all_lanes & (at_ty < counts["ty"] - 1)
-    keep_cols = ((lane >= margin // 2) & (at_tx > 0)) | (
-        (lane < margin // 2) & (at_tx < counts["tx"] - 1)
-    )
-
+    keeps = grid_masks(counts, margin)
     before, after = ordered("ty", counts, mine_ref[...], other_ref[...])
     before = before.astype(jnp.float32)
     after = after.astype(jnp.float32)
@@ -288,41 +400,43 @@
     for ref in level_refs:
         ref[:PAD] = jnp.zeros((PAD, margin), jnp.float32)
         ref[PAD + rows :] = jnp.zeros((PAD, margin), jnp.float32)
-    for block in range(blocks):
-        first[block][PAD : PAD + rows] = frame_ref[:, block * margin : (block + 1) * margin]
-
+
+    def store(target, at, block, level):
+        level = within(keeps, rows, blocks, at, block, level)
+        target[block][PAD + at : 2 * PAD + at] = level
+
+    for at in range(0, rows, PAD):
+        for block in range(blocks):
+            lanes = slice(block * margin, (block + 1) * margin)
+            level = (
+                base_ref[at : at + PAD, lanes]
+                - speed_ref[at : at + PAD, lanes] * root_ref[at : at + PAD, lanes]
+            )
+            store(first, at, block, level)
     source, target = first, last
-    for step in range(LS_STEPS):
+    copies = []
+    for step in range(1, LS_STEPS):
         final = step == LS_STEPS - 1
         for at in range(PAD if final else 0, rows - PAD if final else rows, PAD):
-            here = [ref[PAD + at : 2 * PAD + at] for ref in source]
-            back = [pltpu.roll(part, 1, 1) for part in here]
-            ahead = [pltpu.roll(part, margin - 1, 1) for part in here]
-            for block in range(blocks - 1 if final else blocks):
-                up = source[block][PAD + at - 1 : 2 * PAD + at - 1]
-                down = source[block][PAD + at + 1 : 2 * PAD + at + 1]
-                left = jnp.where(lane == 0, back[block - 1], back[block])
-                right = jnp.where(lane == margin - 1, ahead[(block + 1) % blocks], ahead[block])
-                slope_y = down - up
-                slope_x = right - left
-                square = GRAD_FLOOR + slope_y * slope_y + slope_x * slope_x
-                level = (
-                    (1.0 - 4.0 * SMOOTHING) * here[block]
-                    + SMOOTHING * ((up + down) + (left + right))
-                    - speed_ref[at : at + PAD, block * margin : (block + 1) * margin]
-                    * (square * lax.rsqrt(square))
+            parts = list(stencil(source, at, blocks - 1 if final else blocks, margin))
+            for block, (base, root) in enumerate(parts):
+                lanes = slice(block * margin, (block + 1) * margin)
+                level = base - speed_ref[at : at + PAD, lanes] * root
+                if final:
+                    done_ref[at - PAD : at, lanes] = 2.0 * level
+                else:
+                    store(target, at, block, level)
+            chunk = tile // CHUNKS
+            if final and at % chunk == 0:
+                piece = slice(at - chunk, at)
+                copy = pltpu.make_async_copy(
+                    done_ref.at[piece, :], out_ref.at[piece, :], sems.at[at // chunk - 1]
                 )
-                if final:
-                    out_ref[at - PAD : at, block * margin : (block + 1) * margin] = 2.0 * level
-                    continue
-                if at == 0:
-                    level = jnp.where(keep_above, level, 0.0)
-                if at == rows - PAD:
-                    level = jnp.where(keep_below, level, 0.0)
-                if block == blocks - 1:
-                    level = jnp.where(keep_cols, level, 0.0)
-                target[block][PAD + at : 2 * PAD + at] = level
+                copy.start()
+                copies.append(copy)
         source, target = target, source
+    for copy in copies:
+        copy.wait()
 
 
 def load_kernel(*refs):
@@ -350,14 +464,14 @@
     )(*[pltpu.with_memory_space_constraint(item, pltpu.HBM) for item in arrays])
 
 
-def call(kernel, out_shape, *args, scratch=(), smem=0):
+def call(kernel, out_shape, *args, scratch=(), smem=0, out_space=()):
     vmem = pl.BlockSpec(memory_space=pltpu.VMEM)
     in_specs = [pl.BlockSpec(memory_space=pltpu.SMEM)] * smem + [vmem] * (len(args) - smem)
     return pl.pallas_call(
         kernel,
         out_shape=[jax.ShapeDtypeStruct(*item) for item in out_shape],
         in_specs=in_specs,
-        out_specs=[vmem] * len(out_shape),
+        out_specs=[pl.BlockSpec(memory_space=space) for space in out_space or [pltpu.VMEM] * len(out_shape)],
         scratch_shapes=list(scratch),
         compiler_params=pltpu.CompilerParams(vmem_limit_bytes=24 << 20),
     )(*args)
@@ -406,12 +520,20 @@
     freqs = KF
     count = kernels.shape[1]
     tables = make_tables(tile, margin, freqs)
-    to_after = 1 - lax.rem(lax.axis_index("corner") + lax.axis_index("ty"), 2)
     bf16, f32 = jnp.bfloat16, jnp.float32
     counts = {"ty": lax.axis_size("ty"), "tx": lax.axis_size("tx")}
-
-    edge = lax.dynamic_slice_in_dim(level_init, to_after * (tile - margin), margin, axis=0)
-    edge = (edge.astype(f32) * 0.125).astype(bf16)
+    edge = pl.pallas_call(
+        edge_kernel,
+        out_shape=jax.ShapeDtypeStruct((margin, tile), bf16),
+        in_specs=[pl.BlockSpec(memory_space=pltpu.HBM)],
+        out_specs=pl.BlockSpec(memory_space=pltpu.VMEM),
+        scratch_shapes=[
+            pltpu.VMEM((EDGE_PARTS, margin // EDGE_PARTS, tile), level_init.dtype),
+            pltpu.SemaphoreType.DMA((EDGE_PARTS,)),
+        ],
+        compiler_params=pltpu.CompilerParams(vmem_limit_bytes=24 << 20),
+        name="edge",
+    )(pltpu.with_memory_space_constraint(level_init, pltpu.HBM))
     rows_mine = along("ty", edge)
     rows_other = across(rows_mine)
     names = sorted(tables)
@@ -435,10 +557,13 @@
         smem=1,
         scratch=[
             pltpu.VMEM((2 * freqs, count * freqs), bf16),
-            pltpu.VMEM((2 * tile, count * freqs), bf16),
+            pltpu.VMEM((tile, 2 * count * freqs), bf16),
             pltpu.VMEM((count, tile, 2 * tile), f32),
             pltpu.VMEM((2 * tile, count * freqs), bf16),
+            pltpu.VMEM((tile, tile), f32),
+            pltpu.SemaphoreType.DMA((BLOCKS,)),
         ],
+        out_space=(pltpu.HBM, pltpu.VMEM),
     )
     grad = (grad + across(grad)).astype(bf16)
     grad_mine = along("tx", grad)
@@ -451,17 +576,24 @@
     piece_mine = along("ty", piece)
     piece_other = across(piece_mine)
     framed = (tile + RIM, tile + margin)
-    own, frame, slope = call(
+    levels = [pltpu.VMEM((framed[0] + 2 * PAD, margin), f32)] * (framed[1] // margin)
+    frame = call(
         functools.partial(frame_kernel, counts),
-        [(framed, f32)] * 3,
+        [(framed, f32)] * 4,
         grad_lift, tables["own_rows"], level_init, rows_mine, rows_other, cols_mine, cols_other,
+        scratch=levels,
     )
     (level,) = call(
         functools.partial(advance_kernel, counts),
         [((tile, tile), f32)],
-        own, piece_mine, piece_other, frame, slope,
-        scratch=[pltpu.VMEM(framed, f32)]
-        + [pltpu.VMEM((framed[0] + 2 * PAD, margin), f32)] * (2 * framed[1] // margin),
+        frame[0], piece_mine, piece_other, *frame[1:],
+        out_space=(pltpu.HBM,),
+        scratch=[
+            pltpu.VMEM(framed, f32),
+            pltpu.VMEM((tile, tile), f32),
+            pltpu.SemaphoreType.DMA((CHUNKS,)),
+        ]
+        + levels * 2,
     )
     return (resist[None], level)
 

time: 33.6 us -> 33.3 us (level)
  other arithmetic: 0.94 us -> 0.02 us
  Pallas kernels: 6.76 us -> 7.51 us
    convert_element_type x1 -> x0, other arithmetic: 0.92 us -> none  [step(): edge = (edge.astype(f32) * 0.125).astype(bf16)]
    pallas_call x0 -> x1, Pallas kernels: none -> 0.86 us  [step(): pl.pallas_call(edge_kernel, out_shape=jax.ShapeDtypeStruct((margin, tile)...]
  transfers between devices with their start and end apart: 9 -> 9, of which waited for: 8 -> 8; matrix products, arithmetic and copies ran while one was open for 0% -> 0% of each run, Pallas kernels for 6% -> 7%
where the time goes in v4:
time: 33.3 us; the launch traced here: 33 us
  waiting for transfers between devices  15.6 us (47%)
  starting transfers between devices  8.58 us (26%)
  Pallas kernels  7.51 us (23%)
  between operations  1.34 us (4%)
    ppermute x4, waiting for transfers between devices, along(): return lax.ppermute(values, ('ty', 'tx', 'corner'), pairs)  11.8 us
    ppermute x4, starting transfers between devices, along(): return lax.ppermute(values, ('ty', 'tx', 'corner'), pairs)  8.24 us
    pallas_call x5, Pallas kernels, call(): pl.pallas_call(kernel, out_shape=[jax.ShapeDtypeStruct(*item) for item in...  4.88 us
    ppermute x5, waiting for transfers between devices, across(): return lax.ppermute(values, 'corner', [(0, 1), (1, 0)])  3.74 us
    pallas_call x1, Pallas kernels, load(): pl.pallas_call(load_kernel, out_shape=[jax.ShapeDtypeStruct(item.shape, i...  1.77 us
    pallas_call x1, Pallas kernels, step(): pl.pallas_call(edge_kernel, out_shape=jax.ShapeDtypeStruct((margin, tile)...  0.86 us
  transfers between devices with their start and end apart: 9, of which 8 were waited for; matrix products, arithmetic and copies ran while one was open for 0% of the time, Pallas kernels for 7%

profile of v4, /device:TPU:0, one launch (start us, length us, event | category | flops | bytes accessed | tf_op | source)
XLA Modules:
  0.0 33.0 jit_solution(9870840457862000435)
XLA Ops:
  0.6 0.9 %edge.1 = bf16[128,256]{1,0:T(8,128)(2,1)S(1)} custom-call(s32[256,256]{1,0:T(8,128)} %level_ref.1), custom_call_target="tpu_custom_call" | custom-call | tf_op jit(solution)/shard_map/edge/pallas_call | solution.py:525
  1.5 3.0 %collective-permute-start = (bf16[128,256]{1,0:T(8,128)(2,1)S(1)}, bf16[128,256]{1,0:T(8,128)(2,1)S(1)}, u32[]{:S(2)}, u32[]{:S(2)}) collective-permute-start(bf16[128,256]{1,0:T(8,128)(2,1)S(1)} %edge.1), channel_id=1, source_target_pairs={{0,8},{8,0},{9,17},{17,9},{16,24},{24,16},{1,3},{3,1},{25,27},{27,... | collective-permute-start | bytes 196616 | tf_op jit(solution)/shard_map/ppermute | solution.py:500
  4.5 2.6 %collective-permute-done.mine_ref = bf16[128,256]{1,0:T(8,128)(2,1)S(1)} collective-permute-done((bf16[128,256]{1,0:T(8,128)(2,1)S(1)}, bf16[128,256]{1,0:T(8,128)(2,1)S(1)}, u32[]{:S(2)}, u32[]{:S(2)}) %collective-permute-start) | collective-permute-done | bytes 65568 | tf_op jit(solution)/shard_map/ppermute | solution.py:500
  7.1 0.0 collective-permute-start.1
  7.1 1.8 %load.1 = (s32[256,256]{1,0:T(8,128)S(1)}, s32[256,256]{1,0:T(8,128)S(1)}, f32[5,2,128,128]{3,2,1,0:T(8,128)S(1)}, bf16[256,512]{1,0:T(8,128)(2,1)S(1)}, bf16[51...) custom-call(s32[256,256]{1,0:T(8,128)} %level_ref.1, ...), custom_call_target="tpu_custom_call" | custom-call | bytes 8388608 | tf_op jit(solution)/shard_map/load/pallas_call | solution.py:455
  8.9 0.0 collective-permute-done.1.other_ref
  8.9 0.3 shard_map.122
  9.2 1.7 %collective-permute-start.2 = (bf16[304,128]{1,0:T(8,128)(2,1)S(1)}, bf16[304,128]{1,0:T(8,128)(2,1)S(1)}, u32[]{:S(2)}, u32[]{:S(2)}) collective-permute-start(bf16[304,128]{1,0:T(8,128)(2,1)S(1)} %get-tuple-element.25), channel_id=1, source_target_pairs={{1,2},{2,1},{3,4},{4,3},{5,6},{6,5},{0,8},{8,0},{7,15},{15,7},{9,1... | collective-permute-start | bytes 233480 | tf_op jit(solution)/shard_map/ppermute | solution.py:500
  11.0 2.7 %collective-permute-done.2.mine_ref.cols_mine_ref = bf16[304,128]{1,0:T(8,128)(2,1)S(1)} collective-permute-done((bf16[304,128]{1,0:T(8,128)(2,1)S(1)}, bf16[304,128]{1,0:T(8,128)(2,1)S(1)}, u32[]{:S(2)}, u32[]{:S(2)}) %collective-permute-start.2) | collective-permute-done | bytes 77856 | tf_op jit(solution)/shard_map/ppermute | solution.py:500
  13.7 0.1 collective-permute-start.3
  14.5 0.5 %collective-permute-done.3.other_ref.cols_other_ref = bf16[304,128]{1,0:T(8,128)(2,1)S(1)} collective-permute-done((bf16[304,128]{1,0:T(8,128)(2,1)S(1)}, bf16[304,128]{1,0:T(8,128)(2,1)S(1)}, u32[]{:S(2)}, u32[]{:S(2)}) %collective-permute-start.3) | collective-permute-done | bytes 77856 | tf_op jit(solution)/shard_map/ppermute | solution.py:514
  15.0 2.2 %shard_map.123 = (f32[256,256]{1,0:T(8,128)}, f32[256,128]{1,0:T(8,128)S(1)}) custom-call(f32[1]{0:T(128)S(6)} %copy.13.dose_ref, bf16[256,256]{1,0:T(8,128)(2,1)S(1)} %get-tuple-element.24.lift_ref, bf16[304,128]{1,0:T(8,128)(2,1)S(1)} %collective-permute-done.2.mine_ref.cols_mine_ref, bf16[304,128]{1,0:T(8,128)(2,1)S(1)} %collective-permute-done.3.other_ref.cols_other_ref, ...), custom_call_target="tpu_custom_call" | custom-call | tf_op jit(solution)/shard_map/pallas_call | solution.py:470
  17.2 0.2 collective-permute-start.4
  17.4 1.2 %collective-permute-done.4 = f32[256,128]{1,0:T(8,128)S(1)} collective-permute-done((f32[256,128]{1,0:T(8,128)S(1)}, f32[256,128]{1,0:T(8,128)S(1)}, u32[]{:S(2)}, u32[]{:S(2)}) %collective-permute-start.4) | collective-permute-done | bytes 131104 | tf_op jit(solution)/shard_map/ppermute | solution.py:514
  18.6 1.7 %collective-permute-start.5 = (bf16[256,128]{1,0:T(8,128)(2,1)S(1)}, bf16[256,128]{1,0:T(8,128)(2,1)S(1)}, u32[]{:S(2)}, u32[]{:S(2)}) collective-permute-start(bf16[256,128]{1,0:T(8,128)(2,1)S(1)} %add_convert_fusion.grad_ref), channel_id=1, source_target_pairs={{1,2},{2,1},{3,4},{4,3},{5,6},{6,5},{0,8},{8,0},{7,15},{15,7},{9,1... | collective-permute-start | bytes 196616 | tf_op jit(solution)/shard_map/ppermute | solution.py:500
  20.3 2.6 %collective-permute-done.5.mine_ref = bf16[256,128]{1,0:T(8,128)(2,1)S(1)} collective-permute-done((bf16[256,128]{1,0:T(8,128)(2,1)S(1)}, bf16[256,128]{1,0:T(8,128)(2,1)S(1)}, u32[]{:S(2)}, u32[]{:S(2)}) %collective-permute-start.5) | collective-permute-done | bytes 65568 | tf_op jit(solution)/shard_map/ppermute | solution.py:500
  22.9 0.0 collective-permute-start.6
  22.9 1.3 %collective-permute-done.6.other_ref = bf16[256,128]{1,0:T(8,128)(2,1)S(1)} collective-permute-done((bf16[256,128]{1,0:T(8,128)(2,1)S(1)}, bf16[256,128]{1,0:T(8,128)(2,1)S(1)}, u32[]{:S(2)}, u32[]{:S(2)}) %collective-permute-start.6) | collective-permute-done | bytes 65568 | tf_op jit(solution)/shard_map/ppermute | solution.py:514
  24.2 0.6 %shard_map.124 = (bf16[256,384]{1,0:T(8,128)(2,1)S(1)}, bf16[144,384]{1,0:T(8,128)(2,1)S(1)}) custom-call(bf16[256,128]{1,0:T(8,128)(2,1)S(1)} %add_convert_fusion.grad_ref, bf16[256,128]{1,0:T(8,128)(2,1)S(1)} %collective-permute-done.5.mine_ref, bf16[256,128]{1,0:T(8,128)(2,1)S(1)} %collective-permute-done.6.other_ref, ...), custom_call_target="tpu_custom_call" | custom-call | tf_op jit(solution)/shard_map/pallas_call | solution.py:470
  24.8 1.7 %collective-permute-start.7 = (bf16[144,384]{1,0:T(8,128)(2,1)S(1)}, bf16[144,384]{1,0:T(8,128)(2,1)S(1)}, u32[]{:S(2)}, u32[]{:S(2)}) collective-permute-start(bf16[144,384]{1,0:T(8,128)(2,1)S(1)} %get-tuple-element.38), channel_id=1, source_target_pairs={{0,8},{8,0},{9,17},{17,9},{16,24},{24,16},{1,3},{3,1},{25,27},{27,... | collective-permute-start | bytes 331784 | tf_op jit(solution)/shard_map/ppermute | solution.py:500
  26.5 3.9 %collective-permute-done.7.mine_ref = bf16[144,384]{1,0:T(8,128)(2,1)S(1)} collective-permute-done((bf16[144,384]{1,0:T(8,128)(2,1)S(1)}, bf16[144,384]{1,0:T(8,128)(2,1)S(1)}, u32[]{:S(2)}, u32[]{:S(2)}) %collective-permute-start.7) | collective-permute-done | bytes 110624 | tf_op jit(solution)/shard_map/ppermute | solution.py:500
  30.4 0.0 collective-permute-start.8
  30.4 0.5 %shard_map.125 = (f32[272,384]{1,0:T(8,128)S(1)}, f32[272,384]{1,0:T(8,128)S(1)}, f32[272,384]{1,0:T(8,128)S(1)}, f32[272,384]{1,0:T(8,128)S(1)}) custom-call(bf16[256,384]{1,0:T(8,128)(2,1)S(1)} %get-tuple-element.35.lift_ref, bf16[272,256]{1,0:T(8,128)(2,1)S(1)} %get-tuple-element.36.own_rows_ref, s32[256,256]{1,0:T(8,128)S(1)} %get-tuple-element.22.level_ref, ...), custom_call_target="tpu_custom_call" | custom-call | tf_op jit(solution)/shard_map/pallas_call | solution.py:470
  31.0 0.8 %collective-permute-done.8.other_ref = bf16[144,384]{1,0:T(8,128)(2,1)S(1)} collective-permute-done((bf16[144,384]{1,0:T(8,128)(2,1)S(1)}, bf16[144,384]{1,0:T(8,128)(2,1)S(1)}, u32[]{:S(2)}, u32[]{:S(2)}) %collective-permute-start.8) | collective-permute-done | bytes 110624 | tf_op jit(solution)/shard_map/ppermute | solution.py:514
  31.8 1.3 %shard_map.126 = f32[256,256]{1,0:T(8,128)} custom-call(f32[272,384]{1,0:T(8,128)S(1)} %get-tuple-element.37.grad_ref, bf16[144,384]{1,0:T(8,128)(2,1)S(1)} %collective-permute-done.7.mine_ref, bf16[144,384]{1,0:T(8,128)(2,1)S(1)} %collective-permute-done.8.other_ref, f32[272,384]{1,0:T(8,128)S(1)} %get-tuple-element.39.slope_ref, ...), custom_call_target="tpu_custom_call" | custom-call | tf_op jit(solution)/shard_map/pallas_call | solution.py:470
  (1 shorter events, 0.0 us)
Async XLA Ops:
  1.5 5.6 %collective-permute-start = (bf16[128,256]{1,0:T(8,128)(2,1)S(1)}, bf16[128,256]{1,0:T(8,128)(2,1)S(1)}, u32[]{:S(2)}, u32[]{:S(2)}) collective-permute-start(bf16[128,256]{1,0:T(8,128)(2,1)S(1)} %edge.1), channel_id=1, source_target_pairs={{0,8},{8,0},{9,17},{17,9},{16,24},{24,16},{1,3},{3,1},{25,27},{27,... | collective-permute-start | bytes 196616 | tf_op jit(solution)/shard_map/ppermute | solution.py:500
  7.1 1.8 %collective-permute-start.1 = (bf16[128,256]{1,0:T(8,128)(2,1)S(1)}, bf16[128,256]{1,0:T(8,128)(2,1)S(1)}, u32[]{:S(2)}, u32[]{:S(2)}) collective-permute-start(bf16[128,256]{1,0:T(8,128)(2,1)S(1)} %collective-permute-done.mine_ref), channel_id=1, source_target_pairs={{0,1},{1,0},{2,3},{3,2},{4,5},{5,4},{6,7},{7,6},{8,9},{9,8},{10,11... | collective-permute-start | bytes 196616 | tf_op jit(solution)/shard_map/ppermute | solution.py:514
  9.2 4.5 %collective-permute-start.2 = (bf16[304,128]{1,0:T(8,128)(2,1)S(1)}, bf16[304,128]{1,0:T(8,128)(2,1)S(1)}, u32[]{:S(2)}, u32[]{:S(2)}) collective-permute-start(bf16[304,128]{1,0:T(8,128)(2,1)S(1)} %get-tuple-element.25), channel_id=1, source_target_pairs={{1,2},{2,1},{3,4},{4,3},{5,6},{6,5},{0,8},{8,0},{7,15},{15,7},{9,1... | collective-permute-start | bytes 233480 | tf_op jit(solution)/shard_map/ppermute | solution.py:500
  13.7 1.3 %collective-permute-start.3 = (bf16[304,128]{1,0:T(8,128)(2,1)S(1)}, bf16[304,128]{1,0:T(8,128)(2,1)S(1)}, u32[]{:S(2)}, u32[]{:S(2)}) collective-permute-start(bf16[304,128]{1,0:T(8,128)(2,1)S(1)} %collective-permute-done.2.mine_ref.cols_mine_ref), channel_id=1, source_target_pairs={{0,1},{1,0},{2,3},{3,2},{4,5},{5,4},{6,7},{7,6},{8,9},{9,8},{10,11... | collective-permute-start | bytes 233480 | tf_op jit(solution)/shard_map/ppermute | solution.py:514
  17.2 1.4 %collective-permute-start.4 = (f32[256,128]{1,0:T(8,128)S(1)}, f32[256,128]{1,0:T(8,128)S(1)}, u32[]{:S(2)}, u32[]{:S(2)}) collective-permute-start(f32[256,128]{1,0:T(8,128)S(1)} %get-tuple-element.32), channel_id=1, source_target_pairs={{0,1},{1,0},{2,3},{3,2},{4,5},{5,4},{6,7},{7,6},{8,9},{9,8},{10,11... | collective-permute-start | bytes 393224 | tf_op jit(solution)/shard_map/ppermute | solution.py:514
  18.6 4.3 %collective-permute-start.5 = (bf16[256,128]{1,0:T(8,128)(2,1)S(1)}, bf16[256,128]{1,0:T(8,128)(2,1)S(1)}, u32[]{:S(2)}, u32[]{:S(2)}) collective-permute-start(bf16[256,128]{1,0:T(8,128)(2,1)S(1)} %add_convert_fusion.grad_ref), channel_id=1, source_target_pairs={{1,2},{2,1},{3,4},{4,3},{5,6},{6,5},{0,8},{8,0},{7,15},{15,7},{9,1... | collective-permute-start | bytes 196616 | tf_op jit(solution)/shard_map/ppermute | solution.py:500
  22.9 1.3 %collective-permute-start.6 = (bf16[256,128]{1,0:T(8,128)(2,1)S(1)}, bf16[256,128]{1,0:T(8,128)(2,1)S(1)}, u32[]{:S(2)}, u32[]{:S(2)}) collective-permute-start(bf16[256,128]{1,0:T(8,128)(2,1)S(1)} %collective-permute-done.5.mine_ref), channel_id=1, source_target_pairs={{0,1},{1,0},{2,3},{3,2},{4,5},{5,4},{6,7},{7,6},{8,9},{9,8},{10,11... | collective-permute-start | bytes 196616 | tf_op jit(solution)/shard_map/ppermute | solution.py:514
  24.8 5.7 %collective-permute-start.7 = (bf16[144,384]{1,0:T(8,128)(2,1)S(1)}, bf16[144,384]{1,0:T(8,128)(2,1)S(1)}, u32[]{:S(2)}, u32[]{:S(2)}) collective-permute-start(bf16[144,384]{1,0:T(8,128)(2,1)S(1)} %get-tuple-element.38), channel_id=1, source_target_pairs={{0,8},{8,0},{9,17},{17,9},{16,24},{24,16},{1,3},{3,1},{25,27},{27,... | collective-permute-start | bytes 331784 | tf_op jit(solution)/shard_map/ppermute | solution.py:500
  30.4 1.3 %collective-permute-start.8 = (bf16[144,384]{1,0:T(8,128)(2,1)S(1)}, bf16[144,384]{1,0:T(8,128)(2,1)S(1)}, u32[]{:S(2)}, u32[]{:S(2)}) collective-permute-start(bf16[144,384]{1,0:T(8,128)(2,1)S(1)} %collective-permute-done.7.mine_ref), channel_id=1, source_target_pairs={{0,1},{1,0},{2,3},{3,2},{4,5},{5,4},{6,7},{7,6},{8,9},{9,8},{10,11... | collective-permute-start | bytes 331784 | tf_op jit(solution)/shard_map/ppermute | solution.py:514

commit v5 on v4

--- a/solution.py
+++ b/solution.py
@@ -53,14 +53,27 @@
     own_rows = np.concatenate([stacked[:, margin : margin + tile].T, rim_rows[1]])
     send_rows = np.stack(
         [
-            np.concatenate([stacked[:, :margin].T, rim_rows[2]]),
-            np.concatenate([stacked[:, tile + margin :].T, rim_rows[0]]),
+            np.concatenate([stacked[:, :margin].T, rim_rows[2][:PAD]]),
+            np.concatenate([stacked[:, tile + margin :].T, rim_rows[0][PAD:]]),
         ]
     )
+    half = freqs // 2
+    packed = np.concatenate([stacked[:half], stacked[freqs : freqs + half], np.zeros((RIM, window))])
+    packed[2 * half] = stacked[half]
+    expand = np.zeros((2 * freqs, 2 * half + RIM))
+    for row in range(freqs):
+        mirror = row if row <= half else freqs - row
+        expand[row, mirror if row != half else 2 * half] = 1.0
+        if row != half:
+            expand[freqs + row, half + mirror] = 1.0 if row < half else -1.0
+    middle = slice(margin, margin + tile)
+    by_place = np.concatenate([stacked[:, middle], stacked[:, :margin], stacked[:, tile + margin :]], 1).T
     as_const = lambda values: np.asarray(values, np.float32).astype(jnp.bfloat16)
     return {
         "fwd": as_const(stacked),
-        "fwd_t": as_const(stacked.T),
+        "fwd_t": as_const(by_place),
+        "packed": as_const(packed),
+        "expand": as_const(expand),
         "inv": as_const(inverse),
         "inv_t": as_const(inverse.T),
         "rim_cols": as_const(rim_cols),
@@ -100,52 +113,77 @@
         edge_ref[at * part : (at + 1) * part] = values.astype(jnp.bfloat16)
 
 
-def lift_kernel(counts, level_ref, mine_ref, other_ref, fwd_ref, lift_ref, send_ref):
+def squash(values):
+    return jnp.tanh(0.25 * values).astype(jnp.bfloat16)
+
+
+def rim_picker(margin):
+    at = lax.broadcasted_iota(jnp.int32, (RIM, margin), 0)
+    lane = lax.broadcasted_iota(jnp.int32, (RIM, margin), 1)
+    first = by_core(lax.axis_index("corner"), 0, margin - LS_STEPS)
+    return ((lane == first + at) & (at < LS_STEPS)).astype(jnp.bfloat16)
+
+
+def own_lift_kernel(level_ref, packed_ref, lift_ref, strip_ref):
     core = lax.axis_index("corner")
     tile = level_ref.shape[0]
-    margin = mine_ref.shape[0]
+    margin = strip_ref.shape[1]
     level = level_ref[...].astype(jnp.float32) * 0.125
-    above, below = ordered("ty", counts, mine_ref[...], other_ref[...])
+    lift_ref[...] = dot(packed_ref[:, margin : margin + tile], squash(level))
+    strip = by_core(core, level[:, :margin], level[:, tile - margin :]).astype(jnp.bfloat16)
+    pick = rim_picker(margin)
+    for block in range(tile // margin):
+        rows = strip[block * margin : (block + 1) * margin]
+        picked = dot_general(pick, rows, 1, 1).astype(jnp.bfloat16)
+        strip_ref[block * RIM : (block + 1) * RIM] = picked
+
+
+def lift_kernel(counts, lift_ref, strip_ref, mine_ref, other_ref, packed_ref, send_ref):
+    core = lax.axis_index("corner")
+    margin, tile = mine_ref.shape
+    rows = lift_ref.shape[0]
+    lanes = pl.ds(pl.multiple_of(core * (tile - margin), margin), margin)
+    above, below = ordered("ty", counts, mine_ref[:, lanes], other_ref[:, lanes])
     above = above.astype(jnp.float32)
     below = below.astype(jnp.float32)
-    squash = lambda values: jnp.tanh(0.25 * values).astype(jnp.bfloat16)
+    send_ref[:rows, :] = (
+        lift_ref[:, lanes]
+        + dot(packed_ref[:, :margin], squash(above))
+        + dot(packed_ref[:, margin + tile :], squash(below))
+    ).astype(jnp.bfloat16)
+    strips = strip_ref.shape[0]
+    send_ref[rows : rows + strips, :] = strip_ref[...]
+    rim = jnp.where(
+        lax.broadcasted_iota(jnp.int32, (RIM, margin), 0) < PAD, below[:RIM], above[margin - RIM :]
+    )
+    rim = jnp.concatenate([rim, jnp.zeros((margin - RIM, margin), jnp.float32)], axis=0)
+    picked = dot_general(rim_picker(margin), rim.astype(jnp.bfloat16), 1, 1)
+    send_ref[rows + strips :, :] = picked.astype(jnp.bfloat16)
+
+
+def own_spec_kernel(
+    counts, lift_ref, mine_ref, other_ref, packed_ref, expand_ref, fwd_t_ref, mixed_ref
+):
+    margin, tile = mine_ref.shape
+    above, below = ordered("ty", counts, mine_ref[...], other_ref[...])
     lift = (
-        dot(fwd_ref[:, :margin], squash(above))
-        + dot(fwd_ref[:, margin : margin + tile], squash(level))
-        + dot(fwd_ref[:, margin + tile :], squash(below))
+        lift_ref[...]
+        + dot(packed_ref[:, :margin], squash(above.astype(jnp.float32)))
+        + dot(packed_ref[:, margin + tile :], squash(below.astype(jnp.float32)))
     ).astype(jnp.bfloat16)
-    lift_ref[...] = lift
-    rows = lift.shape[0]
-    send_ref[:rows, :] = by_core(core, lift[:, :margin], lift[:, tile - margin :])
-    at = lax.broadcasted_iota(jnp.int32, (RIM, margin), 0)
-    lane = lax.broadcasted_iota(jnp.int32, (RIM, margin), 1)
-    first = by_core(core, 0, margin - LS_STEPS)
-    pick = ((lane == first + at) & (at < LS_STEPS)).astype(jnp.bfloat16)
-    rim = jnp.where(
-        lax.broadcasted_iota(jnp.int32, (RIM, tile), 0) < RIM // 2,
-        below[:RIM],
-        above[margin - RIM :],
-    )
-    strip = by_core(core, level[:, :margin], level[:, tile - margin :]).astype(jnp.bfloat16)
-    rim_strip = by_core(core, rim[:, :margin], rim[:, tile - margin :]).astype(jnp.bfloat16)
-    for block in range(tile // margin):
-        picked = dot_general(pick, strip[block * margin : (block + 1) * margin], 1, 1)
-        send_ref[rows + block * RIM : rows + (block + 1) * RIM, :] = picked.astype(jnp.bfloat16)
-    padded = jnp.concatenate([rim_strip, jnp.zeros((margin - RIM, margin), jnp.bfloat16)], axis=0)
-    block = tile // margin
-    send_ref[rows + block * RIM : rows + (block + 1) * RIM, :] = dot_general(
-        pick, padded, 1, 1
-    ).astype(jnp.bfloat16)
+    lift = dot(expand_ref[...], lift).astype(jnp.bfloat16)
+    mixed_ref[...] = dot(lift, fwd_t_ref[:tile])
 
 
 def corner_kernel(
     counts,
     dose_ref,
-    lift_ref,
+    mixed_ref,
     mine_ref,
     other_ref,
     kernels_ref,
     target_ref,
+    expand_ref,
     fwd_t_ref,
     inv_ref,
     inv_t_ref,
@@ -159,16 +197,12 @@
     sems,
 ):
     tile = target_ref.shape[0]
-    rows = lift_ref.shape[0]
-    freqs = rows // 2
-    margin = mine_ref.shape[1]
+    freqs = expand_ref.shape[0] // 2
+    rows = expand_ref.shape[1]
     count = kernels_ref.shape[0]
-    left, right = ordered("tx", counts, mine_ref[:rows, :], other_ref[:rows, :])
-    mixed = (
-        dot(left, fwd_t_ref[:margin, :])
-        + dot(lift_ref[...], fwd_t_ref[margin : margin + tile, :])
-        + dot(right, fwd_t_ref[margin + tile :, :])
-    )
+    sides = ordered("tx", counts, mine_ref[:rows, :], other_ref[:rows, :])
+    sides = dot(expand_ref[...], jnp.concatenate(sides, axis=1)).astype(jnp.bfloat16)
+    mixed = mixed_ref[...] + dot(sides, fwd_t_ref[tile:])
     spec_re = mixed[:freqs, :freqs] - mixed[freqs:, freqs:]
     spec_im = mixed[:freqs, freqs:] + mixed[freqs:, :freqs]
     lanes = [slice(g * freqs, (g + 1) * freqs) for g in range(count)]
@@ -252,37 +286,38 @@
         copy.wait()
 
 
+def both_parts(values):
+    freqs = values.shape[0] // 2
+    low_re = values[:freqs]
+    low_im = values[freqs:]
+    upper = jnp.concatenate([low_re, low_im], axis=1)
+    lower = jnp.concatenate([low_im, -low_re], axis=1)
+    return jnp.concatenate([upper, lower], axis=0)
+
+
+def own_grad_kernel(grad_ref, fwd_ref, rim_ref, lift_ref):
+    margin = rim_ref.shape[2]
+    tile = fwd_ref.shape[1] - 2 * margin
+    here = both_parts(grad_ref[...])
+    lift_ref[:, :tile] = dot(here, fwd_ref[:, margin : margin + tile])
+    lift_ref[:, tile:] = dot(here, rim_ref[1])
+
+
 def lift_grad_kernel(
-    counts,
-    grad_ref, mine_ref, other_ref, fwd_ref, rim_ref, send_rows_ref, lift_ref, send_ref
+    counts, own_ref, mine_ref, other_ref, fwd_ref, rim_ref, send_rows_ref, lift_ref, send_ref
 ):
     to_after = 1 - lax.rem(lax.axis_index("corner") + lax.axis_index("ty"), 2)
-    freqs = grad_ref.shape[0] // 2
     margin = rim_ref.shape[2]
     tile = fwd_ref.shape[1] - 2 * margin
-    last = tile + margin
-
-    def both(values):
-        low_re = values[:freqs]
-        low_im = values[freqs:]
-        upper = jnp.concatenate([low_re, low_im], axis=1)
-        lower = jnp.concatenate([low_im, -low_re], axis=1)
-        return jnp.concatenate([upper, lower], axis=0)
-
     before, after = ordered("tx", counts, mine_ref[...], other_ref[...])
-    before = both(before)
-    here = both(grad_ref[...])
-    after = both(after)
-    middle = dot(here, fwd_ref[:, margin : margin + tile])
-    lift_ref[:, :margin] = (middle[:, :margin] + dot(before, fwd_ref[:, last:])).astype(
-        jnp.bfloat16
-    )
-    lift_ref[:, tile - margin : tile] = (
-        middle[:, tile - margin :] + dot(after, fwd_ref[:, :margin])
-    ).astype(jnp.bfloat16)
-    lift_ref[:, tile:] = (
-        dot(before, rim_ref[0]) + dot(here, rim_ref[1]) + dot(after, rim_ref[2])
-    ).astype(jnp.bfloat16)
+    before = both_parts(before)
+    after = both_parts(after)
+    first = own_ref[:, :margin] + dot(before, fwd_ref[:, tile + margin :])
+    last = own_ref[:, tile - margin : tile] + dot(after, fwd_ref[:, :margin])
+    rim = own_ref[:, tile:] + dot(before, rim_ref[0]) + dot(after, rim_ref[2])
+    lift_ref[:, :margin] = first.astype(jnp.bfloat16)
+    lift_ref[:, tile - margin : tile] = last.astype(jnp.bfloat16)
+    lift_ref[:, tile:] = rim.astype(jnp.bfloat16)
     send_ref[...] = dot(send_rows_ref[to_after], lift_ref[...]).astype(jnp.bfloat16)
 
 
@@ -334,8 +369,8 @@
 ):
     tile = level_ref.shape[0]
     margin = mine_ref.shape[0]
-    rows = lift_ref.shape[0]
     grad_ref[...] = dot(own_rows_ref[...], lift_ref[...])
+    rows = cols_mine_ref.shape[0] - (tile // margin + 1) * RIM
     above, below = ordered("ty", counts, mine_ref[...], other_ref[...])
     blocks = len(level_refs)
     extent = slope_ref.shape[0]
@@ -389,9 +424,8 @@
     before, after = ordered("ty", counts, mine_ref[...], other_ref[...])
     before = before.astype(jnp.float32)
     after = after.astype(jnp.float32)
-    rim = before[margin:] + after[margin:] + grad_ref[tile:]
-    speed_ref[:PAD] = rim[PAD:] * slope_ref[:PAD]
-    speed_ref[PAD + tile :] = rim[:PAD] * slope_ref[PAD + tile :]
+    speed_ref[:PAD] = (before[margin:] + grad_ref[tile + PAD :]) * slope_ref[:PAD]
+    speed_ref[PAD + tile :] = (after[margin:] + grad_ref[tile : tile + PAD]) * slope_ref[PAD + tile :]
     for half, part in ((0, before), (1, after)):
         at = half * margin
         speed_ref[PAD + at : PAD + at + margin] = (
@@ -541,19 +575,30 @@
         level_init, target, kernels[0], *(tables[name] for name in names)
     )
     tables = dict(zip(names, loaded))
-    strip_rows = (tile // margin + 1) * RIM
-    lift, send = call(
+    strips = tile // margin * RIM
+    packed = tables["packed"].shape[0]
+    own_lift, strip = call(
+        own_lift_kernel,
+        [((packed, tile), f32), ((strips, margin), bf16)],
+        level_init, tables["packed"],
+    )
+    (send,) = call(
         functools.partial(lift_kernel, counts),
-        [((2 * freqs, tile), bf16), ((2 * freqs + strip_rows, margin), bf16)],
-        level_init, rows_mine, rows_other, tables["fwd"],
+        [((packed + strips + RIM, margin), bf16)],
+        own_lift, strip, rows_mine, rows_other, tables["packed"],
     )
     cols_mine = along("tx", send)
     cols_other = across(cols_mine)
+    (mixed,) = call(
+        functools.partial(own_spec_kernel, counts),
+        [((2 * freqs, 2 * freqs), f32)],
+        own_lift, rows_mine, rows_other, tables["packed"], tables["expand"], tables["fwd_t"],
+    )
     resist, grad = call(
         functools.partial(corner_kernel, counts),
         [((tile, tile), f32), ((2 * freqs, freqs), f32)],
-        corner_doses, lift, cols_mine, cols_other, kernels, target,
-        tables["fwd_t"], tables["inv"], tables["inv_t"],
+        corner_doses, mixed, cols_mine, cols_other, kernels, target,
+        tables["expand"], tables["fwd_t"], tables["inv"], tables["inv_t"],
         smem=1,
         scratch=[
             pltpu.VMEM((2 * freqs, count * freqs), bf16),
@@ -568,10 +613,15 @@
     grad = (grad + across(grad)).astype(bf16)
     grad_mine = along("tx", grad)
     grad_other = across(grad_mine)
+    (own_grad,) = call(
+        own_grad_kernel,
+        [((2 * freqs, tile + margin), f32)],
+        grad, tables["fwd"], tables["rim_cols"],
+    )
     grad_lift, piece = call(
         functools.partial(lift_grad_kernel, counts),
-        [((2 * freqs, tile + margin), bf16), ((margin + RIM, tile + margin), bf16)],
-        grad, grad_mine, grad_other, tables["fwd"], tables["rim_cols"], tables["send_rows"],
+        [((2 * freqs, tile + margin), bf16), ((margin + PAD, tile + margin), bf16)],
+        own_grad, grad_mine, grad_other, tables["fwd"], tables["rim_cols"], tables["send_rows"],
     )
     piece_mine = along("ty", piece)
     piece_other = across(piece_mine)

time: 33.3 us -> 33 us (level)
  waiting for transfers between devices: 15.6 us -> 14.1 us
  Pallas kernels: 7.51 us -> 8.33 us
  starting transfers between devices: 8.58 us -> 8.93 us
    ppermute x5, waiting for transfers between devices: 3.74 us -> 2.69 us  [across(): return lax.ppermute(values, 'corner', [(0, 1), (1, 0)])]
    pallas_call x5 -> x8, Pallas kernels: 4.88 us -> 5.61 us  [call(): pl.pallas_call(kernel, out_shape=[jax.ShapeDtypeStruct(*item) for item in...]
    ppermute x4, waiting for transfers between devices: 11.8 us -> 11.4 us  [along(): return lax.ppermute(values, ('ty', 'tx', 'corner'), pairs)]
    ppermute x5, starting transfers between devices: 0.34 us -> 0.7 us  [across(): return lax.ppermute(values, 'corner', [(0, 1), (1, 0)])]
  transfers between devices with their start and end apart: 9 -> 9, of which waited for: 8 -> 7; matrix products, arithmetic and copies ran while one was open for 0% -> 0% of each run, Pallas kernels for 7% -> 10%
where the time goes in v5:
time: 33 us; the launch traced here: 32.8 us
  waiting for transfers between devices  14.1 us (43%)
  starting transfers between devices  8.93 us (27%)
  Pallas kernels  8.33 us (25%)
  between operations  1.37 us (4%)
    ppermute x4, waiting for transfers between devices, along(): return lax.ppermute(values, ('ty', 'tx', 'corner'), pairs)  11.4 us
    ppermute x4, starting transfers between devices, along(): return lax.ppermute(values, ('ty', 'tx', 'corner'), pairs)  8.23 us
    pallas_call x8, Pallas kernels, call(): pl.pallas_call(kernel, out_shape=[jax.ShapeDtypeStruct(*item) for item in...  5.61 us
    ppermute x5, waiting for transfers between devices, across(): return lax.ppermute(values, 'corner', [(0, 1), (1, 0)])  2.69 us
    pallas_call x1, Pallas kernels, load(): pl.pallas_call(load_kernel, out_shape=[jax.ShapeDtypeStruct(item.shape, i...  1.86 us
    pallas_call x1, Pallas kernels, step(): pl.pallas_call(edge_kernel, out_shape=jax.ShapeDtypeStruct((margin, tile)...  0.86 us
    ppermute x5, starting transfers between devices, across(): return lax.ppermute(values, 'corner', [(0, 1), (1, 0)])  0.7 us
  transfers between devices with their start and end apart: 9, of which 7 were waited for; matrix products, arithmetic and copies ran while one was open for 0% of the time, Pallas kernels for 10%

profile of v5, /device:TPU:0, one launch (start us, length us, event | category | flops | bytes accessed | tf_op | source)
XLA Modules:
  0.0 32.8 jit_solution(5404050706009481991)
XLA Ops:
  0.6 0.9 %edge.1 = bf16[128,256]{1,0:T(8,128)(2,1)S(1)} custom-call(s32[256,256]{1,0:T(8,128)} %level_ref.1), custom_call_target="tpu_custom_call" | custom-call | tf_op jit(solution)/shard_map/edge/pallas_call | solution.py:559
  1.5 3.0 %collective-permute-start = (bf16[128,256]{1,0:T(8,128)(2,1)S(1)}, bf16[128,256]{1,0:T(8,128)(2,1)S(1)}, u32[]{:S(2)}, u32[]{:S(2)}) collective-permute-start(bf16[128,256]{1,0:T(8,128)(2,1)S(1)} %edge.1), channel_id=1, source_target_pairs={{0,8},{8,0},{9,17},{17,9},{16,24},{24,16},{1,3},{3,1},{25,27},{27,... | collective-permute-start | bytes 196616 | tf_op jit(solution)/shard_map/ppermute | solution.py:534
  4.5 2.6 %collective-permute-done.mine_ref = bf16[128,256]{1,0:T(8,128)(2,1)S(1)} collective-permute-done((bf16[128,256]{1,0:T(8,128)(2,1)S(1)}, bf16[128,256]{1,0:T(8,128)(2,1)S(1)}, u32[]{:S(2)}, u32[]{:S(2)}) %collective-permute-start) | collective-permute-done | bytes 65568 | tf_op jit(solution)/shard_map/ppermute | solution.py:534
  7.1 0.0 collective-permute-start.1
  7.1 1.9 %load.1 = (s32[256,256]{1,0:T(8,128)S(1)}, s32[256,256]{1,0:T(8,128)S(1)}, f32[5,2,128,128]{3,2,1,0:T(8,128)S(1)}, bf16[256,144]{1,0:T(8,128)(2,1)S(1)}, bf16[25...) custom-call(s32[256,256]{1,0:T(8,128)} %level_ref.1, ...), custom_call_target="tpu_custom_call" | custom-call | bytes 8388608 | tf_op jit(solution)/shard_map/load/pallas_call | solution.py:489
  9.0 0.2 shard_map.140
  9.2 0.0 collective-permute-done.1.other_ref
  9.2 0.2 shard_map.142
  9.4 1.7 %collective-permute-start.2 = (bf16[192,128]{1,0:T(8,128)(2,1)S(1)}, bf16[192,128]{1,0:T(8,128)(2,1)S(1)}, u32[]{:S(2)}, u32[]{:S(2)}) collective-permute-start(bf16[192,128]{1,0:T(8,128)(2,1)S(1)} %shard_map.142), channel_id=1, source_target_pairs={{1,2},{2,1},{3,4},{4,3},{5,6},{6,5},{0,8},{8,0},{7,15},{15,7},{9,1... | collective-permute-start | bytes 147464 | tf_op jit(solution)/shard_map/ppermute | solution.py:534
  11.2 2.4 %collective-permute-done.2.mine_ref.cols_mine_ref = bf16[192,128]{1,0:T(8,128)(2,1)S(1)} collective-permute-done((bf16[192,128]{1,0:T(8,128)(2,1)S(1)}, bf16[192,128]{1,0:T(8,128)(2,1)S(1)}, u32[]{:S(2)}, u32[]{:S(2)}) %collective-permute-start.2) | collective-permute-done | bytes 49184 | tf_op jit(solution)/shard_map/ppermute | solution.py:534
  13.6 0.1 collective-permute-start.3
  14.4 0.5 %shard_map.141.mixed_ref = f32[256,256]{1,0:T(8,128)S(1)} custom-call(f32[144,256]{1,0:T(8,128)S(1)} %get-tuple-element.26.lift_ref, bf16[128,256]{1,0:T(8,128)(2,1)S(1)} %collective-permute-done.mine_ref, bf16[128,256]{1,0:T(8,128)(2,1)S(1)} %collective-permute-done.1.other_ref, bf16[144,512]{1,0:T(8,128)(2,1)S(1)} %get-tuple-element.25.packed_ref, ...), custom_call_target="tpu_custom_call" | custom-call | tf_op jit(solution)/shard_map/pallas_call | solution.py:504
  14.9 0.0 collective-permute-done.3.other_ref.cols_other_ref
  14.9 2.2 %shard_map.143 = (f32[256,256]{1,0:T(8,128)}, f32[256,128]{1,0:T(8,128)S(1)}) custom-call(f32[1]{0:T(128)S(6)} %copy.15.dose_ref, f32[256,256]{1,0:T(8,128)S(1)} %shard_map.141.mixed_ref, bf16[192,128]{1,0:T(8,128)(2,1)S(1)} %collective-permute-done.2.mine_ref.cols_mine_ref, bf16[192,128]{1,0:T(8,128)(2,1)S(1)} %collective-permute-done.3.other_ref.cols_other_ref, ...), custom_call_target="tpu_custom_call" | custom-call | tf_op jit(solution)/shard_map/pallas_call | solution.py:504
  17.1 0.5 %collective-permute-start.4 = (f32[256,128]{1,0:T(8,128)S(1)}, f32[256,128]{1,0:T(8,128)S(1)}, u32[]{:S(2)}, u32[]{:S(2)}) collective-permute-start(f32[256,128]{1,0:T(8,128)S(1)} %get-tuple-element.35), channel_id=1, source_target_pairs={{0,1},{1,0},{2,3},{3,2},{4,5},{5,4},{6,7},{7,6},{8,9},{9,8},{10,11... | collective-permute-start | bytes 393224 | tf_op jit(solution)/shard_map/ppermute | solution.py:548
  17.5 1.0 %collective-permute-done.4 = f32[256,128]{1,0:T(8,128)S(1)} collective-permute-done((f32[256,128]{1,0:T(8,128)S(1)}, f32[256,128]{1,0:T(8,128)S(1)}, u32[]{:S(2)}, u32[]{:S(2)}) %collective-permute-start.4) | collective-permute-done | bytes 131104 | tf_op jit(solution)/shard_map/ppermute | solution.py:548
  18.6 1.7 %collective-permute-start.5 = (bf16[256,128]{1,0:T(8,128)(2,1)S(1)}, bf16[256,128]{1,0:T(8,128)(2,1)S(1)}, u32[]{:S(2)}, u32[]{:S(2)}) collective-permute-start(bf16[256,128]{1,0:T(8,128)(2,1)S(1)} %add_convert_fusion.grad_ref), channel_id=1, source_target_pairs={{1,2},{2,1},{3,4},{4,3},{5,6},{6,5},{0,8},{8,0},{7,15},{15,7},{9,1... | collective-permute-start | bytes 196616 | tf_op jit(solution)/shard_map/ppermute | solution.py:534
  20.3 2.6 %collective-permute-done.5.mine_ref = bf16[256,128]{1,0:T(8,128)(2,1)S(1)} collective-permute-done((bf16[256,128]{1,0:T(8,128)(2,1)S(1)}, bf16[256,128]{1,0:T(8,128)(2,1)S(1)}, u32[]{:S(2)}, u32[]{:S(2)}) %collective-permute-start.5) | collective-permute-done | bytes 65568 | tf_op jit(solution)/shard_map/ppermute | solution.py:534
  22.9 0.1 collective-permute-start.6
  23.0 0.2 shard_map.144.own_ref
  23.2 0.9 %collective-permute-done.6.other_ref = bf16[256,128]{1,0:T(8,128)(2,1)S(1)} collective-permute-done((bf16[256,128]{1,0:T(8,128)(2,1)S(1)}, bf16[256,128]{1,0:T(8,128)(2,1)S(1)}, u32[]{:S(2)}, u32[]{:S(2)}) %collective-permute-start.6) | collective-permute-done | bytes 65568 | tf_op jit(solution)/shard_map/ppermute | solution.py:548
  24.1 0.5 %shard_map.145 = (bf16[256,384]{1,0:T(8,128)(2,1)S(1)}, bf16[136,384]{1,0:T(8,128)(2,1)S(1)}) custom-call(f32[256,384]{1,0:T(8,128)S(1)} %shard_map.144.own_ref, bf16[256,128]{1,0:T(8,128)(2,1)S(1)} %collective-permute-done.5.mine_ref, bf16[256,128]{1,0:T(8,128)(2,1)S(1)} %collective-permute-done.6.other_ref, ...), custom_call_target="tpu_custom_call" | custom-call | tf_op jit(solution)/shard_map/pallas_call | solution.py:504
  24.6 1.7 %collective-permute-start.7 = (bf16[136,384]{1,0:T(8,128)(2,1)S(1)}, bf16[136,384]{1,0:T(8,128)(2,1)S(1)}, u32[]{:S(2)}, u32[]{:S(2)}) collective-permute-start(bf16[136,384]{1,0:T(8,128)(2,1)S(1)} %get-tuple-element.42), channel_id=1, source_target_pairs={{0,8},{8,0},{9,17},{17,9},{16,24},{24,16},{1,3},{3,1},{25,27},{27,... | collective-permute-start | bytes 313352 | tf_op jit(solution)/shard_map/ppermute | solution.py:534
  26.4 3.8 %collective-permute-done.7.mine_ref = bf16[136,384]{1,0:T(8,128)(2,1)S(1)} collective-permute-done((bf16[136,384]{1,0:T(8,128)(2,1)S(1)}, bf16[136,384]{1,0:T(8,128)(2,1)S(1)}, u32[]{:S(2)}, u32[]{:S(2)}) %collective-permute-start.7) | collective-permute-done | bytes 104480 | tf_op jit(solution)/shard_map/ppermute | solution.py:534
  30.2 0.0 collective-permute-start.8
  30.2 0.5 %shard_map.146 = (f32[272,384]{1,0:T(8,128)S(1)}, f32[272,384]{1,0:T(8,128)S(1)}, f32[272,384]{1,0:T(8,128)S(1)}, f32[272,384]{1,0:T(8,128)S(1)}) custom-call(bf16[256,384]{1,0:T(8,128)(2,1)S(1)} %get-tuple-element.39.lift_ref, bf16[272,256]{1,0:T(8,128)(2,1)S(1)} %get-tuple-element.40.own_rows_ref, s32[256,256]{1,0:T(8,128)S(1)} %get-tuple-element.24.level_ref, ...), custom_call_target="tpu_custom_call" | custom-call | tf_op jit(solution)/shard_map/pallas_call | solution.py:504
  30.7 0.8 %collective-permute-done.8.other_ref = bf16[136,384]{1,0:T(8,128)(2,1)S(1)} collective-permute-done((bf16[136,384]{1,0:T(8,128)(2,1)S(1)}, bf16[136,384]{1,0:T(8,128)(2,1)S(1)}, u32[]{:S(2)}, u32[]{:S(2)}) %collective-permute-start.8) | collective-permute-done | bytes 104480 | tf_op jit(solution)/shard_map/ppermute | solution.py:548
  31.5 1.3 %shard_map.147 = f32[256,256]{1,0:T(8,128)} custom-call(f32[272,384]{1,0:T(8,128)S(1)} %get-tuple-element.41.grad_ref, bf16[136,384]{1,0:T(8,128)(2,1)S(1)} %collective-permute-done.7.mine_ref, bf16[136,384]{1,0:T(8,128)(2,1)S(1)} %collective-permute-done.8.other_ref, f32[272,384]{1,0:T(8,128)S(1)} %get-tuple-element.43.slope_ref, ...), custom_call_target="tpu_custom_call" | custom-call | tf_op jit(solution)/shard_map/pallas_call | solution.py:504
  (1 shorter events, 0.0 us)
Async XLA Ops:
  1.5 5.6 %collective-permute-start = (bf16[128,256]{1,0:T(8,128)(2,1)S(1)}, bf16[128,256]{1,0:T(8,128)(2,1)S(1)}, u32[]{:S(2)}, u32[]{:S(2)}) collective-permute-start(bf16[128,256]{1,0:T(8,128)(2,1)S(1)} %edge.1), channel_id=1, source_target_pairs={{0,8},{8,0},{9,17},{17,9},{16,24},{24,16},{1,3},{3,1},{25,27},{27,... | collective-permute-start | bytes 196616 | tf_op jit(solution)/shard_map/ppermute | solution.py:534
  7.1 2.1 %collective-permute-start.1 = (bf16[128,256]{1,0:T(8,128)(2,1)S(1)}, bf16[128,256]{1,0:T(8,128)(2,1)S(1)}, u32[]{:S(2)}, u32[]{:S(2)}) collective-permute-start(bf16[128,256]{1,0:T(8,128)(2,1)S(1)} %collective-permute-done.mine_ref), channel_id=1, source_target_pairs={{0,1},{1,0},{2,3},{3,2},{4,5},{5,4},{6,7},{7,6},{8,9},{9,8},{10,11... | collective-permute-start | bytes 196616 | tf_op jit(solution)/shard_map/ppermute | solution.py:548
  9.4 4.2 %collective-permute-start.2 = (bf16[192,128]{1,0:T(8,128)(2,1)S(1)}, bf16[192,128]{1,0:T(8,128)(2,1)S(1)}, u32[]{:S(2)}, u32[]{:S(2)}) collective-permute-start(bf16[192,128]{1,0:T(8,128)(2,1)S(1)} %shard_map.142), channel_id=1, source_target_pairs={{1,2},{2,1},{3,4},{4,3},{5,6},{6,5},{0,8},{8,0},{7,15},{15,7},{9,1... | collective-permute-start | bytes 147464 | tf_op jit(solution)/shard_map/ppermute | solution.py:534
  13.6 1.3 %collective-permute-start.3 = (bf16[192,128]{1,0:T(8,128)(2,1)S(1)}, bf16[192,128]{1,0:T(8,128)(2,1)S(1)}, u32[]{:S(2)}, u32[]{:S(2)}) collective-permute-start(bf16[192,128]{1,0:T(8,128)(2,1)S(1)} %collective-permute-done.2.mine_ref.cols_mine_ref), channel_id=1, source_target_pairs={{0,1},{1,0},{2,3},{3,2},{4,5},{5,4},{6,7},{7,6},{8,9},{9,8},{10,11... | collective-permute-start | bytes 147464 | tf_op jit(solution)/shard_map/ppermute | solution.py:548
  17.1 1.5 %collective-permute-start.4 = (f32[256,128]{1,0:T(8,128)S(1)}, f32[256,128]{1,0:T(8,128)S(1)}, u32[]{:S(2)}, u32[]{:S(2)}) collective-permute-start(f32[256,128]{1,0:T(8,128)S(1)} %get-tuple-element.35), channel_id=1, source_target_pairs={{0,1},{1,0},{2,3},{3,2},{4,5},{5,4},{6,7},{7,6},{8,9},{9,8},{10,11... | collective-permute-start | bytes 393224 | tf_op jit(solution)/shard_map/ppermute | solution.py:548
  18.6 4.3 %collective-permute-start.5 = (bf16[256,128]{1,0:T(8,128)(2,1)S(1)}, bf16[256,128]{1,0:T(8,128)(2,1)S(1)}, u32[]{:S(2)}, u32[]{:S(2)}) collective-permute-start(bf16[256,128]{1,0:T(8,128)(2,1)S(1)} %add_convert_fusion.grad_ref), channel_id=1, source_target_pairs={{1,2},{2,1},{3,4},{4,3},{5,6},{6,5},{0,8},{8,0},{7,15},{15,7},{9,1... | collective-permute-start | bytes 196616 | tf_op jit(solution)/shard_map/ppermute | solution.py:534
  22.9 1.3 %collective-permute-start.6 = (bf16[256,128]{1,0:T(8,128)(2,1)S(1)}, bf16[256,128]{1,0:T(8,128)(2,1)S(1)}, u32[]{:S(2)}, u32[]{:S(2)}) collective-permute-start(bf16[256,128]{1,0:T(8,128)(2,1)S(1)} %collective-permute-done.5.mine_ref), channel_id=1, source_target_pairs={{0,1},{1,0},{2,3},{3,2},{4,5},{5,4},{6,7},{7,6},{8,9},{9,8},{10,11... | collective-permute-start | bytes 196616 | tf_op jit(solution)/shard_map/ppermute | solution.py:548
  24.6 5.5 %collective-permute-start.7 = (bf16[136,384]{1,0:T(8,128)(2,1)S(1)}, bf16[136,384]{1,0:T(8,128)(2,1)S(1)}, u32[]{:S(2)}, u32[]{:S(2)}) collective-permute-start(bf16[136,384]{1,0:T(8,128)(2,1)S(1)} %get-tuple-element.42), channel_id=1, source_target_pairs={{0,8},{8,0},{9,17},{17,9},{16,24},{24,16},{1,3},{3,1},{25,27},{27,... | collective-permute-start | bytes 313352 | tf_op jit(solution)/shard_map/ppermute | solution.py:534
  30.2 1.3 %collective-permute-start.8 = (bf16[136,384]{1,0:T(8,128)(2,1)S(1)}, bf16[136,384]{1,0:T(8,128)(2,1)S(1)}, u32[]{:S(2)}, u32[]{:S(2)}) collective-permute-start(bf16[136,384]{1,0:T(8,128)(2,1)S(1)} %collective-permute-done.7.mine_ref), channel_id=1, source_target_pairs={{0,1},{1,0},{2,3},{3,2},{4,5},{5,4},{6,7},{7,6},{8,9},{9,8},{10,11... | collective-permute-start | bytes 313352 | tf_op jit(solution)/shard_map/ppermute | solution.py:548

commit v6 on v5

--- a/solution.py
+++ b/solution.py
@@ -50,11 +50,12 @@
     offsets = (margin + tile, margin, margin - tile)
     rim_cols = np.stack([rim(margin, offset) for offset in offsets])
     rim_rows = [rim(RIM, offset).T for offset in offsets]
-    own_rows = np.concatenate([stacked[:, margin : margin + tile].T, rim_rows[1]])
+    own_rows = stacked[:, margin : margin + tile].T
+    own_rows = np.concatenate([rim_rows[1][PAD:], own_rows, rim_rows[1][:PAD]])
     send_rows = np.stack(
         [
             np.concatenate([stacked[:, :margin].T, rim_rows[2][:PAD]]),
-            np.concatenate([stacked[:, tile + margin :].T, rim_rows[0][PAD:]]),
+            np.concatenate([rim_rows[0][PAD:], stacked[:, tile + margin :].T]),
         ]
     )
     half = freqs // 2
@@ -319,29 +320,6 @@
     lift_ref[:, tile - margin : tile] = last.astype(jnp.bfloat16)
     lift_ref[:, tile:] = rim.astype(jnp.bfloat16)
     send_ref[...] = dot(send_rows_ref[to_after], lift_ref[...]).astype(jnp.bfloat16)
-
-
-def grid_masks(counts, margin):
-    lane = lax.broadcasted_iota(jnp.int32, (PAD, margin), 1)
-    at_ty, at_tx = lax.axis_index("ty"), lax.axis_index("tx")
-    every = lane >= 0
-    above = every & (at_ty > 0)
-    below = every & (at_ty < counts["ty"] - 1)
-    beside = ((lane >= margin // 2) & (at_tx > 0)) | (
-        (lane < margin // 2) & (at_tx < counts["tx"] - 1)
-    )
-    return above, below, beside
-
-
-def within(keeps, rows, blocks, at, block, level):
-    above, below, beside = keeps
-    if at == 0:
-        level = jnp.where(above, level, 0.0)
-    if at == rows - PAD:
-        level = jnp.where(below, level, 0.0)
-    if block == blocks - 1:
-        level = jnp.where(beside, level, 0.0)
-    return level
 
 
 def stencil(source, at, wanted, margin):
@@ -411,64 +389,107 @@
             slope_ref[at : at + PAD, lanes] = (SPEED_GAIN * 0.5 * 0.25) * (1.0 - trans * trans)
 
 
-def advance_kernel(
-    counts, grad_ref, mine_ref, other_ref, slope_ref, base_ref, root_ref, out_ref,
+def half_of_piece():
+    return lax.rem(lax.axis_index("corner") + lax.axis_index("ty") + 1, 2)
+
+
+def valid_piece(counts, half, piece):
+    at_ty = lax.axis_index("ty")
+    inside = jnp.where(half == 0, at_ty, counts["ty"] - 1 - at_ty) > 0
+    return jnp.where(inside, piece, jnp.zeros_like(piece)).astype(jnp.float32)
+
+
+def advance_rows(counts, start, size, speed_ref, base_ref, root_ref, level_refs, store):
+    rows, cols = base_ref.shape
+    blocks = len(level_refs) // 2
+    margin = cols // blocks
+    lane = lax.broadcasted_iota(jnp.int32, (PAD, margin), 1)
+    at_ty, at_tx = lax.axis_index("ty"), lax.axis_index("tx")
+    every = lane >= 0
+    above = every & (at_ty + start > 0)
+    below = every & (counts["ty"] - 1 - at_ty + (rows - size - start) > 0)
+    beside = ((lane >= margin // 2) & (at_tx > 0)) | (
+        (lane < margin // 2) & (at_tx < counts["tx"] - 1)
+    )
+    for ref in level_refs:
+        ref[:PAD] = jnp.zeros((PAD, margin), jnp.float32)
+        ref[PAD + size : 2 * PAD + size] = jnp.zeros((PAD, margin), jnp.float32)
+    source, target = level_refs[:blocks], level_refs[blocks:]
+    for step in range(LS_STEPS):
+        final = step == LS_STEPS - 1
+        for at in range(PAD if final else 0, size - PAD if final else size, PAD):
+            here = pl.ds(pl.multiple_of(start + at, PAD), PAD)
+            lanes = [slice(block * margin, (block + 1) * margin) for block in range(blocks)]
+            if step == 0:
+                parts = [(base_ref[here, cut], root_ref[here, cut]) for cut in lanes]
+            else:
+                parts = stencil(source, at, blocks - 1 if final else blocks, margin)
+            for block, (base, root) in enumerate(parts):
+                level = base - speed_ref[at : at + PAD, lanes[block]] * root
+                if final:
+                    store(at, lanes[block], 2.0 * level)
+                    continue
+                if at == 0:
+                    level = jnp.where(above, level, 0.0)
+                if at == size - PAD:
+                    level = jnp.where(below, level, 0.0)
+                if block == blocks - 1:
+                    level = jnp.where(beside, level, 0.0)
+                target[block][PAD + at : 2 * PAD + at] = level
+        source, target = target, source
+
+
+def advance_mine_kernel(
+    counts, grad_ref, mine_ref, slope_ref, base_ref, root_ref, speed_ref, done_ref, *level_refs
+):
+    half = half_of_piece()
+    size = mine_ref.shape[0]
+    start = half * (grad_ref.shape[0] - size)
+    here = pl.ds(pl.multiple_of(start, PAD), size)
+    piece = valid_piece(counts, half, mine_ref[...])
+    speed_ref[...] = (grad_ref[here, :] + piece) * slope_ref[here, :]
+
+    def store(at, lanes, level):
+        done_ref[at - PAD : at, lanes] = level
+
+    advance_rows(counts, start, size, speed_ref, base_ref, root_ref, level_refs, store)
+
+
+def advance_rest_kernel(
+    counts, grad_ref, other_ref, slope_ref, base_ref, root_ref, mine_speed_ref, mine_ref, out_ref,
     speed_ref, done_ref, sems, *level_refs,
 ):
-    rows, cols = slope_ref.shape
-    tile = out_ref.shape[0]
-    margin = cols - tile
-    blocks = cols // margin
-    first, last = level_refs[:blocks], level_refs[blocks:]
-    keeps = grid_masks(counts, margin)
-    before, after = ordered("ty", counts, mine_ref[...], other_ref[...])
-    before = before.astype(jnp.float32)
-    after = after.astype(jnp.float32)
-    speed_ref[:PAD] = (before[margin:] + grad_ref[tile + PAD :]) * slope_ref[:PAD]
-    speed_ref[PAD + tile :] = (after[margin:] + grad_ref[tile : tile + PAD]) * slope_ref[PAD + tile :]
-    for half, part in ((0, before), (1, after)):
-        at = half * margin
-        speed_ref[PAD + at : PAD + at + margin] = (
-            grad_ref[at : at + margin] + part[:margin]
-        ) * slope_ref[PAD + at : PAD + at + margin]
-    for ref in level_refs:
-        ref[:PAD] = jnp.zeros((PAD, margin), jnp.float32)
-        ref[PAD + rows :] = jnp.zeros((PAD, margin), jnp.float32)
-
-    def store(target, at, block, level):
-        level = within(keeps, rows, blocks, at, block, level)
-        target[block][PAD + at : 2 * PAD + at] = level
-
-    for at in range(0, rows, PAD):
-        for block in range(blocks):
-            lanes = slice(block * margin, (block + 1) * margin)
-            level = (
-                base_ref[at : at + PAD, lanes]
-                - speed_ref[at : at + PAD, lanes] * root_ref[at : at + PAD, lanes]
-            )
-            store(first, at, block, level)
-    source, target = first, last
-    copies = []
-    for step in range(1, LS_STEPS):
-        final = step == LS_STEPS - 1
-        for at in range(PAD if final else 0, rows - PAD if final else rows, PAD):
-            parts = list(stencil(source, at, blocks - 1 if final else blocks, margin))
-            for block, (base, root) in enumerate(parts):
-                lanes = slice(block * margin, (block + 1) * margin)
-                level = base - speed_ref[at : at + PAD, lanes] * root
-                if final:
-                    done_ref[at - PAD : at, lanes] = 2.0 * level
-                else:
-                    store(target, at, block, level)
-            chunk = tile // CHUNKS
-            if final and at % chunk == 0:
-                piece = slice(at - chunk, at)
-                copy = pltpu.make_async_copy(
-                    done_ref.at[piece, :], out_ref.at[piece, :], sems.at[at // chunk - 1]
-                )
-                copy.start()
-                copies.append(copy)
-        source, target = target, source
+    half = half_of_piece()
+    size = other_ref.shape[0]
+    rows = mine_ref.shape[0]
+    rest = out_ref.shape[0] - rows
+    place = pl.ds(pl.multiple_of(half * rest, PAD), rows)
+    copies = [pltpu.make_async_copy(mine_ref, out_ref.at[place, :], sems.at[0])]
+    copies[0].start()
+    here = pl.ds(pl.multiple_of((1 - half) * (grad_ref.shape[0] - size), PAD), size)
+    piece = valid_piece(counts, 1 - half, other_ref[...])
+    target = pl.ds(pl.multiple_of((1 - half) * 2 * PAD, PAD), size)
+    speed_ref[target, :] = (grad_ref[here, :] + piece) * slope_ref[here, :]
+    source = pl.ds(pl.multiple_of((1 - half) * (size - 2 * PAD), PAD), 2 * PAD)
+    target = pl.ds(pl.multiple_of(half * size, PAD), 2 * PAD)
+    speed_ref[target, :] = mine_speed_ref[source, :]
+    first = (1 - half) * rows
+
+    def store(at, lanes, level):
+        done_ref[at - PAD : at, lanes] = level
+        chunk = rest // CHUNKS // PAD * PAD
+        if lanes.start == 0 or (at % chunk and at != rest):
+            return
+        begin = (at - 1) // chunk * chunk
+        target = pl.ds(pl.multiple_of(first + begin, PAD), at - begin)
+        copy = pltpu.make_async_copy(
+            done_ref.at[begin:at, :], out_ref.at[target, :], sems.at[len(copies)]
+        )
+        copy.start()
+        copies.append(copy)
+
+    start = (1 - half) * (grad_ref.shape[0] - size - 2 * PAD)
+    advance_rows(counts, start, size + 2 * PAD, speed_ref, base_ref, root_ref, level_refs, store)
     for copy in copies:
         copy.wait()
 
@@ -633,17 +654,31 @@
         grad_lift, tables["own_rows"], level_init, rows_mine, rows_other, cols_mine, cols_other,
         scratch=levels,
     )
+    own_piece, frame = frame[0], frame[1:]
+    mine_rows = margin + PAD
+    done_rows = mine_rows - 2 * PAD
+    rest_rows = mine_rows + 2 * PAD
+
+    def levels_of(size):
+        return [pltpu.VMEM((size + 2 * PAD, margin), f32)] * (2 * framed[1] // margin)
+
+    mine_speed, mine_done = call(
+        functools.partial(advance_mine_kernel, counts),
+        [((mine_rows, framed[1]), f32), ((done_rows, tile), f32)],
+        own_piece, piece_mine, *frame,
+        scratch=levels_of(mine_rows),
+    )
     (level,) = call(
-        functools.partial(advance_kernel, counts),
+        functools.partial(advance_rest_kernel, counts),
         [((tile, tile), f32)],
-        frame[0], piece_mine, piece_other, *frame[1:],
+        own_piece, piece_other, *frame, mine_speed, mine_done,
         out_space=(pltpu.HBM,),
         scratch=[
-            pltpu.VMEM(framed, f32),
-            pltpu.VMEM((tile, tile), f32),
-            pltpu.SemaphoreType.DMA((CHUNKS,)),
+            pltpu.VMEM((rest_rows, framed[1]), f32),
+            pltpu.VMEM((tile - done_rows, tile), f32),
+            pltpu.SemaphoreType.DMA((CHUNKS + 2,)),
         ]
-        + levels * 2,
+        + levels_of(rest_rows),
     )
     return (resist[None], level)
 

time: 33 us -> 32.7 us (level)
    ppermute x5, waiting for transfers between devices: 2.69 us -> 2.34 us  [across(): return lax.ppermute(values, 'corner', [(0, 1), (1, 0)])]
    pallas_call x8 -> x9, Pallas kernels: 5.61 us -> 5.69 us  [call(): pl.pallas_call(kernel, out_shape=[jax.ShapeDtypeStruct(*item) for item in...]
  transfers between devices with their start and end apart: 9 -> 9, of which waited for: 7 -> 7; matrix products, arithmetic and copies ran while one was open for 0% -> 0% of each run, Pallas kernels for 10% -> 11%
where the time goes in v6:
time: 32.7 us; the launch traced here: 32.5 us
  waiting for transfers between devices  13.8 us (42%)
  starting transfers between devices  8.92 us (27%)
  Pallas kernels  8.41 us (26%)
  between operations  1.37 us (4%)
    ppermute x4, waiting for transfers between devices, along(): return lax.ppermute(values, ('ty', 'tx', 'corner'), pairs)  11.4 us
    ppermute x4, starting transfers between devices, along(): return lax.ppermute(values, ('ty', 'tx', 'corner'), pairs)  8.23 us
    pallas_call x9, Pallas kernels, call(): pl.pallas_call(kernel, out_shape=[jax.ShapeDtypeStruct(*item) for item in...  5.69 us
    ppermute x5, waiting for transfers between devices, across(): return lax.ppermute(values, 'corner', [(0, 1), (1, 0)])  2.34 us
    pallas_call x1, Pallas kernels, load(): pl.pallas_call(load_kernel, out_shape=[jax.ShapeDtypeStruct(item.shape, i...  1.86 us
    pallas_call x1, Pallas kernels, step(): pl.pallas_call(edge_kernel, out_shape=jax.ShapeDtypeStruct((margin, tile)...  0.86 us
    ppermute x5, starting transfers between devices, across(): return lax.ppermute(values, 'corner', [(0, 1), (1, 0)])  0.69 us
  transfers between devices with their start and end apart: 9, of which 7 were waited for; matrix products, arithmetic and copies ran while one was open for 0% of the time, Pallas kernels for 11%

profile of v6, /device:TPU:0, one launch (start us, length us, event | category | flops | bytes accessed | tf_op | source)
XLA Modules:
  0.0 32.5 jit_solution(2495259574651872189)
XLA Ops:
  0.6 0.9 %edge.1 = bf16[128,256]{1,0:T(8,128)(2,1)S(1)} custom-call(s32[256,256]{1,0:T(8,128)} %level_ref.1), custom_call_target="tpu_custom_call" | custom-call | tf_op jit(solution)/shard_map/edge/pallas_call | solution.py:580
  1.5 3.0 %collective-permute-start = (bf16[128,256]{1,0:T(8,128)(2,1)S(1)}, bf16[128,256]{1,0:T(8,128)(2,1)S(1)}, u32[]{:S(2)}, u32[]{:S(2)}) collective-permute-start(bf16[128,256]{1,0:T(8,128)(2,1)S(1)} %edge.1), channel_id=1, source_target_pairs={{0,8},{8,0},{9,17},{17,9},{16,24},{24,16},{1,3},{3,1},{25,27},{27,... | collective-permute-start | bytes 196616 | tf_op jit(solution)/shard_map/ppermute | solution.py:555
  4.5 2.6 %collective-permute-done.mine_ref = bf16[128,256]{1,0:T(8,128)(2,1)S(1)} collective-permute-done((bf16[128,256]{1,0:T(8,128)(2,1)S(1)}, bf16[128,256]{1,0:T(8,128)(2,1)S(1)}, u32[]{:S(2)}, u32[]{:S(2)}) %collective-permute-start) | collective-permute-done | bytes 65568 | tf_op jit(solution)/shard_map/ppermute | solution.py:555
  7.1 0.0 collective-permute-start.1
  7.1 1.9 %load.1 = (s32[256,256]{1,0:T(8,128)S(1)}, s32[256,256]{1,0:T(8,128)S(1)}, f32[5,2,128,128]{3,2,1,0:T(8,128)S(1)}, bf16[256,144]{1,0:T(8,128)(2,1)S(1)}, bf16[25...) custom-call(s32[256,256]{1,0:T(8,128)} %level_ref.1, ...), custom_call_target="tpu_custom_call" | custom-call | bytes 8388608 | tf_op jit(solution)/shard_map/load/pallas_call | solution.py:510
  9.0 0.2 shard_map.140
  9.2 0.0 collective-permute-done.1.other_ref
  9.2 0.2 shard_map.142
  9.4 1.7 %collective-permute-start.2 = (bf16[192,128]{1,0:T(8,128)(2,1)S(1)}, bf16[192,128]{1,0:T(8,128)(2,1)S(1)}, u32[]{:S(2)}, u32[]{:S(2)}) collective-permute-start(bf16[192,128]{1,0:T(8,128)(2,1)S(1)} %shard_map.142), channel_id=1, source_target_pairs={{1,2},{2,1},{3,4},{4,3},{5,6},{6,5},{0,8},{8,0},{7,15},{15,7},{9,1... | collective-permute-start | bytes 147464 | tf_op jit(solution)/shard_map/ppermute | solution.py:555
  11.2 2.4 %collective-permute-done.2.mine_ref.cols_mine_ref = bf16[192,128]{1,0:T(8,128)(2,1)S(1)} collective-permute-done((bf16[192,128]{1,0:T(8,128)(2,1)S(1)}, bf16[192,128]{1,0:T(8,128)(2,1)S(1)}, u32[]{:S(2)}, u32[]{:S(2)}) %collective-permute-start.2) | collective-permute-done | bytes 49184 | tf_op jit(solution)/shard_map/ppermute | solution.py:555
  13.6 0.1 collective-permute-start.3
  14.4 0.5 %shard_map.141.mixed_ref = f32[256,256]{1,0:T(8,128)S(1)} custom-call(f32[144,256]{1,0:T(8,128)S(1)} %get-tuple-element.28.lift_ref, bf16[128,256]{1,0:T(8,128)(2,1)S(1)} %collective-permute-done.mine_ref, bf16[128,256]{1,0:T(8,128)(2,1)S(1)} %collective-permute-done.1.other_ref, bf16[144,512]{1,0:T(8,128)(2,1)S(1)} %get-tuple-element.27.packed_ref, ...), custom_call_target="tpu_custom_call" | custom-call | tf_op jit(solution)/shard_map/pallas_call | solution.py:525
  14.9 0.0 collective-permute-done.3.other_ref.cols_other_ref
  14.9 2.2 %shard_map.143 = (f32[256,256]{1,0:T(8,128)}, f32[256,128]{1,0:T(8,128)S(1)}) custom-call(f32[1]{0:T(128)S(6)} %copy.15.dose_ref, f32[256,256]{1,0:T(8,128)S(1)} %shard_map.141.mixed_ref, bf16[192,128]{1,0:T(8,128)(2,1)S(1)} %collective-permute-done.2.mine_ref.cols_mine_ref, bf16[192,128]{1,0:T(8,128)(2,1)S(1)} %collective-permute-done.3.other_ref.cols_other_ref, ...), custom_call_target="tpu_custom_call" | custom-call | tf_op jit(solution)/shard_map/pallas_call | solution.py:525
  17.1 0.5 %collective-permute-start.4 = (f32[256,128]{1,0:T(8,128)S(1)}, f32[256,128]{1,0:T(8,128)S(1)}, u32[]{:S(2)}, u32[]{:S(2)}) collective-permute-start(f32[256,128]{1,0:T(8,128)S(1)} %get-tuple-element.37), channel_id=1, source_target_pairs={{0,1},{1,0},{2,3},{3,2},{4,5},{5,4},{6,7},{7,6},{8,9},{9,8},{10,11... | collective-permute-start | bytes 393224 | tf_op jit(solution)/shard_map/ppermute | solution.py:569
  17.5 1.0 %collective-permute-done.4 = f32[256,128]{1,0:T(8,128)S(1)} collective-permute-done((f32[256,128]{1,0:T(8,128)S(1)}, f32[256,128]{1,0:T(8,128)S(1)}, u32[]{:S(2)}, u32[]{:S(2)}) %collective-permute-start.4) | collective-permute-done | bytes 131104 | tf_op jit(solution)/shard_map/ppermute | solution.py:569
  18.5 1.7 %collective-permute-start.5 = (bf16[256,128]{1,0:T(8,128)(2,1)S(1)}, bf16[256,128]{1,0:T(8,128)(2,1)S(1)}, u32[]{:S(2)}, u32[]{:S(2)}) collective-permute-start(bf16[256,128]{1,0:T(8,128)(2,1)S(1)} %add_convert_fusion.grad_ref), channel_id=1, source_target_pairs={{1,2},{2,1},{3,4},{4,3},{5,6},{6,5},{0,8},{8,0},{7,15},{15,7},{9,1... | collective-permute-start | bytes 196616 | tf_op jit(solution)/shard_map/ppermute | solution.py:555
  20.3 2.6 %collective-permute-done.5.mine_ref = bf16[256,128]{1,0:T(8,128)(2,1)S(1)} collective-permute-done((bf16[256,128]{1,0:T(8,128)(2,1)S(1)}, bf16[256,128]{1,0:T(8,128)(2,1)S(1)}, u32[]{:S(2)}, u32[]{:S(2)}) %collective-permute-start.5) | collective-permute-done | bytes 65568 | tf_op jit(solution)/shard_map/ppermute | solution.py:555
  22.9 0.1 collective-permute-start.6
  23.0 0.2 shard_map.144.own_ref
  23.2 0.9 %collective-permute-done.6.other_ref = bf16[256,128]{1,0:T(8,128)(2,1)S(1)} collective-permute-done((bf16[256,128]{1,0:T(8,128)(2,1)S(1)}, bf16[256,128]{1,0:T(8,128)(2,1)S(1)}, u32[]{:S(2)}, u32[]{:S(2)}) %collective-permute-start.6) | collective-permute-done | bytes 65568 | tf_op jit(solution)/shard_map/ppermute | solution.py:569
  24.1 0.5 %shard_map.145 = (bf16[256,384]{1,0:T(8,128)(2,1)S(1)}, bf16[136,384]{1,0:T(8,128)(2,1)S(1)}) custom-call(f32[256,384]{1,0:T(8,128)S(1)} %shard_map.144.own_ref, bf16[256,128]{1,0:T(8,128)(2,1)S(1)} %collective-permute-done.5.mine_ref, bf16[256,128]{1,0:T(8,128)(2,1)S(1)} %collective-permute-done.6.other_ref, ...), custom_call_target="tpu_custom_call" | custom-call | tf_op jit(solution)/shard_map/pallas_call | solution.py:525
  24.6 1.7 %collective-permute-start.7 = (bf16[136,384]{1,0:T(8,128)(2,1)S(1)}, bf16[136,384]{1,0:T(8,128)(2,1)S(1)}, u32[]{:S(2)}, u32[]{:S(2)}) collective-permute-start(bf16[136,384]{1,0:T(8,128)(2,1)S(1)} %get-tuple-element.44), channel_id=1, source_target_pairs={{0,8},{8,0},{9,17},{17,9},{16,24},{24,16},{1,3},{3,1},{25,27},{27,... | collective-permute-start | bytes 313352 | tf_op jit(solution)/shard_map/ppermute | solution.py:555
  26.3 3.8 %collective-permute-done.7.mine_ref = bf16[136,384]{1,0:T(8,128)(2,1)S(1)} collective-permute-done((bf16[136,384]{1,0:T(8,128)(2,1)S(1)}, bf16[136,384]{1,0:T(8,128)(2,1)S(1)}, u32[]{:S(2)}, u32[]{:S(2)}) %collective-permute-start.7) | collective-permute-done | bytes 104480 | tf_op jit(solution)/shard_map/ppermute | solution.py:555
  30.2 0.0 collective-permute-start.8
  30.2 0.5 %shard_map.146 = (f32[272,384]{1,0:T(8,128)S(1)}, f32[272,384]{1,0:T(8,128)S(1)}, f32[272,384]{1,0:T(8,128)S(1)}, f32[272,384]{1,0:T(8,128)S(1)}) custom-call(bf16[256,384]{1,0:T(8,128)(2,1)S(1)} %get-tuple-element.41.lift_ref, bf16[272,256]{1,0:T(8,128)(2,1)S(1)} %get-tuple-element.42.own_rows_ref, s32[256,256]{1,0:T(8,128)S(1)} %get-tuple-element.26.level_ref, ...), custom_call_target="tpu_custom_call" | custom-call | tf_op jit(solution)/shard_map/pallas_call | solution.py:525
  30.7 0.3 %shard_map.147 = (f32[136,384]{1,0:T(8,128)S(1)}, f32[120,256]{1,0:T(8,128)S(1)}) custom-call(f32[272,384]{1,0:T(8,128)S(1)} %get-tuple-element.43.grad_ref, bf16[136,384]{1,0:T(8,128)(2,1)S(1)} %collective-permute-done.7.mine_ref, f32[272,384]{1,0:T(8,128)S(1)} %get-tuple-element.45.slope_ref, f32[272,384]{1,0:T(8,128)S(1)} %get-tuple-element.46.base_ref, ...), custom_call_target="tpu_custom_call" | custom-call | tf_op jit(solution)/shard_map/pallas_call | solution.py:525
  31.0 0.4 %collective-permute-done.8.other_ref = bf16[136,384]{1,0:T(8,128)(2,1)S(1)} collective-permute-done((bf16[136,384]{1,0:T(8,128)(2,1)S(1)}, bf16[136,384]{1,0:T(8,128)(2,1)S(1)}, u32[]{:S(2)}, u32[]{:S(2)}) %collective-permute-start.8) | collective-permute-done | bytes 104480 | tf_op jit(solution)/shard_map/ppermute | solution.py:569
  31.5 1.0 %shard_map.148 = f32[256,256]{1,0:T(8,128)} custom-call(f32[272,384]{1,0:T(8,128)S(1)} %get-tuple-element.43.grad_ref, bf16[136,384]{1,0:T(8,128)(2,1)S(1)} %collective-permute-done.8.other_ref, f32[272,384]{1,0:T(8,128)S(1)} %get-tuple-element.45.slope_ref, f32[272,384]{1,0:T(8,128)S(1)} %get-tuple-element.46.base_ref, ...), custom_call_target="tpu_custom_call" | custom-call | tf_op jit(solution)/shard_map/pallas_call | solution.py:525
  (1 shorter events, 0.0 us)
Async XLA Ops:
  1.5 5.6 %collective-permute-start = (bf16[128,256]{1,0:T(8,128)(2,1)S(1)}, bf16[128,256]{1,0:T(8,128)(2,1)S(1)}, u32[]{:S(2)}, u32[]{:S(2)}) collective-permute-start(bf16[128,256]{1,0:T(8,128)(2,1)S(1)} %edge.1), channel_id=1, source_target_pairs={{0,8},{8,0},{9,17},{17,9},{16,24},{24,16},{1,3},{3,1},{25,27},{27,... | collective-permute-start | bytes 196616 | tf_op jit(solution)/shard_map/ppermute | solution.py:555
  7.1 2.1 %collective-permute-start.1 = (bf16[128,256]{1,0:T(8,128)(2,1)S(1)}, bf16[128,256]{1,0:T(8,128)(2,1)S(1)}, u32[]{:S(2)}, u32[]{:S(2)}) collective-permute-start(bf16[128,256]{1,0:T(8,128)(2,1)S(1)} %collective-permute-done.mine_ref), channel_id=1, source_target_pairs={{0,1},{1,0},{2,3},{3,2},{4,5},{5,4},{6,7},{7,6},{8,9},{9,8},{10,11... | collective-permute-start | bytes 196616 | tf_op jit(solution)/shard_map/ppermute | solution.py:569
  9.4 4.2 %collective-permute-start.2 = (bf16[192,128]{1,0:T(8,128)(2,1)S(1)}, bf16[192,128]{1,0:T(8,128)(2,1)S(1)}, u32[]{:S(2)}, u32[]{:S(2)}) collective-permute-start(bf16[192,128]{1,0:T(8,128)(2,1)S(1)} %shard_map.142), channel_id=1, source_target_pairs={{1,2},{2,1},{3,4},{4,3},{5,6},{6,5},{0,8},{8,0},{7,15},{15,7},{9,1... | collective-permute-start | bytes 147464 | tf_op jit(solution)/shard_map/ppermute | solution.py:555
  13.6 1.3 %collective-permute-start.3 = (bf16[192,128]{1,0:T(8,128)(2,1)S(1)}, bf16[192,128]{1,0:T(8,128)(2,1)S(1)}, u32[]{:S(2)}, u32[]{:S(2)}) collective-permute-start(bf16[192,128]{1,0:T(8,128)(2,1)S(1)} %collective-permute-done.2.mine_ref.cols_mine_ref), channel_id=1, source_target_pairs={{0,1},{1,0},{2,3},{3,2},{4,5},{5,4},{6,7},{7,6},{8,9},{9,8},{10,11... | collective-permute-start | bytes 147464 | tf_op jit(solution)/shard_map/ppermute | solution.py:569
  17.1 1.4 %collective-permute-start.4 = (f32[256,128]{1,0:T(8,128)S(1)}, f32[256,128]{1,0:T(8,128)S(1)}, u32[]{:S(2)}, u32[]{:S(2)}) collective-permute-start(f32[256,128]{1,0:T(8,128)S(1)} %get-tuple-element.37), channel_id=1, source_target_pairs={{0,1},{1,0},{2,3},{3,2},{4,5},{5,4},{6,7},{7,6},{8,9},{9,8},{10,11... | collective-permute-start | bytes 393224 | tf_op jit(solution)/shard_map/ppermute | solution.py:569
  18.5 4.3 %collective-permute-start.5 = (bf16[256,128]{1,0:T(8,128)(2,1)S(1)}, bf16[256,128]{1,0:T(8,128)(2,1)S(1)}, u32[]{:S(2)}, u32[]{:S(2)}) collective-permute-start(bf16[256,128]{1,0:T(8,128)(2,1)S(1)} %add_convert_fusion.grad_ref), channel_id=1, source_target_pairs={{1,2},{2,1},{3,4},{4,3},{5,6},{6,5},{0,8},{8,0},{7,15},{15,7},{9,1... | collective-permute-start | bytes 196616 | tf_op jit(solution)/shard_map/ppermute | solution.py:555
  22.9 1.3 %collective-permute-start.6 = (bf16[256,128]{1,0:T(8,128)(2,1)S(1)}, bf16[256,128]{1,0:T(8,128)(2,1)S(1)}, u32[]{:S(2)}, u32[]{:S(2)}) collective-permute-start(bf16[256,128]{1,0:T(8,128)(2,1)S(1)} %collective-permute-done.5.mine_ref), channel_id=1, source_target_pairs={{0,1},{1,0},{2,3},{3,2},{4,5},{5,4},{6,7},{7,6},{8,9},{9,8},{10,11... | collective-permute-start | bytes 196616 | tf_op jit(solution)/shard_map/ppermute | solution.py:569
  24.6 5.5 %collective-permute-start.7 = (bf16[136,384]{1,0:T(8,128)(2,1)S(1)}, bf16[136,384]{1,0:T(8,128)(2,1)S(1)}, u32[]{:S(2)}, u32[]{:S(2)}) collective-permute-start(bf16[136,384]{1,0:T(8,128)(2,1)S(1)} %get-tuple-element.44), channel_id=1, source_target_pairs={{0,8},{8,0},{9,17},{17,9},{16,24},{24,16},{1,3},{3,1},{25,27},{27,... | collective-permute-start | bytes 313352 | tf_op jit(solution)/shard_map/ppermute | solution.py:555
  30.2 1.3 %collective-permute-start.8 = (bf16[136,384]{1,0:T(8,128)(2,1)S(1)}, bf16[136,384]{1,0:T(8,128)(2,1)S(1)}, u32[]{:S(2)}, u32[]{:S(2)}) collective-permute-start(bf16[136,384]{1,0:T(8,128)(2,1)S(1)} %collective-permute-done.7.mine_ref), channel_id=1, source_target_pairs={{0,1},{1,0},{2,3},{3,2},{4,5},{5,4},{6,7},{7,6},{8,9},{9,8},{10,11... | collective-permute-start | bytes 313352 | tf_op jit(solution)/shard_map/ppermute | solution.py:569
